TPU v7x, 32 devices: a whole 2x2x4 slice. The times are simulated.
32 devices in a mesh: seq: 16 (over z, y, x), head: 2 (over core).
Axes of the slice: x: 2, y: 2, z: 4, core: 2. Of those that a mesh axis runs over, the one named last changes fastest.
Arguments:
- queries: bfloat16 [16384, 2048], P('seq', 'head'), may hold values from -5 to 5
- lin_keys: bfloat16 [16384, 2048], P('seq', 'head'), may hold values from -6 to 6
- lin_values: bfloat16 [16384, 2048], P('seq', 'head'), may hold values from -6 to 6
- window_keys: bfloat16 [16384, 512], P('seq', 'head'), may hold values from -5 to 5
- window_values: bfloat16 [16384, 512], P('seq', 'head'), may hold values from -6 to 6
- level_index: int32 [15, 16384], P(None, 'seq'), may hold values from 0 to 7
- level_table: float32 [8, 16], P(None, 'head'), may hold values from 0.25 to 2
- seq_lengths: int32 [4], replicated, may hold values from 1 to 8, 16 in all
- gain_linear: float32 [2048], P('head'), may hold values from 0.25 to 1.75
- gain_window: float32 [2048], P('head'), may hold values from 0.25 to 1.75
- w_out: bfloat16 [2048, 2048], P('head'), may hold values from -0.125 to 0.125
Outputs:
- mixed: bfloat16 [16384, 2048], P(('seq', 'head'))
Inputs may be any that keep to these rules, and one draw needn't show every extreme that they name: `seq_lengths`: lengths of 4 consecutive sequences in whole shards of 1024 tokens, in order from token 0; they add up to the shards of seq and the longest has exactly half of them.
All inputs are finite; a program needn't handle non-finite values.
Results may differ from a plain program's by a relative error of at most 0.0095.
Values may be sent and summed in bfloat16 or wider, within the bound.
No kernel may reach another device: no remote copies, remote signals or barrier semaphores. Data moves between devices by JAX's collectives and lax.ppermute only.
A program may use at most 128 MiB of HBM per device.

v0:
```python
import jax
import jax.numpy as jnp
from jax import lax
from jax.sharding import PartitionSpec as P

DH = 128
WINDOW = 256
BLOCK = 512


PRECISE = lax.Precision.HIGHEST
EPSILON = 1e-06


def passed_along(block, axis, distance):
    devices = range(lax.axis_size(axis))
    route = [(i - distance, i) for i in devices if i - distance in devices]
    return lax.ppermute(block, axis, route)


def bit_count(values, bit_width):
    running_total = jnp.zeros_like(values)
    for shift_by in range(bit_width):
        running_total = running_total + (values >= 1 << shift_by).astype(values.dtype)
    return running_total


def rms_scale(values, gain_vector):
    mean_square = jnp.mean(values * values, axis=-1, keepdims=True)
    return values * lax.rsqrt(mean_square + EPSILON) * gain_vector


def shards(
    queries,
    lin_keys,
    lin_values,
    window_keys,
    window_values,
    level_index,
    level_table,
    seq_lengths,
    gain_linear,
    gain_window,
    w_out,
):
    local_tokens = queries.shape[0]
    local_heads = level_table.shape[1]
    local_groups = window_keys.shape[1] // DH
    members = local_heads // local_groups
    level_total = level_index.shape[0]
    block_bits = BLOCK.bit_length() - 1
    local_blocks = local_tokens // BLOCK
    shard_bits = lax.axis_size("seq").bit_length() - 1
    shard_id = lax.axis_index("seq")
    seq_ends = jnp.cumsum(seq_lengths)
    seq_starts = seq_ends - seq_lengths
    seq_begin = jnp.max(jnp.where(seq_starts <= shard_id, seq_starts, 0))
    opens_here = seq_begin == shard_id
    table_rows = jnp.arange(level_table.shape[0], dtype=jnp.int32)
    one_hot = (level_index[:, :, None] == table_rows[None, None, :]).astype(jnp.float32)
    level_scale = jnp.exp2(-0.5 * jnp.arange(level_total, dtype=jnp.float32))
    weights = (
        jnp.einsum("ltk,kh->lth", one_hot, level_table, precision=PRECISE)
        * level_scale[:, None, None]
    )
    query_heads = queries.reshape(local_tokens, local_heads, DH)
    key_heads = lin_keys.reshape(local_tokens, local_heads, DH)
    value_heads = lin_values.reshape(local_tokens, local_heads, DH)
    window_key_heads = window_keys.reshape(local_tokens, local_groups, DH)
    window_value_heads = window_values.reshape(local_tokens, local_groups, DH)
    rim_keys, rim_values = passed_along(
        (window_key_heads[local_tokens - WINDOW :], window_value_heads[local_tokens - WINDOW :]),
        "seq",
        1,
    )
    block_states = jnp.einsum(
        "cshd,cshe->chde",
        key_heads.reshape(local_blocks, BLOCK, local_heads, DH),
        value_heads.reshape(local_blocks, BLOCK, local_heads, DH),
        preferred_element_type=jnp.float32,
    )
    shard_state = jnp.sum(block_states, axis=0)
    piece_states = lax.all_gather(
        shard_state[None].astype(jnp.bfloat16), "seq", axis=0, tiled=True
    ).astype(jnp.float32)
    sources = jnp.arange(piece_states.shape[0], dtype=jnp.int32)
    highest = bit_count(jnp.bitwise_xor(sources, shard_id), shard_bits) - 1
    usable = (sources < shard_id) & (sources >= seq_begin)
    selector = (
        (highest[:, None] == jnp.arange(shard_bits, dtype=jnp.int32)[None, :]) & usable[:, None]
    ).astype(jnp.float32)
    shard_levels = jnp.zeros((shard_bits, local_heads, DH, DH), jnp.float32) + jnp.einsum(
        "nl,nhde->lhde", selector, piece_states, precision=PRECISE
    )
    extended_keys = jnp.concatenate([rim_keys, window_key_heads], axis=0)
    extended_values = jnp.concatenate([rim_values, window_value_heads], axis=0)
    offsets = jnp.arange(BLOCK, dtype=jnp.int32)
    level_grid = bit_count(jnp.bitwise_xor(offsets[:, None], offsets[None, :]), block_bits)
    causal = offsets[None, :] <= offsets[:, None]
    window_offsets = jnp.arange(BLOCK + WINDOW, dtype=jnp.int32) - WINDOW
    linear_gain = gain_linear.reshape(local_heads, DH)
    window_gain = gain_window.reshape(local_heads, DH)
    zero_state = jnp.zeros((local_heads, DH, DH), jnp.float32)
    outputs = []
    for block_id in range(local_blocks):
        first_row = block_id * BLOCK
        query_block = query_heads[first_row : first_row + BLOCK]
        key_block = key_heads[first_row : first_row + BLOCK]
        value_block = value_heads[first_row : first_row + BLOCK]
        weight_block = weights[:, first_row : first_row + BLOCK]
        scores = jnp.einsum(
            "thd,shd->hts", query_block, key_block, preferred_element_type=jnp.float32
        )
        mixing = jnp.zeros((local_heads, BLOCK, BLOCK), jnp.float32)
        for level_id in range(block_bits + 1):
            mixing = (
                mixing
                + jnp.where(level_grid == level_id, 1.0, 0.0)[None, :, :]
                * weight_block[level_id].T[:, :, None]
            )
        mixing = jnp.where(causal[None, :, :], mixing, 0.0)
        near_part = jnp.einsum(
            "hts,shd->thd",
            (scores * mixing).astype(jnp.bfloat16),
            value_block,
            preferred_element_type=jnp.float32,
        )
        local_levels = []
        group_span = 1 << 0
        upper_edge = block_id // group_span * group_span
        if block_id // group_span % 2 == 1:
            local_levels.append(jnp.sum(block_states[upper_edge - group_span : upper_edge], axis=0))
        else:
            local_levels.append(zero_state)
        states_stack = jnp.concatenate([jnp.stack(local_levels), shard_levels], axis=0)
        far_weights = weight_block[block_bits + 1 :]
        query_float = query_block.astype(jnp.float32)
        far_part = jnp.zeros((BLOCK, local_heads, DH), jnp.float32)
        for level_id in range(states_stack.shape[0]):
            reached = jnp.einsum(
                "thd,hde->the", query_float, states_stack[level_id], precision=PRECISE
            )
            far_part = far_part + far_weights[level_id][:, :, None] * reached
        linear_part = rms_scale(near_part + far_part, linear_gain)
        key_window = extended_keys[first_row : first_row + BLOCK + WINDOW]
        value_window = extended_values[first_row : first_row + BLOCK + WINDOW]
        key_pos = first_row + window_offsets
        query_pos = first_row + offsets
        allowed = (
            (key_pos[None, :] <= query_pos[:, None])
            & (key_pos[None, :] > query_pos[:, None] - WINDOW)
            & ((key_pos[None, :] >= 0) | jnp.logical_not(opens_here))
        )
        grouped = query_block.reshape(BLOCK, local_groups, members, DH)
        logits = jnp.einsum(
            "tkgd,skd->kgts", grouped, key_window, preferred_element_type=jnp.float32
        ) * DH ** (-0.5)
        logits = jnp.where(allowed[None, None, :, :], logits, -1e30)
        row_peak = jnp.max(logits, axis=-1, keepdims=True)
        exponents = jnp.exp(logits - row_peak)
        window_weights = (exponents / jnp.sum(exponents, axis=-1, keepdims=True)).astype(
            jnp.bfloat16
        )
        window_raw = jnp.einsum(
            "kgts,skd->tkgd", window_weights, value_window, preferred_element_type=jnp.float32
        ).reshape(BLOCK, local_heads, DH)
        window_part = rms_scale(window_raw, window_gain)
        outputs.append(
            (linear_part + window_part).astype(jnp.bfloat16).reshape(BLOCK, local_heads * DH)
        )
    attended = jnp.concatenate(outputs, axis=0)
    return lax.psum_scatter(
        jnp.dot(attended, w_out, preferred_element_type=jnp.float32).astype(jnp.bfloat16),
        "head",
        scatter_dimension=0,
        tiled=True,
    )


def solution(mesh):
    placed = (
        P("seq", "head"),
        P("seq", "head"),
        P("seq", "head"),
        P("seq", "head"),
        P("seq", "head"),
        P(None, "seq"),
        P(None, "head"),
        P(),
        P("head"),
        P("head"),
        P("head", None),
    )
    return jax.shard_map(
        shards, mesh=mesh, in_specs=placed, out_specs=P(("seq", "head"), None), check_vma=False
    )
```

profile of v0, /device:TPU:0, one launch (start us, length us, event | category | flops | bytes accessed | tf_op | source)
XLA Modules:
  0.0 171.8 jit_solution(13455842207525485610)
XLA Ops:
  6.5 2.4 %copy.199 = bf16[128,8,8,128]{3,2,1,0:T(8,128)(2,1)S(1)} copy(bf16[128,8,8,128]{3,1,2,0:T(8,128)(2,1)} %bitcast.332) | data formatting | bytes 4194304
  9.6 2.9 %fusion.107 = (bf16[8,128,128]{2,1,0:T(8,128)(2,1)}, f32[2,8,128,128]{3,2,1,0:T(8,128)}) fusion(bf16[2,512,8,128]{3,2,1,0:T(8,128)(2,1)S(1)} %bitcast.346, bf16[2,512,8,128]{3,2,1,0:T(8,128)(2,1)S(1)} %bitcast.345), kind=kOutput, calls=%fused_computation.184 | convolution fusion | flops 268566528 | bytes 5505024 | tf_op jit(solution)/shard_map/cshd,cshe->chde/dot_general | solution.py:76
  12.8 0.8 copy.134
  13.6 5.5 %collective-permute-start.1 = (bf16[256,2,128]{2,0,1:T(8,128)(2,1)}, bf16[256,2,128]{2,0,1:T(8,128)(2,1)}, u32[]{:S(2)}, u32[]{:S(2)}) collective-permute-start(bf16[256,2,128]{2,0,1:T(8,128)(2,1)} %copy.134), channel_id=1, source_target_pairs={{0,2},{2,4},{4,6},{6,8},{8,10},{10,12},{12,14},{14,16},{16,18},{18... | collective-permute-start | bytes 393224 | tf_op jit(solution)/shard_map/ppermute | solution.py:18
  19.9 3.7 %collective-permute-start = (bf16[256,2,128]{0,2,1:T(8,128)(2,1)}, bf16[256,2,128]{0,2,1:T(8,128)(2,1)}, u32[]{:S(2)}, u32[]{:S(2)}) collective-permute-start(bf16[256,2,128]{0,2,1:T(8,128)(2,1)} %bitcast.45), channel_id=1, source_target_pairs={{0,2},{2,4},{4,6},{6,8},{8,10},{10,12},{12,14},{14,16},{16,18},{18... | collective-permute-start | bytes 393224 | tf_op jit(solution)/shard_map/ppermute | solution.py:18
  24.2 1.8 %compare_select_fusion = (f32[512,512]{1,0:T(8,128)}, f32[512,512]{1,0:T(8,128)}) fusion(), kind=kLoop, calls=%fused_computation.86 | loop fusion | flops 8126464 | bytes 2097152 | tf_op jit(solution)/shard_map/jit(_where)/select_n | solution.py:118
  25.9 1.7 compare_select_fusion.2
  27.7 1.7 compare_select_fusion.4
  29.4 1.7 compare_select_fusion.6
  31.1 1.7 %compare_select_fusion.8 = (f32[512,512]{1,0:T(8,128)}, f32[512,512]{1,0:T(8,128)}) fusion(), kind=kLoop, calls=%fused_computation.94 | loop fusion | flops 8126464 | bytes 2097152 | tf_op jit(solution)/shard_map/jit(_where)/select_n | solution.py:118
  32.8 1.5 fusion.98
  34.3 1.6 fusion.99
  35.9 0.8 iota_compare_fusion.1
  38.1 1.5 fusion.100
  39.7 1.6 copy.197
  41.3 1.4 copy.198
  42.6 2.3 %copy.143 = bf16[512,1024]{0,1:T(8,128)(2,1)} copy(bf16[512,1024]{1,0:T(8,128)(2,1)} %get-tuple-element.8) | data formatting | bytes 2097152 | tf_op jit(solution)/shard_map/slice | solution.py:109
  44.9 1.5 copy.195
  46.5 1.3 copy.196
  47.8 2.3 %copy.118 = bf16[512,1024]{0,1:T(8,128)(2,1)} copy(bf16[512,1024]{1,0:T(8,128)(2,1)} %get-tuple-element.7) | data formatting | bytes 2097152 | tf_op jit(solution)/shard_map/slice | solution.py:109
  50.0 0.8 reduce-window.9
  50.9 1.4 fusion.84
  52.9 1.2 copy.157
  54.1 1.1 and_and_fusion
  55.2 7.6 %fusion.108 = (f32[2,4,512]{2,1,0:T(4,128)S(1)}, f32[2,4,512,768]{2,3,1,0:T(8,128)}) fusion(pred[512,768]{0,1:T(8,128)(4,1)S(1)} %and_and_fusion, bf16[768,2,128,1]{0,2,3,1:T(8,128)(2,1)S(1)} %bitcast.337, bf16[512,2,4,128]{0,3,2,1:T(8,128)(2,1)S(1)} %bitcast.325), kind=kOutput, calls=%fused_computation.185 | convolution fusion | flops 817890048 | bytes 14434304 | tf_op jit(solution)/shard_map/sub | solution.py:160
  62.8 7.6 %fusion.29 = (f32[512,2,4]{0,2,1:T(4,128)S(1)}, f32[2,4,512,128]{2,3,1,0:T(8,128)}) fusion(bf16[768,2,128,1]{0,2,3,1:T(8,128)(2,1)S(1)} %bitcast.355, f32[2,4,512,768]{2,3,1,0:T(8,128)} %get-tuple-element.56, f32[2,4,512]{2,1,0:T(4,128)S(1)} %get-tuple-element.55), kind=kOutput, calls=%fused_computation.39 | convolution fusion | flops 812642304 | bytes 15106048 | tf_op jit(solution)/shard_map/kgts,skd->tkgd/dot_general | solution.py:164
  73.4 2.3 %fusion.64 = f32[8,128,512]{2,1,0:T(8,128)} fusion(bf16[512,8,128]{0,2,1:T(8,128)(2,1)S(1)} %bitcast.318), kind=kOutput, calls=%fused_computation.104 | convolution fusion | flops 805306368 | bytes 3145728 | tf_op jit(solution)/shard_map/thd,hde->the/dot_general | solution.py:140
  75.7 2.5 %fusion.59 = f32[8,128,512]{2,1,0:T(8,128)} fusion(bf16[512,8,128]{0,2,1:T(8,128)(2,1)S(1)} %bitcast.326, f32[2,8,128,128]{3,2,1,0:T(8,128)S(1)} %copy-done.20), kind=kOutput, calls=%fused_computation.97 | convolution fusion | flops 805306368 | bytes 3670016 | tf_op jit(solution)/shard_map/thd,hde->the/dot_general | solution.py:140
  78.1 13.7 %fusion.15 = f32[8,512,128]{1,2,0:T(8,128)} fusion(bf16[512,8,128]{0,2,1:T(8,128)(2,1)} %bitcast.352, f32[8,512]{1,0:T(8,128)} %get-tuple-element.21, f32[8,512]{1,0:T(8,128)} %get-tuple-element.22, f32[8,512]{1,0:T(8,128)} %get-tuple-element.23, f32[8,512]{1,0:T(8,128)} %get-tuple-element.24, f32[8,512]{1,0:T(8,128)} %get-tuple-element.25, ...), kind=kOutput, calls=%fused_computation.23 | convolution fusion | flops 1119879168 | bytes 16154624 | tf_op jit(solution)/shard_map/hts,shd->thd/dot_general | solution.py:122
  91.8 13.1 %fusion.14 = f32[8,512,128]{1,2,0:T(8,128)} fusion(bf16[512,8,128]{0,2,1:T(8,128)(2,1)} %bitcast.350, f32[8,512]{1,0:T(8,128)} %get-tuple-element.35, f32[512,512]{1,0:T(8,128)} %get-tuple-element.61, f32[8,512]{1,0:T(8,128)} %get-tuple-element.36, f32[512,512]{1,0:T(8,128)} %get-tuple-element.62, f32[8,512]{1,0:T(8,128)} %get-tuple-element.37, ...), kind=kOutput, calls=%fused_computation.22 | convolution fusion | flops 1119879168 | bytes 16154624 | tf_op jit(solution)/shard_map/hts,shd->thd/dot_general | solution.py:122
  105.6 1.0 copy.132
  106.7 1.3 rsqrt.43
  108.3 10.8 %fusion.102 = (f32[2,4,512]{2,1,0:T(4,128)}, f32[2,4,512,768]{2,3,1,0:T(8,128)}) fusion(pred[512,768]{0,1:T(8,128)(4,1)S(1)} %fusion.45, bf16[512,2,4,128]{0,3,2,1:T(8,128)(2,1)S(1)} %bitcast.320, bf16[1024,2,128]{2,0,1:T(8,128)(2,1)S(1)} %copy.136, bf16[256,2,128]{2,0,1:T(8,128)(2,1)} %collective-permute-done.1), kind=kOutput, calls=%fused_computation.183 | convolution fusion | flops 818676480 | bytes 14696448 | tf_op jit(solution)/shard_map/sub | solution.py:160
  119.1 7.1 %fusion.35 = (f32[512,2,4]{0,2,1:T(4,128)S(1)}, f32[2,128,4,512]{3,1,2,0:T(8,128)}) fusion(f32[2,4,512,768]{2,3,1,0:T(8,128)} %get-tuple-element.48, f32[2,4,512]{2,1,0:T(4,128)} %get-tuple-element.47, bf16[1024,2,128]{0,2,1:T(8,128)(2,1)S(1)} %bitcast.353, bf16[256,2,128]{0,2,1:T(8,128)(2,1)} %collective-permute-done), kind=kOutput, calls=%fused_computation.51 | convolution fusion | flops 813428736 | bytes 15368192 | tf_op jit(solution)/shard_map/kgts,skd->tkgd/dot_general | solution.py:164
  126.2 4.7 %fusion.12 = f32[4,8,128,128]{3,0,2,1:T(4,128)S(1)} fusion(bf16[16,8,128,128]{3,2,1,0:T(8,128)(2,1)} %bitcast.344, s32[16]{0:T(128)S(1)} %fusion.83, pred[16]{0:T(512)(128)(4,1)S(1)} %compare_and_fusion), kind=kOutput, calls=%fused_computation.20 | convolution fusion | flops 16777344 | bytes 6291536 | tf_op jit(solution)/shard_map/nl,nhde->lhde/dot_general | solution.py:92
  130.9 1.9 %fusion.101 = (f32[1,8,128,128]{3,0,2,1:T(1,128)S(1)}, f32[1,8,128,128]{3,0,2,1:T(1,128)S(1)}, f32[1,8,128,128]{3,0,2,1:T(1,128)S(1)}, f32[1,8,128,128]{3,0,2,1:T(1,128)S(1)}) fusion(f32[4,8,128,128]{3,0,2,1:T(4,128)S(1)} %fusion.12), kind=kLoop, calls=%fused_computation.182 | loop fusion | bytes 4194304 | tf_op jit(solution)/shard_map/slice | solution.py:141
  132.8 1.1 fusion.112
  133.8 1.3 fusion.109
  135.1 1.1 fusion.113
  136.2 1.1 fusion.110
  137.4 1.1 fusion.114
  138.4 1.1 fusion.111
  139.7 1.9 %multiply_reduce_fusion = (f32[512,8]{0,1:T(8,128)S(1)}, f32[512,8,128]{0,2,1:T(8,128)S(1)}) fusion(f32[8,128,128]{2,1,0:T(8,128)S(1)} %bitcast.334, bf16[512,8,128]{0,2,1:T(8,128)(2,1)S(1)} %bitcast.331, f32[512,8]{0,1:T(8,128)S(1)} %copy-done.26, f32[8,128,512]{2,1,0:T(8,128)S(1)} %fusion.114, f32[512,8]{0,1:T(8,128)S(1)} %copy-done.27, ...), kind=kOutput, calls=%fused_computation.65 | convolution fusion | flops 811593728 | bytes 14254080 | tf_op jit(solution)/shard_map/thd,hde->the/dot_general | solution.py:140
  141.9 1.9 %multiply_reduce_fusion.1 = (f32[512,8]{0,1:T(8,128)S(1)}, f32[512,8,128]{0,2,1:T(8,128)S(1)}) fusion(f32[8,128,128]{2,1,0:T(8,128)S(1)} %bitcast.335, bf16[512,8,128]{0,2,1:T(8,128)(2,1)S(1)} %bitcast.324, f32[512,8]{0,1:T(8,128)S(1)} %copy-done.23, f32[8,128,512]{2,1,0:T(8,128)S(1)} %fusion.111, f32[512,8]{0,1:T(8,128)S(1)} %copy-done.24, ...), kind=kOutput, calls=%fused_computation.66 | convolution fusion | flops 811593728 | bytes 14254080 | tf_op jit(solution)/shard_map/thd,hde->the/dot_general | solution.py:140
  144.1 1.1 fusion.28
  145.2 1.1 copy-done.36
  146.3 6.2 %convolution_convert_fusion = bf16[1024,2048]{1,0:T(8,128)(2,1)} fusion(bf16[1024,2048]{1,0:T(8,128)(2,1)S(1)} %copy-done.36, bf16[512,1024]{0,1:T(8,128)(2,1)S(1)} %bitcast.348, bf16[512,1024]{0,1:T(8,128)(2,1)S(1)} %bitcast.347), kind=kOutput, calls=%fused_computation.24 | convolution fusion | flops 4301258752 | bytes 10485760 | tf_op jit(solution)/shard_map/dot_general | solution.py:173
  152.5 12.2 %reduce-scatter.2.cloned.1.call-done = bf16[512,2048]{1,0:T(8,128)(2,1)} async-done(((bf16[1024,2048]{1,0:T(8,128)(2,1)}), bf16[512,2048]{1,0:T(8,128)(2,1)}) %reduce-scatter.2.cloned.1.call-update) | async-done | bytes 2097168 | tf_op jit(solution)/shard_map/reduce_scatter | solution.py:172
  (108 shorter events, 8.3 us)
Async XLA Ops:
  6.5 64.5 %copy-start = (f32[8,8]{1,0:T(8,128)S(1)}, f32[8,8]{1,0:T(8,128)}, u32[]{:S(2)}) copy-start(f32[8,8]{1,0:T(8,128)} %param.17) | copy-start | bytes 772
  6.5 2.4 %copy-start.5 = (bf16[1024,1024]{1,0:T(8,128)(2,1)S(1)}, bf16[1024,1024]{1,0:T(8,128)(2,1)}, u32[]{:S(2)}) copy-start(bf16[1024,1024]{1,0:T(8,128)(2,1)} %param.13) | copy-start | bytes 6291460
  6.5 119.7 %all-gather.3.cloned.1.call-start = ((), (), s32[]{:S(2)}) async-start(), calls=%async_computation.2 | async-start | bytes 4456448 | tf_op jit(solution)/shard_map/all_gather | solution.py:83
  8.9 3.7 %copy-start.18 = (bf16[1024,256]{1,0:T(8,128)(2,1)S(1)}, bf16[1024,256]{1,0:T(8,128)(2,1)}, u32[]{:S(2)}) copy-start(bf16[1024,256]{1,0:T(8,128)(2,1)} %param.14) | copy-start | bytes 1572868
  9.6 9.6 %slice-start.1 = ((bf16[1024,256]{1,0:T(8,128)(2,1)}), bf16[256,256]{1,0:T(8,128)(2,1)S(1)}, s32[]{:S(2)}) async-start(bf16[1024,256]{1,0:T(8,128)(2,1)} %param.15), calls=%async_computation.4 | async-start | bytes 262144 | tf_op jit(solution)/shard_map/slice | solution.py:72
  12.5 152.2 %reduce-scatter.2.cloned.1.call-start = ((), (), s32[]{:S(2)}) async-start(), calls=%async_computation.1 | async-start | bytes 6291456 | tf_op jit(solution)/shard_map/reduce_scatter | solution.py:172
  12.8 24.5 %copy-start.6 = (bf16[1024,256]{0,1:T(8,128)(2,1)}, bf16[1024,256]{0,1:T(8,128)(2,1)S(1)}, u32[]{:S(2)}) copy-start(bf16[1024,256]{0,1:T(8,128)(2,1)S(1)} %copy.133) | copy-start | bytes 1572868
  13.6 94.7 %collective-permute-start.1 = (bf16[256,2,128]{2,0,1:T(8,128)(2,1)}, bf16[256,2,128]{2,0,1:T(8,128)(2,1)}, u32[]{:S(2)}, u32[]{:S(2)}) collective-permute-start(bf16[256,2,128]{2,0,1:T(8,128)(2,1)} %copy.134), channel_id=1, source_target_pairs={{0,2},{2,4},{4,6},{6,8},{8,10},{10,12},{12,14},{14,16},{16,18},{18... | collective-permute-start | bytes 393224 | tf_op jit(solution)/shard_map/ppermute | solution.py:18
  19.9 99.2 %collective-permute-start = (bf16[256,2,128]{0,2,1:T(8,128)(2,1)}, bf16[256,2,128]{0,2,1:T(8,128)(2,1)}, u32[]{:S(2)}, u32[]{:S(2)}) collective-permute-start(bf16[256,2,128]{0,2,1:T(8,128)(2,1)} %bitcast.45), channel_id=1, source_target_pairs={{0,2},{2,4},{4,6},{6,8},{8,10},{10,12},{12,14},{14,16},{16,18},{18... | collective-permute-start | bytes 393224 | tf_op jit(solution)/shard_map/ppermute | solution.py:18
  25.9 6.9 %copy-start.4 = (bf16[1024,1024]{1,0:T(8,128)(2,1)S(1)}, bf16[1024,1024]{1,0:T(8,128)(2,1)}, u32[]{:S(2)}) copy-start(bf16[1024,1024]{1,0:T(8,128)(2,1)} %param.12) | copy-start | bytes 6291460
  32.8 4.5 %copy-start.13 = (bf16[1024,256]{1,0:T(8,128)(2,1)S(1)}, bf16[1024,256]{1,0:T(8,128)(2,1)}, u32[]{:S(2)}) copy-start(bf16[1024,256]{1,0:T(8,128)(2,1)} %param.15) | copy-start | bytes 1572868
  32.8 5.3 %copy-start.12 = (bf16[1024,1024]{1,0:T(8,128)(2,1)S(1)}, bf16[1024,1024]{1,0:T(8,128)(2,1)}, u32[]{:S(2)}) copy-start(bf16[1024,1024]{1,0:T(8,128)(2,1)} %param.11) | copy-start | bytes 6291460
  35.9 5.3 %copy-start.9 = (bf16[512,1024]{1,0:T(8,128)(2,1)S(1)}, bf16[512,1024]{1,0:T(8,128)(2,1)}, u32[]{:S(2)}) copy-start(bf16[512,1024]{1,0:T(8,128)(2,1)} %get-tuple-element.6) | copy-start | bytes 3145732
  39.7 6.8 %copy-start.8 = (bf16[512,1024]{1,0:T(8,128)(2,1)S(1)}, bf16[512,1024]{1,0:T(8,128)(2,1)}, u32[]{:S(2)}) copy-start(bf16[512,1024]{1,0:T(8,128)(2,1)} %get-tuple-element.5) | copy-start | bytes 3145732
  44.9 10.3 %slice-start = ((bf16[1024,256]{0,1:T(8,128)(2,1)}), bf16[768,256]{0,1:T(8,128)(2,1)S(1)}, s32[]{:S(2)}) async-start(bf16[1024,256]{0,1:T(8,128)(2,1)} %copy-done.6), calls=%async_computation.3 | async-start | bytes 786432 | tf_op jit(solution)/shard_map/slice | solution.py:145
  62.8 8.2 %copy-start.32 = (s32[15,1024]{1,0:T(8,128)S(1)}, s32[15,1024]{1,0:T(8,128)}, u32[]{:S(2)}) copy-start(s32[15,1024]{1,0:T(8,128)} %param.16) | copy-start | bytes 184324
  62.8 8.2 %copy-start.35 = (f32[15]{0:T(128)S(1)}, f32[15]{0:T(128)}, u32[]{:S(2)}) copy-start(f32[15]{0:T(128)} %multiply_exponential_fusion) | copy-start | bytes 184
  70.4 5.3 %copy-start.20 = (f32[2,8,128,128]{3,2,1,0:T(8,128)S(1)}, f32[2,8,128,128]{3,2,1,0:T(8,128)}, u32[]{:S(2)}) copy-start(f32[2,8,128,128]{3,2,1,0:T(8,128)} %get-tuple-element.50) | copy-start | bytes 3145732
  71.5 6.7 %copy-start.17 = (f32[512,512]{1,0:T(8,128)S(1)}, f32[512,512]{1,0:T(8,128)}, u32[]{:S(2)}) copy-start(f32[512,512]{1,0:T(8,128)} %get-tuple-element.61) | copy-start | bytes 3145732
  91.8 13.8 %copy-start.14 = (bf16[1024,256]{1,0:T(8,128)(2,1)S(1)}, bf16[1024,256]{1,0:T(8,128)(2,1)}, u32[]{:S(2)}) copy-start(bf16[1024,256]{1,0:T(8,128)(2,1)} %param.15) | copy-start | bytes 1572868
  91.8 16.2 %copy-start.7 = (bf16[1024,256]{0,1:T(8,128)(2,1)S(1)}, bf16[1024,256]{0,1:T(8,128)(2,1)}, u32[]{:S(2)}) copy-start(bf16[1024,256]{0,1:T(8,128)(2,1)} %copy-done.6) | copy-start | bytes 1572868
  108.3 10.8 %copy-start.19 = (bf16[1024,256]{0,1:T(8,128)(2,1)S(1)}, bf16[1024,256]{0,1:T(8,128)(2,1)}, u32[]{:S(2)}) copy-start(bf16[1024,256]{0,1:T(8,128)(2,1)} %copy.132) | copy-start | bytes 1572868
  137.3 2.2 %copy-start.2 = (f32[8,128,512]{2,1,0:T(8,128)S(1)}, f32[8,128,512]{2,1,0:T(8,128)}, u32[]{:S(2)}) copy-start(f32[8,128,512]{2,1,0:T(8,128)} %fusion.59) | copy-start | bytes 6291460
  137.3 2.2 %copy-start.11 = (f32[8,512,128]{1,2,0:T(8,128)S(1)}, f32[8,512,128]{1,2,0:T(8,128)}, u32[]{:S(2)}) copy-start(f32[8,512,128]{1,2,0:T(8,128)} %fusion.15) | copy-start | bytes 6291460
  137.3 2.2 %copy-start.26 = (f32[512,8]{0,1:T(8,128)S(1)}, f32[512,8]{0,1:T(8,128)}, u32[]{:S(2)}) copy-start(f32[512,8]{0,1:T(8,128)} %get-tuple-element.16) | copy-start | bytes 49156
  137.3 2.2 %copy-start.27 = (f32[512,8]{0,1:T(8,128)S(1)}, f32[512,8]{0,1:T(8,128)}, u32[]{:S(2)}) copy-start(f32[512,8]{0,1:T(8,128)} %get-tuple-element.17) | copy-start | bytes 49156
  137.3 2.2 %copy-start.28 = (f32[512,8]{0,1:T(8,128)S(1)}, f32[512,8]{0,1:T(8,128)}, u32[]{:S(2)}) copy-start(f32[512,8]{0,1:T(8,128)} %get-tuple-element.18) | copy-start | bytes 49156
  137.3 2.2 %copy-start.29 = (f32[512,8]{0,1:T(8,128)S(1)}, f32[512,8]{0,1:T(8,128)}, u32[]{:S(2)}) copy-start(f32[512,8]{0,1:T(8,128)} %get-tuple-element.19) | copy-start | bytes 49156
  137.4 2.2 %copy-start.30 = (f32[512,8]{0,1:T(8,128)S(1)}, f32[512,8]{0,1:T(8,128)}, u32[]{:S(2)}) copy-start(f32[512,8]{0,1:T(8,128)} %get-tuple-element.20) | copy-start | bytes 49156
  139.6 2.0 %copy-start.3 = (f32[8,128,512]{2,1,0:T(8,128)S(1)}, f32[8,128,512]{2,1,0:T(8,128)}, u32[]{:S(2)}) copy-start(f32[8,128,512]{2,1,0:T(8,128)} %fusion.64) | copy-start | bytes 6291460
  139.6 2.2 %copy-start.10 = (f32[8,512,128]{1,2,0:T(8,128)S(1)}, f32[8,512,128]{1,2,0:T(8,128)}, u32[]{:S(2)}) copy-start(f32[8,512,128]{1,2,0:T(8,128)} %fusion.14) | copy-start | bytes 6291460
  139.6 2.2 %copy-start.21 = (f32[512,8]{0,1:T(8,128)S(1)}, f32[512,8]{0,1:T(8,128)}, u32[]{:S(2)}) copy-start(f32[512,8]{0,1:T(8,128)} %get-tuple-element.34) | copy-start | bytes 49156
  139.6 2.2 %copy-start.22 = (f32[512,8]{0,1:T(8,128)S(1)}, f32[512,8]{0,1:T(8,128)}, u32[]{:S(2)}) copy-start(f32[512,8]{0,1:T(8,128)} %get-tuple-element.15) | copy-start | bytes 49156
  139.6 2.2 %copy-start.23 = (f32[512,8]{0,1:T(8,128)S(1)}, f32[512,8]{0,1:T(8,128)}, u32[]{:S(2)}) copy-start(f32[512,8]{0,1:T(8,128)} %get-tuple-element.31) | copy-start | bytes 49156
  139.6 2.2 %copy-start.24 = (f32[512,8]{0,1:T(8,128)S(1)}, f32[512,8]{0,1:T(8,128)}, u32[]{:S(2)}) copy-start(f32[512,8]{0,1:T(8,128)} %get-tuple-element.32) | copy-start | bytes 49156
  139.7 2.2 %copy-start.25 = (f32[512,8]{0,1:T(8,128)S(1)}, f32[512,8]{0,1:T(8,128)}, u32[]{:S(2)}) copy-start(f32[512,8]{0,1:T(8,128)} %get-tuple-element.33) | copy-start | bytes 49156
  141.8 1.9 %copy-start.15 = (f32[2,4,512,128]{2,3,1,0:T(8,128)S(1)}, f32[2,4,512,128]{2,3,1,0:T(8,128)}, u32[]{:S(2)}) copy-start(f32[2,4,512,128]{2,3,1,0:T(8,128)} %get-tuple-element.58) | copy-start | bytes 6291460
  141.9 2.2 %copy-start.16 = (f32[2,128,4,512]{3,1,2,0:T(8,128)S(1)}, f32[2,128,4,512]{3,1,2,0:T(8,128)}, u32[]{:S(2)}) copy-start(f32[2,128,4,512]{3,1,2,0:T(8,128)} %get-tuple-element.52) | copy-start | bytes 6291460
  141.9 2.2 %copy-start.31 = (f32[512,8]{0,1:T(8,128)S(1)}, f32[512,8]{0,1:T(8,128)}, u32[]{:S(2)}) copy-start(f32[512,8]{0,1:T(8,128)} %rsqrt.43) | copy-start | bytes 49156
  141.9 2.2 %copy-start.33 = (f32[1024]{0:T(1024)S(1)}, f32[1024]{0:T(1024)}, u32[]{:S(2)}) copy-start(f32[1024]{0:T(1024)} %param.20) | copy-start | bytes 12292
  141.9 2.2 %copy-start.34 = (f32[1024]{0:T(1024)S(1)}, f32[1024]{0:T(1024)}, u32[]{:S(2)}) copy-start(f32[1024]{0:T(1024)} %param.19) | copy-start | bytes 12292
  144.1 2.2 %copy-start.36 = (bf16[1024,2048]{1,0:T(8,128)(2,1)S(1)}, bf16[1024,2048]{1,0:T(8,128)(2,1)}, u32[]{:S(2)}) copy-start(bf16[1024,2048]{1,0:T(8,128)(2,1)} %param.21) | copy-start | bytes 12582916
  146.3 18.4 %copy-start.1 = (f32[8,8]{1,0:T(8,128)S(1)}, f32[8,8]{1,0:T(8,128)}, u32[]{:S(2)}) copy-start(f32[8,8]{1,0:T(8,128)} %param.17) | copy-start | bytes 772
Sparse Core Ops, SparseCore 0:
  12.6 78.6 all-gather.2
  152.7 12.0 reduce-scatter.1
where the time goes:
time: 175 us; the launch traced here: 172 us
  matrix products  89.3 us (51%)
  local copies, waits for them, and re-layouts  29.4 us (17%)
  other arithmetic  16.8 us (10%)
  between operations  14.9 us (9%)
  waiting for transfers between devices  12.2 us (7%)
  starting transfers between devices  9.23 us (5%)
    dot_general x2, matrix products, shards(): jnp.einsum('hts,shd->thd', (scores * mixing).astype(jnp.bfloat16), value_...  26.8 us
    sub x2, matrix products, shards(): exponents = jnp.exp(logits - row_peak)  18.4 us
    dot_general x10, matrix products, shards(): jnp.einsum('thd,hde->the', query_float, states_stack[level_id], precision...  15.1 us
    dot_general x2, matrix products, shards(): jnp.einsum('kgts,skd->tkgd', window_weights, value_window, preferred_elem...  14.7 us
    reduce_scatter x1, waiting for transfers between devices, shards(): lax.psum_scatter(jnp.dot(attended, w_out, preferred_element_type=jnp.floa...  12.2 us
    unnamed x82, local copies, waits for them, and re-layouts  11.7 us
    ppermute x2, starting transfers between devices, passed_along(): return lax.ppermute(block, axis, route)  9.19 us
    select_n x5, other arithmetic, shards(): jnp.where(level_grid == level_id, 1.0, 0.0)[None, :, :]  8.61 us
  transfers between devices with their start and end apart: 4, of which 1 were waited for; matrix products, arithmetic and copies ran while one was open for 60% of the time, Pallas kernels for 0%

commit v1 on v0

v1 whole, which is shorter than its diff:
```python
import functools

import jax
import jax.numpy as jnp
from jax import lax
from jax.experimental import pallas as pl
from jax.experimental.pallas import tpu as pltpu
from jax.sharding import PartitionSpec as P

DH = 128
WINDOW = 256
BLOCK = 512
NEAR = 256
TILE = 128
GROUP = 8
EPSILON = 1e-06
LOG2_E = 1.4426950408889634
BF16 = jnp.bfloat16
F32 = jnp.float32


def dot(a, b):
    return lax.dot_general(a, b, (((1,), (0,)), ((), ())), preferred_element_type=F32)


def dot_nt(a, b):
    return lax.dot_general(a, b, (((1,), (1,)), ((), ())), preferred_element_type=F32)


def local_buckets(tokens):
    blocks = tokens // NEAR
    found = []
    span = 1
    while span < blocks:
        for group in range(1, blocks // span, 2):
            found.append((span, group))
        span *= 2
    return found


def weight_rows(index, table_ref, head, first_level):
    rows = jnp.zeros(index.shape, F32)
    for k in range(table_ref.shape[0]):
        rows = jnp.where(index == k, table_ref[k, head], rows)
    level = lax.broadcasted_iota(jnp.int32, index.shape, 0) + first_level
    return rows * jnp.exp2(-0.5 * level.astype(F32))


def gain_columns(gain_ref):
    return jnp.broadcast_to(gain_ref[0], (DH, DH)).T


def state_kernel(k_ref, v_ref, vt_ref, local_ref, total_ref):
    tokens = k_ref.shape[0]
    blocks = tokens // NEAR
    values_t = v_ref[...].T
    vt_ref[...] = values_t
    states = [
        dot(values_t[:, b * NEAR : (b + 1) * NEAR], k_ref[b * NEAR : (b + 1) * NEAR, :])
        for b in range(blocks)
    ]
    for place, (span, group) in enumerate(local_buckets(tokens)):
        members = states[(group - 1) * span : group * span]
        local_ref[place] = functools.reduce(jnp.add, members).astype(BF16)
    total_ref[...] = functools.reduce(jnp.add, states).astype(BF16)


def tile_mixing(weights):
    shape = (GROUP, TILE)
    row = lax.broadcasted_iota(jnp.int32, shape, 0)
    lane = lax.broadcasted_iota(jnp.int32, shape, 1)
    inner_bits = GROUP.bit_length() - 1
    within = lane % GROUP
    differ = row ^ within
    inner = jnp.where(differ == 0, weights[0:1], 0.0)
    for bit in range(inner_bits):
        inner = jnp.where((differ >> bit == 1) & (row < within), weights[bit + 1 : bit + 2], inner)
    shape = (TILE // GROUP, TILE)
    row = lax.broadcasted_iota(jnp.int32, shape, 0)
    above = lax.broadcasted_iota(jnp.int32, shape, 1) // GROUP
    differ = row ^ above
    outer = jnp.zeros(shape, F32)
    for bit in range((TILE // GROUP).bit_length() - 1):
        level = inner_bits + 1 + bit
        outer = jnp.where((differ >> bit == 1) & (row < above), weights[level : level + 1], outer)
    pieces = [
        jnp.where(lane // GROUP == g, inner, jnp.broadcast_to(outer[g : g + 1], (GROUP, TILE)))
        for g in range(TILE // GROUP)
    ]
    return jnp.concatenate(pieces, axis=0)


def near_kernel(table_ref, index_ref, q_ref, k_ref, vt_ref, local_ref, out_ref):
    tokens = q_ref.shape[0]
    buckets = local_buckets(tokens)
    weights = weight_rows(index_ref[...], table_ref, pl.program_id(0), 0)
    near_bits = NEAR.bit_length() - 1
    for b in range(tokens // NEAR):
        at = slice(b * NEAR, (b + 1) * NEAR)
        queries = q_ref[at, :]
        scores = dot_nt(k_ref[at, :], queries)
        w_block = weights[:, at]
        low = scores[:TILE, :TILE] * tile_mixing(w_block[:, :TILE])
        cross = scores[:TILE, TILE:] * w_block[near_bits : near_bits + 1, TILE:]
        high = scores[TILE:, TILE:] * tile_mixing(w_block[:, TILE:])
        mixed = jnp.concatenate(
            [
                jnp.concatenate([low.astype(BF16), cross.astype(BF16)], axis=1),
                jnp.concatenate([jnp.zeros((TILE, TILE), BF16), high.astype(BF16)], axis=1),
            ],
            axis=0,
        )
        part = dot(vt_ref[:, at], mixed)
        for place, (span, group) in enumerate(buckets):
            if b // span == group:
                level = near_bits + 1 + span.bit_length() - 1
                part = part + dot_nt(local_ref[place], queries) * w_block[level : level + 1]
        out_ref[:, at] = part


def window_kernel(bias_ref, q_ref, k_ref, v_ref, rim_k_ref, rim_v_ref, gain_ref, out_ref, ext_k, ext_vt):
    tokens = k_ref.shape[0]
    pairs = q_ref.shape[1] // DH
    scale = LOG2_E * DH**-0.5

    @pl.when(pl.program_id(1) == 0)
    def _():
        ext_k[:WINDOW, :] = rim_k_ref[...]
        ext_k[WINDOW:, :] = k_ref[...]
        ext_vt[:, :WINDOW] = rim_v_ref[...].T
        ext_vt[:, WINDOW:] = v_ref[...].T

    bias = bias_ref[0]
    key_row = lax.broadcasted_iota(jnp.int32, (TILE, TILE * pairs), 0)
    query_lane = lax.broadcasted_iota(jnp.int32, (TILE, TILE * pairs), 1) % TILE
    causal = key_row <= query_lane
    gains = [jnp.broadcast_to(gain_ref[:, p * DH : (p + 1) * DH], (DH, DH)).T for p in range(pairs)]
    gain = jnp.concatenate(gains, axis=1)
    zero = jnp.zeros((), BF16)
    for b in range(tokens // TILE):
        at = slice(b * TILE, (b + 1) * TILE)
        queries = jnp.concatenate([q_ref[at, p * DH : (p + 1) * DH] for p in range(pairs)], axis=0)
        scores = dot_nt(ext_k[b * TILE : b * TILE + WINDOW + TILE, :], queries)
        oldest, middle, newest = scores[:TILE], scores[TILE : 2 * TILE], scores[2 * TILE :]
        if b * TILE < WINDOW:
            oldest = oldest + bias
        if (b + 1) * TILE < WINDOW:
            middle = middle + bias
        edge = jnp.where(causal, newest, oldest)
        peak = jnp.max(jnp.maximum(edge, middle), axis=0, keepdims=True)
        edge = jnp.exp2((edge - peak) * scale)
        middle = jnp.exp2((middle - peak) * scale)
        total = jnp.sum(edge + middle, axis=0, keepdims=True)
        edge = edge.astype(BF16)
        probs = jnp.concatenate(
            [jnp.where(causal, zero, edge), middle.astype(BF16), jnp.where(causal, edge, zero)], axis=0
        )
        raw = dot(ext_vt[:, b * TILE : b * TILE + WINDOW + TILE], probs)
        mean = jnp.sum(raw * raw, axis=0, keepdims=True) * (1.0 / DH)
        raw = (raw * lax.rsqrt(mean + EPSILON * total * total) * gain).astype(BF16)
        for p in range(pairs):
            out_ref[p * DH : (p + 1) * DH, at] = raw[:, p * TILE : (p + 1) * TILE]


def final_kernel(
    row_ref, mask_ref, table_ref, index_ref, q_ref, near_ref, win_ref, gain_ref, *rest, levels, has_added
):
    bucket_refs = rest[:levels]
    w_ref = rest[levels]
    added_ref = rest[levels + 1] if has_added else None
    out_ref, att, weights_out, sem = rest[levels + 1 + int(has_added) :]
    head = pl.program_id(0)
    copy = pltpu.make_async_copy(w_ref, weights_out, sem)

    @pl.when(head == 0)
    def _():
        copy.start()

    rows = q_ref.shape[0]
    first = index_ref.shape[0] - levels
    weights = weight_rows(index_ref[first:, :], table_ref, head, first)
    stacked = jnp.concatenate([ref[...] for ref in bucket_refs], axis=0)
    reached = dot_nt(stacked, q_ref[...])
    total = near_ref[...].astype(F32)
    for level in range(levels):
        total = total + reached[level * DH : (level + 1) * DH] * (
            weights[level : level + 1] * mask_ref[level]
        )
    mean = jnp.sum(total * total, axis=0, keepdims=True) * (1.0 / DH)
    gain = jnp.concatenate([gain_columns(gain_ref)] * (rows // DH), axis=1)
    total = total * lax.rsqrt(mean + EPSILON) * gain
    att[head] = (total + win_ref[...].astype(F32)).astype(BF16).T

    @pl.when(head == pl.num_programs(0) - 1)
    def _():
        copy.wait()
        heads = att.shape[0]
        attended = jnp.concatenate([att[h] for h in range(heads)], axis=1)
        columns = w_ref.shape[1]
        step = min(columns, 256)
        for c in range(0, columns, step):
            product = dot(attended, weights_out[:, c : c + step])
            if has_added:
                product = product + added_ref[:, c : c + step].astype(F32)
            out_ref[:, c : c + step] = product.astype(BF16)


def whole(shape):
    return pl.BlockSpec(shape, lambda *_: (0,) * len(shape))


SMEM = pl.BlockSpec(memory_space=pltpu.SMEM)


def make_shards(seq_count, head_count):
    def shards(
        queries,
        lin_keys,
        lin_values,
        window_keys,
        window_values,
        level_index,
        level_table,
        seq_lengths,
        gain_linear,
        gain_window,
        w_out,
    ):
        tokens = queries.shape[0]
        heads = level_table.shape[1]
        groups = window_keys.shape[1] // DH
        members = heads // groups
        pairs = 2 if members % 2 == 0 else 1
        levels = seq_count.bit_length() - 1
        buckets = len(local_buckets(tokens))
        shard = lax.axis_index("seq")

        starts = [jnp.int32(0)]
        for s in range(seq_lengths.shape[0] - 1):
            starts.append(starts[-1] + seq_lengths[s])

        def begin_of(index):
            begin = jnp.zeros_like(index)
            for start in starts[1:]:
                begin = jnp.where(start <= index, start, begin)
            return begin

        rim = jnp.concatenate([window_keys[tokens - WINDOW :], window_values[tokens - WINDOW :]], axis=1)
        rim = lax.ppermute(rim, "seq", [(i, (i + 1) % seq_count) for i in range(seq_count)])

        column = pl.BlockSpec((tokens, DH), lambda h: (0, h))
        row = pl.BlockSpec((DH, tokens), lambda h: (h, 0))
        values_t, local_states, state = pl.pallas_call(
            state_kernel,
            grid=(heads,),
            in_specs=[column, column],
            out_specs=[
                row,
                pl.BlockSpec((None, buckets, DH, DH), lambda h: (h, 0, 0, 0)),
                pl.BlockSpec((DH, DH), lambda h: (h, 0)),
            ],
            out_shape=[
                jax.ShapeDtypeStruct((heads * DH, tokens), BF16),
                jax.ShapeDtypeStruct((heads, buckets, DH, DH), BF16),
                jax.ShapeDtypeStruct((heads * DH, DH), BF16),
            ],
            name="states",
        )(lin_keys, lin_values)

        received = []
        for level in range(levels):
            arrived = lax.ppermute(state, "seq", [(i, i ^ (1 << level)) for i in range(seq_count)])
            received.append(arrived)
            if level < levels - 1:
                last = shard | ((2 << level) - 1)
                middle = last - (1 << level)
                joined = (begin_of(last) <= middle).astype(F32)
                right = (shard >> level) % 2 == 1
                own = jnp.where(right, 1.0, joined)
                other = jnp.where(right, joined, 1.0)
                state = (state.astype(F32) * own + arrived.astype(F32) * other).astype(BF16)

        level_ids = jnp.arange(levels, dtype=jnp.int32)
        bit_set = (shard >> level_ids) % 2 == 1
        below = ((shard >> level_ids) << level_ids) - 1
        begin = begin_of(shard)
        mask = (bit_set & (begin <= below)).astype(F32)
        bias = jnp.where(begin == shard, -1e30, 0.0).reshape(1).astype(F32)

        near = pl.pallas_call(
            near_kernel,
            grid=(heads,),
            in_specs=[
                SMEM,
                whole(level_index.shape),
                column,
                column,
                row,
                pl.BlockSpec((None, buckets, DH, DH), lambda h: (h, 0, 0, 0)),
            ],
            out_specs=row,
            out_shape=jax.ShapeDtypeStruct((heads * DH, tokens), F32),
            name="near",
        )(level_table, level_index, queries, lin_keys, values_t, local_states)

        per_group = members // pairs
        windowed = pl.pallas_call(
            window_kernel,
            grid=(groups, per_group),
            in_specs=[
                SMEM,
                pl.BlockSpec((tokens, pairs * DH), lambda g, p: (0, g * per_group + p)),
                pl.BlockSpec((tokens, DH), lambda g, p: (0, g)),
                pl.BlockSpec((tokens, DH), lambda g, p: (0, g)),
                pl.BlockSpec((WINDOW, DH), lambda g, p: (0, g)),
                pl.BlockSpec((WINDOW, DH), lambda g, p: (0, g + groups)),
                pl.BlockSpec((1, pairs * DH), lambda g, p: (0, g * per_group + p)),
            ],
            out_specs=pl.BlockSpec((pairs * DH, tokens), lambda g, p: (g * per_group + p, 0)),
            out_shape=jax.ShapeDtypeStruct((heads * DH, tokens), BF16),
            scratch_shapes=[
                pltpu.VMEM((tokens + WINDOW, DH), BF16),
                pltpu.VMEM((DH, tokens + WINDOW), BF16),
            ],
            name="window",
        )(bias, queries, window_keys, window_values, rim, rim, gain_window.reshape(1, heads * DH))

        rows = tokens // head_count
        width = w_out.shape[1]
        gain_rows = gain_linear.reshape(heads, 1, DH)

        def finish(block, added):
            has_added = added is not None
            bucket = pl.BlockSpec((DH, DH), lambda h, r: (h, 0))
            specs = [
                SMEM,
                SMEM,
                pl.BlockSpec((level_index.shape[0], rows), lambda h, r: (0, r[0])),
                pl.BlockSpec((rows, DH), lambda h, r: (r[0], h)),
                pl.BlockSpec((DH, rows), lambda h, r: (h, r[0])),
                pl.BlockSpec((DH, rows), lambda h, r: (h, r[0])),
                pl.BlockSpec((1, 1, DH), lambda h, r: (h, 0, 0)),
            ]
            specs += [bucket] * levels
            specs += [pl.BlockSpec(memory_space=pl.ANY)]
            operands = [mask, level_table, level_index, queries, near, windowed, gain_rows]
            operands += received + [w_out]
            if has_added:
                specs.append(pl.BlockSpec((rows, width), lambda h, r: (0, 0)))
                operands.append(added)
            return pl.pallas_call(
                functools.partial(final_kernel, levels=levels, has_added=has_added),
                grid_spec=pltpu.PrefetchScalarGridSpec(
                    num_scalar_prefetch=1,
                    grid=(heads,),
                    in_specs=specs,
                    out_specs=pl.BlockSpec((rows, width), lambda h, r: (0, 0)),
                    scratch_shapes=[
                        pltpu.VMEM((heads, rows, DH), BF16),
                        pltpu.VMEM(w_out.shape, BF16),
                        pltpu.SemaphoreType.DMA,
                    ],
                ),
                out_shape=jax.ShapeDtypeStruct((rows, width), BF16),
                name="final",
            )(block.reshape(1), *operands)

        place = lax.axis_index("head")
        arrived = []
        for away in range(1, head_count):
            partial = finish((place + away) % head_count, None)
            arrived.append(
                lax.ppermute(partial, "head", [(i, (i + away) % head_count) for i in range(head_count)])
            )
        own = finish(place, None)
        total = own.astype(F32)
        for part in arrived:
            total = total + part.astype(F32)
        return total.astype(BF16)

    return shards


def solution(mesh):
    placed = (
        P("seq", "head"),
        P("seq", "head"),
        P("seq", "head"),
        P("seq", "head"),
        P("seq", "head"),
        P(None, "seq"),
        P(None, "head"),
        P(),
        P("head"),
        P("head"),
        P("head", None),
    )
    return jax.shard_map(
        make_shards(mesh.shape["seq"], mesh.shape["head"]),
        mesh=mesh,
        in_specs=placed,
        out_specs=P(("seq", "head"), None),
        check_vma=False,
    )
```

time: 175 us -> 94.2 us (0.54)
  the two profiles are of different devices: /device:TPU:0 before, /device:TPU:7 now
where the time goes in v1:
time: 94.2 us; the launch traced here: 92.4 us
  Pallas kernels  54.6 us (58%)
  starting transfers between devices  12.7 us (13%)
  waiting for transfers between devices  10.3 us (11%)
  between operations  7.14 us (8%)
  other arithmetic  5.6 us (6%)
  local copies, waits for them, and re-layouts  2.07 us (2%)
    pallas_call x2, Pallas kernels, finish(): pl.pallas_call(functools.partial(final_kernel, levels=levels, has_added=h...  23.3 us
    pallas_call x1, Pallas kernels, shards(): pl.pallas_call(window_kernel, grid=(groups, per_group), in_specs=[SMEM, p...  14.6 us
    ppermute x4, waiting for transfers between devices, shards(): lax.ppermute(state, 'seq', [(i, i ^ 1 << level) for i in range(seq_count)])  10.2 us
    pallas_call x1, Pallas kernels, shards(): pl.pallas_call(near_kernel, grid=(heads,), in_specs=[SMEM, whole(level_in...  10 us
    ppermute x1, starting transfers between devices, shards(): lax.ppermute(partial, 'head', [(i, (i + away) % head_count) for i in rang...  7.85 us
    pallas_call x1, Pallas kernels, shards(): pl.pallas_call(state_kernel, grid=(heads,), in_specs=[column, column], ou...  6.77 us
    ppermute x4, starting transfers between devices, shards(): lax.ppermute(state, 'seq', [(i, i ^ 1 << level) for i in range(seq_count)])  4.4 us
    convert_element_type x1, other arithmetic, shards(): return total.astype(BF16)  3.69 us
  transfers between devices with their start and end apart: 6, of which 3 were waited for; matrix products, arithmetic and copies ran while one was open for 1% of the time, Pallas kernels for 39%

profile of v1, /device:TPU:7, one launch (start us, length us, event | category | flops | bytes accessed | tf_op | source)
XLA Modules:
  0.0 92.4 jit_solution(17433317617771055190)
XLA Ops:
  0.0 0.0 copy-start.5
  0.0 6.8 %states.1 = (bf16[1024,1024]{1,0:T(8,128)(2,1)}, bf16[8,3,128,128]{3,2,1,0:T(8,128)(2,1)}, bf16[1024,128]{1,0:T(8,128)(2,1)}) custom-call(bf16[1024,1024]{1,0:T(8,128)(2,1)} %k_ref.4, bf16[1024,1024]{1,0:T(8,128)(2,1)} %v_ref.2), custom_call_target="tpu_custom_call" | custom-call | tf_op jit(solution)/shard_map/states/pallas_call | solution.py:253
  6.8 0.0 slice-start
  6.8 0.0 slice-start.1
  6.8 0.3 collective-permute-start.1
  7.1 0.0 copy-done.5
  7.1 0.6 fusion.1
  10.9 3.3 %collective-permute-done.1.rest_0_ = bf16[1024,128]{1,0:T(8,128)(2,1)S(1)} collective-permute-done((bf16[1024,128]{1,0:T(8,128)(2,1)}, bf16[1024,128]{1,0:T(8,128)(2,1)S(1)}, u32[]{:S(2)}, u32[]{:S(2)}) %collective-permute-start.1) | collective-permute-done | bytes 262176 | tf_op jit(solution)/shard_map/ppermute | solution.py:272
  14.2 0.0 copy-start
  14.2 1.1 %add_convert_fusion.3 = bf16[1024,128]{1,0:T(8,128)(2,1)S(1)} fusion(bf16[1024,128]{1,0:T(8,128)(2,1)S(1)} %collective-permute-done.1.rest_0_, bf16[1024,128]{1,0:T(8,128)(2,1)} %get-tuple-element.10, f32[]{:T(128)S(6)} %select_n.95, f32[]{:T(128)S(6)} %select_n.94), kind=kLoop, calls=%fused_computation.3 | loop fusion | flops 786432 | bytes 786440 | tf_op jit(solution)/shard_map/convert_element_type | solution.py:281
  15.4 0.3 collective-permute-start.2
  17.0 4.8 %collective-permute-done.2.rest_1_ = bf16[1024,128]{1,0:T(8,128)(2,1)S(1)} collective-permute-done((bf16[1024,128]{1,0:T(8,128)(2,1)S(1)}, bf16[1024,128]{1,0:T(8,128)(2,1)S(1)}, u32[]{:S(2)}, u32[]{:S(2)}) %collective-permute-start.2) | collective-permute-done | bytes 262176 | tf_op jit(solution)/shard_map/ppermute | solution.py:272
  21.8 0.0 copy-start.1
  21.8 0.1 add_convert_fusion.2
  21.9 1.4 %collective-permute-start.3 = (bf16[1024,128]{1,0:T(8,128)(2,1)S(1)}, bf16[1024,128]{1,0:T(8,128)(2,1)S(1)}, u32[]{:S(2)}, u32[]{:S(2)}) collective-permute-start(bf16[1024,128]{1,0:T(8,128)(2,1)S(1)} %add_convert_fusion.2), channel_id=1, source_target_pairs={{0,8},{2,10},{4,12},{6,14},{8,0},{10,2},{12,4},{14,6},{16,24},{18,... | collective-permute-start | bytes 786440 | tf_op jit(solution)/shard_map/ppermute | solution.py:272
  23.3 0.0 slice-done
  23.3 0.0 slice-done.1
  23.3 0.4 collective-permute-start
  25.1 2.1 %collective-permute-done.3.rest_2_ = bf16[1024,128]{1,0:T(8,128)(2,1)S(1)} collective-permute-done((bf16[1024,128]{1,0:T(8,128)(2,1)S(1)}, bf16[1024,128]{1,0:T(8,128)(2,1)S(1)}, u32[]{:S(2)}, u32[]{:S(2)}) %collective-permute-start.3) | collective-permute-done | bytes 262176 | tf_op jit(solution)/shard_map/ppermute | solution.py:272
  27.2 0.0 copy-start.2
  27.2 0.1 add_convert_fusion.1
  27.3 2.4 %collective-permute-start.4 = (bf16[1024,128]{1,0:T(8,128)(2,1)S(1)}, bf16[1024,128]{1,0:T(8,128)(2,1)S(1)}, u32[]{:S(2)}, u32[]{:S(2)}) collective-permute-start(bf16[1024,128]{1,0:T(8,128)(2,1)S(1)} %add_convert_fusion.1), channel_id=1, source_target_pairs={{0,16},{2,18},{4,20},{6,22},{8,24},{10,26},{12,28},{14,30},{16,0},... | collective-permute-start | bytes 786440 | tf_op jit(solution)/shard_map/ppermute | solution.py:272
  31.0 10.0 %near.1.near_ref = f32[1024,1024]{1,0:T(8,128)} custom-call(f32[8,8]{1,0:T(8,128)} %table_ref.5, s32[15,1024]{1,0:T(8,128)} %index_ref.5, bf16[1024,1024]{1,0:T(8,128)(2,1)} %q_ref.7, bf16[1024,1024]{1,0:T(8,128)(2,1)} %k_ref.4, bf16[1024,1024]{1,0:T(8,128)(2,1)} %get-tuple-element.8.vt_ref, bf16[8,3,128,128]{3,2,1,0:T(8,128)(2,1)} %get-tuple-element.9.local_ref), custom_call_target="tpu_custom_call" | custom-call | tf_op jit(solution)/shard_map/near/pallas_call | solution.py:290
  41.0 0.0 copy-done
  41.0 0.0 copy-done.1
  41.0 0.0 copy-done.2
  41.0 0.5 and_convert_fusion.mask_ref
  41.6 0.0 collective-permute-done.rim_k_ref.rim_v_ref
  41.6 0.0 copy-start.4
  41.6 0.7 copy-done.4
  42.3 14.6 %window.1.win_ref = bf16[1024,1024]{1,0:T(8,128)(2,1)} custom-call(f32[1]{0:T(128)} %bitcast.4.bias_ref, bf16[1024,1024]{1,0:T(8,128)(2,1)} %q_ref.7, bf16[1024,256]{1,0:T(8,128)(2,1)} %k_ref.5, bf16[1024,256]{1,0:T(8,128)(2,1)} %v_ref.3, bf16[256,512]{1,0:T(8,128)(2,1)} %copy-done.4, bf16[256,512]{1,0:T(8,128)(2,1)} %copy-done.4, f32[1,1024]{1,0:T(1,128)} %bitcast.10), custom_call_target="tpu_custom_call" | custom-call | tf_op jit(solution)/shard_map/window/pallas_call | solution.py:307
  56.9 0.0 collective-permute-done.4.rest_3_
  56.9 0.0 copy-start.3
  56.9 0.7 copy-done.3
  57.6 11.6 %final.3 = bf16[512,2048]{1,0:T(8,128)(2,1)} custom-call(s32[1]{0:T(128)} %bitcast.7.row_ref, f32[4]{0:T(128)} %and_convert_fusion.mask_ref, f32[8,8]{1,0:T(8,128)} %table_ref.5, s32[15,1024]{1,0:T(8,128)} %index_ref.5, bf16[1024,1024]{1,0:T(8,128)(2,1)} %q_ref.7, f32[1024,1024]{1,0:T(8,128)} %near.1.near_ref, bf16[1024,1024]{1,0:T(8,128)(2,1)} %window.1.win_ref, ...), custom_call_target="tpu_custom_call" | custom-call | tf_op jit(solution)/shard_map/final/pallas_call | solution.py:351
  69.2 7.8 %collective-permute-start.5 = (bf16[512,2048]{1,0:T(8,128)(2,1)}, bf16[512,2048]{1,0:T(8,128)(2,1)S(1)}, u32[]{:S(2)}, u32[]{:S(2)}) collective-permute-start(bf16[512,2048]{1,0:T(8,128)(2,1)} %final.3), channel_id=1, source_target_pairs={{0,1},{1,0},{2,3},{3,2},{4,5},{5,4},{6,7},{7,6},{8,9},{9,8},{10,11... | collective-permute-start | bytes 6291464 | tf_op jit(solution)/shard_map/ppermute | solution.py:373
  77.0 11.6 %final.2 = bf16[512,2048]{1,0:T(8,128)(2,1)} custom-call(s32[1]{0:T(128)} %bitcast.row_ref, f32[4]{0:T(128)} %and_convert_fusion.mask_ref, f32[8,8]{1,0:T(8,128)} %table_ref.5, s32[15,1024]{1,0:T(8,128)} %index_ref.5, bf16[1024,1024]{1,0:T(8,128)(2,1)} %q_ref.7, f32[1024,1024]{1,0:T(8,128)} %near.1.near_ref, bf16[1024,1024]{1,0:T(8,128)(2,1)} %window.1.win_ref, ...), custom_call_target="tpu_custom_call" | custom-call | tf_op jit(solution)/shard_map/final/pallas_call | solution.py:351
  88.7 0.0 collective-permute-done.5
  88.7 3.7 %add_convert_fusion = bf16[512,2048]{1,0:T(8,128)(2,1)} fusion(bf16[512,2048]{1,0:T(8,128)(2,1)S(1)} %collective-permute-done.5, bf16[512,2048]{1,0:T(8,128)(2,1)} %final.2), kind=kLoop, calls=%fused_computation | loop fusion | flops 4194304 | bytes 6291456 | tf_op jit(solution)/shard_map/convert_element_type | solution.py:379
  (1 shorter events, 0.0 us)
Async XLA Ops:
  0.0 7.1 %copy-start.5 = (s32[4]{0:T(128)S(1)}, s32[4]{0:T(128)}, u32[]{:S(2)}) copy-start(s32[4]{0:T(128)} %param.18) | copy-start | bytes 52
  6.8 16.5 %slice-start = ((bf16[1024,256]{1,0:T(8,128)(2,1)}), bf16[256,256]{1,0:T(8,128)(2,1)S(1)}, s32[]{:S(2)}) async-start(bf16[1024,256]{1,0:T(8,128)(2,1)} %k_ref.5), calls=%async_computation | async-start | bytes 262144 | tf_op jit(solution)/shard_map/slice | solution.py:248
  6.8 16.5 %slice-start.1 = ((bf16[1024,256]{1,0:T(8,128)(2,1)}), bf16[256,256]{1,0:T(8,128)(2,1)S(1)}, s32[]{:S(2)}) async-start(bf16[1024,256]{1,0:T(8,128)(2,1)} %v_ref.3), calls=%async_computation.1 | async-start | bytes 262144 | tf_op jit(solution)/shard_map/slice | solution.py:248
  6.8 7.5 %collective-permute-start.1 = (bf16[1024,128]{1,0:T(8,128)(2,1)}, bf16[1024,128]{1,0:T(8,128)(2,1)S(1)}, u32[]{:S(2)}, u32[]{:S(2)}) collective-permute-start(bf16[1024,128]{1,0:T(8,128)(2,1)} %get-tuple-element.10), channel_id=1, source_target_pairs={{0,2},{2,0},{4,6},{6,4},{8,10},{10,8},{12,14},{14,12},{16,18},{18,... | collective-permute-start | bytes 786440 | tf_op jit(solution)/shard_map/ppermute | solution.py:272
  14.2 26.8 %copy-start = (bf16[1024,128]{1,0:T(8,128)(2,1)}, bf16[1024,128]{1,0:T(8,128)(2,1)S(1)}, u32[]{:S(2)}) copy-start(bf16[1024,128]{1,0:T(8,128)(2,1)S(1)} %collective-permute-done.1.rest_0_) | copy-start | bytes 786436
  15.4 6.4 %collective-permute-start.2 = (bf16[1024,128]{1,0:T(8,128)(2,1)S(1)}, bf16[1024,128]{1,0:T(8,128)(2,1)S(1)}, u32[]{:S(2)}, u32[]{:S(2)}) collective-permute-start(bf16[1024,128]{1,0:T(8,128)(2,1)S(1)} %add_convert_fusion.3), channel_id=1, source_target_pairs={{0,4},{2,6},{4,0},{6,2},{8,12},{10,14},{12,8},{14,10},{16,20},{18,... | collective-permute-start | bytes 786440 | tf_op jit(solution)/shard_map/ppermute | solution.py:272
  21.8 19.2 %copy-start.1 = (bf16[1024,128]{1,0:T(8,128)(2,1)}, bf16[1024,128]{1,0:T(8,128)(2,1)S(1)}, u32[]{:S(2)}) copy-start(bf16[1024,128]{1,0:T(8,128)(2,1)S(1)} %collective-permute-done.2.rest_1_) | copy-start | bytes 786436
  21.9 5.3 %collective-permute-start.3 = (bf16[1024,128]{1,0:T(8,128)(2,1)S(1)}, bf16[1024,128]{1,0:T(8,128)(2,1)S(1)}, u32[]{:S(2)}, u32[]{:S(2)}) collective-permute-start(bf16[1024,128]{1,0:T(8,128)(2,1)S(1)} %add_convert_fusion.2), channel_id=1, source_target_pairs={{0,8},{2,10},{4,12},{6,14},{8,0},{10,2},{12,4},{14,6},{16,24},{18,... | collective-permute-start | bytes 786440 | tf_op jit(solution)/shard_map/ppermute | solution.py:272
  23.3 18.3 %collective-permute-start = (bf16[256,512]{1,0:T(8,128)(2,1)S(1)}, bf16[256,512]{1,0:T(8,128)(2,1)S(1)}, u32[]{:S(2)}, u32[]{:S(2)}) collective-permute-start(bf16[256,512]{1,0:T(8,128)(2,1)S(1)} %pad_maximum_fusion), channel_id=1, source_target_pairs={{0,2},{2,4},{4,6},{6,8},{8,10},{10,12},{12,14},{14,16},{16,18},{18... | collective-permute-start | bytes 786440 | tf_op jit(solution)/shard_map/ppermute | solution.py:249
  27.2 13.8 %copy-start.2 = (bf16[1024,128]{1,0:T(8,128)(2,1)}, bf16[1024,128]{1,0:T(8,128)(2,1)S(1)}, u32[]{:S(2)}) copy-start(bf16[1024,128]{1,0:T(8,128)(2,1)S(1)} %collective-permute-done.3.rest_2_) | copy-start | bytes 786436
  27.3 29.6 %collective-permute-start.4 = (bf16[1024,128]{1,0:T(8,128)(2,1)S(1)}, bf16[1024,128]{1,0:T(8,128)(2,1)S(1)}, u32[]{:S(2)}, u32[]{:S(2)}) collective-permute-start(bf16[1024,128]{1,0:T(8,128)(2,1)S(1)} %add_convert_fusion.1), channel_id=1, source_target_pairs={{0,16},{2,18},{4,20},{6,22},{8,24},{10,26},{12,28},{14,30},{16,0},... | collective-permute-start | bytes 786440 | tf_op jit(solution)/shard_map/ppermute | solution.py:272
  41.6 0.7 copy-start.4
  56.9 0.7 copy-start.3
  69.2 19.5 %collective-permute-start.5 = (bf16[512,2048]{1,0:T(8,128)(2,1)}, bf16[512,2048]{1,0:T(8,128)(2,1)S(1)}, u32[]{:S(2)}, u32[]{:S(2)}) collective-permute-start(bf16[512,2048]{1,0:T(8,128)(2,1)} %final.3), channel_id=1, source_target_pairs={{0,1},{1,0},{2,3},{3,2},{4,5},{5,4},{6,7},{7,6},{8,9},{9,8},{10,11... | collective-permute-start | bytes 6291464 | tf_op jit(solution)/shard_map/ppermute | solution.py:373

commit v2 on v0

v2 whole, which is shorter than its diff:
```python
import functools

import jax
import jax.numpy as jnp
from jax import lax
from jax.experimental import pallas as pl
from jax.experimental.pallas import tpu as pltpu
from jax.sharding import PartitionSpec as P

DH = 128
WINDOW = 256
BLOCK = 512
NEAR = 256
TILE = 128
GROUP = 8
EPSILON = 1e-06
LOG2_E = 1.4426950408889634
MEGABYTE = 1 << 20
BF16 = jnp.bfloat16
F32 = jnp.float32


def dot(a, b):
    return lax.dot_general(a, b, (((1,), (0,)), ((), ())), preferred_element_type=F32)


def dot_nt(a, b):
    return lax.dot_general(a, b, (((1,), (1,)), ((), ())), preferred_element_type=F32)


def local_spans(tokens):
    spans = []
    span = 1
    while span < tokens // NEAR:
        spans.append(span)
        span *= 2
    return spans


def local_buckets(tokens):
    blocks = tokens // NEAR
    return [(span, group) for span in local_spans(tokens) for group in range(1, blocks // span, 2)]


def weight_rows(index, table_ref, head, first_level):
    rows = jnp.zeros(index.shape, F32)
    for k in range(table_ref.shape[0]):
        rows = jnp.where(index == k, table_ref[k, head], rows)
    level = lax.broadcasted_iota(jnp.int32, index.shape, 0) + first_level
    return rows * jnp.exp2(-0.5 * level.astype(F32))


def head_columns(h):
    return slice(h * DH, (h + 1) * DH)


def state_kernel(
    lengths_ref, k_hbm, v_hbm, k_ref, v_ref, local_ref, total_ref, flags_ref, states, sems, *, levels
):
    blocks = states.shape[0]
    heads = k_ref.shape[1] // DH
    copies = []
    for b in range(blocks):
        rows = pl.ds(b * NEAR, NEAR)
        pair = [
            pltpu.make_async_copy(k_hbm.at[rows], k_ref.at[rows], sems.at[0, b]),
            pltpu.make_async_copy(v_hbm.at[rows], v_ref.at[rows], sems.at[1, b]),
        ]
        for copy in pair:
            copy.start()
        copies.append(pair)
    for b in range(blocks):
        rows = slice(b * NEAR, (b + 1) * NEAR)
        for copy in copies[b]:
            copy.wait()
        for h in range(heads):
            at = head_columns(h)
            states[b, at, :] = dot(v_ref[rows, at].T, k_ref[rows, at])
    for place, (span, group) in enumerate(local_buckets(blocks * NEAR)):
        members = [states[b] for b in range((group - 1) * span, group * span)]
        local_ref[place] = functools.reduce(jnp.add, members).astype(BF16)
    total_ref[...] = functools.reduce(jnp.add, [states[b] for b in range(blocks)]).astype(BF16)

    shard = lax.axis_index("seq")
    starts = [jnp.int32(0)]
    for s in range(lengths_ref.shape[0] - 1):
        starts.append(starts[-1] + lengths_ref[s])

    def begin_of(index):
        begin = jnp.int32(0)
        for start in starts[1:]:
            begin = jnp.where(start <= index, start, begin)
        return begin

    begin = begin_of(shard)
    for level in range(levels):
        last = shard | ((2 << level) - 1)
        middle = last - (1 << level)
        joined = jnp.where(begin_of(last) <= middle, 1.0, 0.0)
        right = (shard & (1 << level)) != 0
        flags_ref[0, level] = jnp.where(right, 1.0, joined)
        flags_ref[1, level] = jnp.where(right, joined, 1.0)
        flags_ref[2, level] = jnp.where(right & (begin <= middle), 1.0, 0.0)
    for row in range(3):
        flags_ref[row, levels] = jnp.where(begin == shard, -1e30, 0.0)


def join_kernel(flags_ref, own_ref, arrived_ref, *rest, level):
    own, arrived = own_ref[...].astype(F32), arrived_ref[...].astype(F32)
    rest[-1][...] = (own * flags_ref[0, level] + arrived * flags_ref[1, level]).astype(BF16)


def tile_mixing(weights):
    shape = (GROUP, TILE)
    row = lax.broadcasted_iota(jnp.int32, shape, 0)
    lane = lax.broadcasted_iota(jnp.int32, shape, 1)
    inner_bits = GROUP.bit_length() - 1
    within = lane % GROUP
    differ = row ^ within
    inner = jnp.where(differ == 0, weights[0:1], 0.0)
    for bit in range(inner_bits):
        inner = jnp.where((differ >> bit == 1) & (row < within), weights[bit + 1 : bit + 2], inner)
    shape = (TILE // GROUP, TILE)
    row = lax.broadcasted_iota(jnp.int32, shape, 0)
    above = lax.broadcasted_iota(jnp.int32, shape, 1) // GROUP
    differ = row ^ above
    outer = jnp.zeros(shape, F32)
    for bit in range((TILE // GROUP).bit_length() - 1):
        level = inner_bits + 1 + bit
        outer = jnp.where((differ >> bit == 1) & (row < above), weights[level : level + 1], outer)
    pieces = [
        jnp.where(lane // GROUP == g, inner, jnp.broadcast_to(outer[g : g + 1], (GROUP, TILE)))
        for g in range(TILE // GROUP)
    ]
    return jnp.concatenate(pieces, axis=0)


def near_kernel(table_ref, index_ref, q_ref, k_ref, v_ref, local_ref, *rest, spans, start):
    out_ref = rest[-1]
    block = start + pl.program_id(0)
    blocks, width, _ = out_ref.shape
    near_bits = NEAR.bit_length() - 1
    tokens = pl.ds(pl.multiple_of(block * NEAR, NEAR), NEAR)
    index = index_ref[:, tokens]
    places, present = [], []
    first = 0
    for span in spans:
        group = block // span
        places.append(first + group // 2)
        present.append((group % 2).astype(F32))
        first += blocks // span // 2
    for h in range(width // DH):
        at = head_columns(h)
        weights = weight_rows(index, table_ref, h, 0)
        queries_t = q_ref[tokens, at].T
        scores = dot(k_ref[tokens, at], queries_t)
        low = scores[:TILE, :TILE] * tile_mixing(weights[:, :TILE])
        cross = scores[:TILE, TILE:] * weights[near_bits : near_bits + 1, TILE:]
        high = scores[TILE:, TILE:] * tile_mixing(weights[:, TILE:])
        lhs = [v_ref[tokens, at].T]
        rhs = [
            jnp.concatenate([low.astype(BF16), cross.astype(BF16)], axis=1),
            jnp.concatenate([jnp.zeros((TILE, TILE), BF16), high.astype(BF16)], axis=1),
        ]
        for i, place in enumerate(places):
            level = near_bits + 1 + i
            row = (weights[level : level + 1] * present[i]).astype(BF16)
            lhs.append(local_ref[place, at, :])
            rhs.append(queries_t * row)
        out_ref[block, at, :] = dot(jnp.concatenate(lhs, axis=1), jnp.concatenate(rhs, axis=0))


def gain_column(gain_ref, h):
    return jnp.broadcast_to(gain_ref[h], (DH, DH)).T


def window_kernel(flags_ref, q_ref, k_ref, v_ref, gain_ref, *rest, has_rim, members, start):
    out_ref, gains = rest[-2:]
    block = start + pl.program_id(0)
    heads = q_ref.shape[1] // DH
    scale = LOG2_E * DH**-0.5

    @pl.when(pl.program_id(0) == 0)
    def _():
        for h in range(heads):
            gains[h] = gain_column(gain_ref, h)

    key_row = lax.broadcasted_iota(jnp.int32, (TILE, TILE), 0)
    query_lane = lax.broadcasted_iota(jnp.int32, (TILE, TILE), 1)
    causal = key_row <= query_lane
    lower = jnp.where(causal, 1.0, 0.0).astype(BF16)
    now = pl.multiple_of(block * NEAR, NEAR)
    if has_rim:
        bias = flags_ref[0, flags_ref.shape[1] - 1]
    for g in range(heads // members):
        at = head_columns(g)
        if has_rim:
            rim_ref = rest[0]
            old_k = rim_ref[:, at]
            old_v = rim_ref[:, head_columns(g + heads // members)]
        else:
            old_k = k_ref[pl.ds(now - WINDOW, WINDOW), at]
            old_v = v_ref[pl.ds(now - WINDOW, WINDOW), at]
        keys = jnp.concatenate([old_k, k_ref[pl.ds(now, NEAR), at]], axis=0)
        values_t = jnp.concatenate([old_v.T, v_ref[pl.ds(now, NEAR), at].T], axis=1)
        for h in range(g * members, (g + 1) * members):
            for tile in range(NEAR // TILE):
                queries = q_ref[pl.ds(now + tile * TILE, TILE), head_columns(h)]
                span = slice(tile * TILE, tile * TILE + WINDOW + TILE)
                scores = dot_nt(keys[span], queries)
                oldest, middle, newest = scores[:TILE], scores[TILE : 2 * TILE], scores[2 * TILE :]
                if has_rim:
                    oldest = oldest + bias
                    if tile == 0:
                        middle = middle + bias
                edge = jnp.where(causal, newest, oldest)
                peak = jnp.max(jnp.maximum(edge, middle), axis=0, keepdims=True)
                edge = jnp.exp2((edge - peak) * scale)
                middle = jnp.exp2((middle - peak) * scale)
                total = jnp.sum(edge + middle, axis=0, keepdims=True)
                edge = edge.astype(BF16)
                newest = edge * lower
                probs = jnp.concatenate([edge - newest, middle.astype(BF16), newest], axis=0)
                raw = dot(values_t[:, span], probs)
                mean = jnp.sum(raw * raw, axis=0, keepdims=True) * (1.0 / DH)
                scaled = raw * lax.rsqrt(mean + EPSILON * total * total) * gains[h]
                out_ref[block, head_columns(h), tile * TILE : (tile + 1) * TILE] = scaled.astype(BF16)


def attend_block(block, flags_ref, table_ref, index_ref, q_ref, near_ref, win_ref, gain_ref, bucket_refs):
    levels = len(bucket_refs)
    width = q_ref.shape[1]
    first = index_ref.shape[0] - levels
    tokens = pl.ds(pl.multiple_of(block * NEAR, NEAR), NEAR)
    index = index_ref[first:, tokens]
    attended = []
    for h in range(width // DH):
        at = head_columns(h)
        weights = weight_rows(index, table_ref, h, first)
        queries_t = q_ref[tokens, at].T
        lhs, rhs = [], []
        for level in range(levels):
            row = (weights[level : level + 1] * flags_ref[2, level]).astype(BF16)
            lhs.append(bucket_refs[level][at, :])
            rhs.append(queries_t * row)
        total = near_ref[block, at, :] + dot(jnp.concatenate(lhs, axis=1), jnp.concatenate(rhs, axis=0))
        mean = jnp.sum(total * total, axis=0, keepdims=True) * (1.0 / DH)
        gain = gain_column(gain_ref, h)
        gain = jnp.concatenate([gain] * (NEAR // DH), axis=1)
        total = total * lax.rsqrt(mean + EPSILON) * gain
        attended.append((total + win_ref[block, at, :].astype(F32)).astype(BF16).T)
    return jnp.concatenate(attended, axis=1)


def project(attended, w_ref, added, out_ref):
    step = 2 * DH
    for c in range(0, w_ref.shape[1], step):
        product = dot(attended, w_ref[:, c : c + step])
        for part in added:
            product = product + part[:, c : c + step].astype(F32)
        out_ref[:, c : c + step] = product.astype(BF16)


def first_block(away, head_count, pieces):
    return lax.rem(lax.axis_index("head") + away, head_count) * pieces


def partial_kernel(*refs, levels, away, head_count, pieces, piece):
    block = first_block(away, head_count, pieces) + piece
    project(attend_block(block, *refs[:7], refs[7 : 7 + levels]), refs[7 + levels], [], refs[-1])


def attend_kernel(*refs, levels, head_count, pieces):
    block = first_block(0, head_count, pieces) + pl.program_id(0)
    rows = pl.ds(pl.multiple_of(pl.program_id(0) * NEAR, NEAR), NEAR)
    refs[-1][rows, :] = attend_block(block, *refs[:7], refs[7 : 7 + levels])


def project_kernel(attended_ref, w_ref, *refs):
    added, out_ref = refs[:-1], refs[-1]
    pieces = len(added) * NEAR // out_ref.shape[0]
    for piece in range(out_ref.shape[0] // NEAR):
        rows = slice(piece * NEAR, (piece + 1) * NEAR)
        product = dot(attended_ref[rows, :], w_ref[...])
        for part in added[piece::out_ref.shape[0] // NEAR]:
            product = product + part[...].astype(F32)
        out_ref[rows, :] = product.astype(BF16)


def in_hbm(array):
    return pltpu.with_memory_space_constraint(array, pltpu.HBM)


SMEM = pl.BlockSpec(memory_space=pltpu.SMEM)
VMEM = pl.BlockSpec(memory_space=pltpu.VMEM)
HELD = pl.BlockSpec(memory_space=pl.ANY)


def make_shards(seq_count, head_count):
    def shards(
        queries,
        lin_keys,
        lin_values,
        window_keys,
        window_values,
        level_index,
        level_table,
        seq_lengths,
        gain_linear,
        gain_window,
        w_out,
    ):
        tokens, width_in = queries.shape
        heads = level_table.shape[1]
        groups = window_keys.shape[1] // DH
        members = heads // groups
        levels = seq_count.bit_length() - 1
        blocks = tokens // NEAR
        buckets = len(local_buckets(tokens))

        def params(megabytes):
            return pltpu.CompilerParams(vmem_limit_bytes=megabytes * MEGABYTE)

        keys, values, local_states, state, flags = pl.pallas_call(
            functools.partial(state_kernel, levels=levels),
            in_specs=[SMEM, HELD, HELD],
            out_specs=[VMEM, VMEM, VMEM, VMEM, SMEM],
            out_shape=[
                jax.ShapeDtypeStruct(lin_keys.shape, BF16),
                jax.ShapeDtypeStruct(lin_values.shape, BF16),
                jax.ShapeDtypeStruct((buckets, width_in, DH), BF16),
                jax.ShapeDtypeStruct((width_in, DH), BF16),
                jax.ShapeDtypeStruct((3, levels + 1), F32),
            ],
            scratch_shapes=[
                pltpu.VMEM((blocks, width_in, DH), F32),
                pltpu.SemaphoreType.DMA((2, blocks)),
            ],
            compiler_params=params(16),
            name="states",
        )(seq_lengths, in_hbm(lin_keys), in_hbm(lin_values))

        rim = jnp.concatenate([window_keys[tokens - WINDOW :], window_values[tokens - WINDOW :]], axis=1)

        def exchanged(level, state):
            return lax.ppermute(state, "seq", [(i, i ^ (1 << level)) for i in range(seq_count)])

        def joined(level, state, arrived, cover):
            return pl.pallas_call(
                functools.partial(join_kernel, level=level),
                in_specs=[SMEM, VMEM, VMEM] + [HELD] * len(cover),
                out_specs=VMEM,
                out_shape=jax.ShapeDtypeStruct(state.shape, BF16),
                compiler_params=params(4),
                name="join",
            )(flags, state, arrived, *cover)

        def neared(start, count, base):
            operands = [level_table, level_index, queries, keys, values, local_states]
            specs = [SMEM] + [VMEM] * 5
            aliases = {}
            if base is not None:
                aliases = {len(operands): 0}
                operands.append(base)
                specs.append(VMEM)
            return pl.pallas_call(
                functools.partial(near_kernel, spans=local_spans(tokens), start=start),
                grid=(count,),
                in_specs=specs,
                out_specs=VMEM,
                out_shape=jax.ShapeDtypeStruct((blocks, width_in, NEAR), F32),
                input_output_aliases=aliases,
                compiler_params=params(8),
                name="near",
            )(*operands)

        window_gains = gain_window.reshape(heads, 1, DH)

        def windowed(start, count, rim, base):
            operands = [flags, queries, window_keys, window_values, window_gains]
            specs = [SMEM] + [VMEM] * 4
            aliases = {}
            if rim is not None:
                operands.append(rim)
                specs.append(VMEM)
            if base is not None:
                aliases = {len(operands): 0}
                operands.append(base)
                specs.append(VMEM)
            return pl.pallas_call(
                functools.partial(window_kernel, has_rim=rim is not None, members=members, start=start),
                grid=(count,),
                in_specs=specs,
                out_specs=VMEM,
                scratch_shapes=[pltpu.VMEM((heads, DH, DH), F32)],
                out_shape=jax.ShapeDtypeStruct((blocks, width_in, NEAR), BF16),
                input_output_aliases=aliases,
                compiler_params=params(8),
                name="window",
            )(*operands)

        received = [exchanged(0, state)]
        near = neared(0, blocks, None)
        state = joined(0, state, received[0], [near])
        received.append(exchanged(1, state))
        windows = windowed(1, blocks - 1, None, None)
        cover = [windows]
        for level in range(1, levels - 1):
            state = joined(level, state, received[level], cover)
            received.append(exchanged(level + 1, state))
            cover = []
        rim = lax.ppermute(rim, "seq", [(i, (i + 1) % seq_count) for i in range(seq_count)])
        windows = windowed(0, 1, rim, windows)

        pieces = tokens // head_count // NEAR
        width = w_out.shape[1]
        shared = [flags, level_table, level_index, queries, near, windows]
        shared += [gain_linear.reshape(heads, 1, DH)] + received
        specs = [SMEM, SMEM] + [VMEM] * (5 + levels)

        arrived = []
        for away in range(1, head_count):
            route = [(i, (i + away) % head_count) for i in range(head_count)]
            for piece in range(pieces):
                partial = pl.pallas_call(
                    functools.partial(
                        partial_kernel,
                        levels=levels,
                        away=away,
                        head_count=head_count,
                        pieces=pieces,
                        piece=piece,
                    ),
                    in_specs=specs + [VMEM],
                    out_specs=VMEM,
                    out_shape=jax.ShapeDtypeStruct((NEAR, width), BF16),
                    compiler_params=params(8),
                    name="partial",
                )(*shared, w_out)
                arrived.append(lax.ppermute(partial, "head", route))
        attended = pl.pallas_call(
            functools.partial(attend_kernel, levels=levels, head_count=head_count, pieces=pieces),
            grid=(pieces,),
            in_specs=specs,
            out_specs=VMEM,
            out_shape=jax.ShapeDtypeStruct((pieces * NEAR, width_in), BF16),
            compiler_params=params(8),
            name="attend",
        )(*shared)
        step = 512
        return pl.pallas_call(
            project_kernel,
            grid=(width // step,),
            in_specs=[pl.BlockSpec((pieces * NEAR, width_in), lambda c: (0, 0))]
            + [pl.BlockSpec((width_in, step), lambda c: (0, c))]
            + [pl.BlockSpec((NEAR, step), lambda c: (0, c))] * len(arrived),
            out_specs=pl.BlockSpec((pieces * NEAR, step), lambda c: (0, c)),
            out_shape=jax.ShapeDtypeStruct((pieces * NEAR, width), BF16),
            compiler_params=params(12),
            name="project",
        )(attended, w_out, *arrived)

    return shards


def solution(mesh):
    placed = (
        P("seq", "head"),
        P("seq", "head"),
        P("seq", "head"),
        P("seq", "head"),
        P("seq", "head"),
        P(None, "seq"),
        P(None, "head"),
        P(),
        P("head"),
        P("head"),
        P("head", None),
    )
    return jax.shard_map(
        make_shards(mesh.shape["seq"], mesh.shape["head"]),
        mesh=mesh,
        in_specs=placed,
        out_specs=P(("seq", "head"), None),
        check_vma=False,
    )
```

time: 175 us -> 57.7 us (0.33)
  the two profiles are of different devices: /device:TPU:0 before, /device:TPU:7 now
where the time goes in v2:
time: 57.7 us; the launch traced here: 57.6 us
  Pallas kernels  28.6 us (50%)
  waiting for transfers between devices  20.5 us (36%)
  starting transfers between devices  7.19 us (12%)
  local copies, waits for them, and re-layouts  1.08 us (2%)
    ppermute x4, waiting for transfers between devices, exchanged(): lax.ppermute(state, 'seq', [(i, i ^ 1 << level) for i in range(seq_count)])  18.3 us
    pallas_call x2, Pallas kernels, windowed(): pl.pallas_call(functools.partial(window_kernel, has_rim=rim is not None,...  6.83 us
    pallas_call x2, Pallas kernels, shards(): pl.pallas_call(functools.partial(partial_kernel, levels=levels, away=away...  5.04 us
    pallas_call x1, Pallas kernels, neared(): pl.pallas_call(functools.partial(near_kernel, spans=local_spans(tokens),...  4.46 us
    ppermute x4, starting transfers between devices, exchanged(): lax.ppermute(state, 'seq', [(i, i ^ 1 << level) for i in range(seq_count)])  4.3 us
    pallas_call x1, Pallas kernels, shards(): pl.pallas_call(project_kernel, grid=(width // step,), in_specs=[pl.BlockS...  4.17 us
    pallas_call x1, Pallas kernels, shards(): pl.pallas_call(functools.partial(state_kernel, levels=levels), in_specs=[...  3.85 us
    ppermute x2, starting transfers between devices, shards(): arrived.append(lax.ppermute(partial, 'head', route))  2.44 us
  transfers between devices with their start and end apart: 7, of which 6 were waited for; matrix products, arithmetic and copies ran while one was open for 0% of the time, Pallas kernels for 29%

profile of v2, /device:TPU:7, one launch (start us, length us, event | category | flops | bytes accessed | tf_op | source)
XLA Modules:
  0.0 57.6 jit_solution(18220023819441503616)
XLA Ops:
  0.0 0.0 copy-start
  0.0 0.0 copy-start.5
  0.0 0.0 copy-start.4
  0.0 0.0 copy-start.8
  0.0 0.8 %copy-done.8 = s32[4]{0:T(128)S(1)} copy-done((s32[4]{0:T(128)S(1)}, s32[4]{0:T(128)}, u32[]{:S(2)}) %copy-start.8) | copy-done | bytes 40
  0.8 3.9 %states.1 = (bf16[1024,1024]{1,0:T(8,128)(2,1)S(1)}, bf16[1024,1024]{1,0:T(8,128)(2,1)S(1)}, bf16[3,1024,128]{2,1,0:T(8,128)(2,1)S(1)}, bf16[1024,128]{1,0:T(8,128)(2,1)S(1)}, f32[3,5]{1,0:T(4,128)S(1)}) custom-call(s32[4]{0:T(128)S(1)} %copy-done.8, bf16[1024,1024]{1,0:T(8,128)(2,1)} %k_hbm.1, bf16[1024,1024]{1,0:T(8,128)(2,1)} %v_hbm.1), custom_call_target="tpu_custom_call" | custom-call | tf_op jit(solution)/shard_map/states/pallas_call | solution.py:324
  4.7 0.3 collective-permute-start.1
  5.0 0.0 copy-done
  5.0 0.0 copy-done.5
  5.0 0.0 copy-done.4
  5.0 4.5 %near.1.rest_0_.refs_4_ = f32[4,1024,256]{2,1,0:T(8,128)S(1)} custom-call(f32[8,8]{1,0:T(8,128)S(1)} %copy-done.5, s32[15,1024]{1,0:T(8,128)S(1)} %copy-done.4, bf16[1024,1024]{1,0:T(8,128)(2,1)S(1)} %copy-done, bf16[1024,1024]{1,0:T(8,128)(2,1)S(1)} %get-tuple-element.11.k_ref, bf16[1024,1024]{1,0:T(8,128)(2,1)S(1)} %get-tuple-element.12.v_ref, ...), custom_call_target="tpu_custom_call" | custom-call | tf_op jit(solution)/shard_map/near/pallas_call | solution.py:366
  9.5 2.5 %collective-permute-done.1.arrived_ref.refs_7_ = bf16[1024,128]{1,0:T(8,128)(2,1)S(1)} collective-permute-done((bf16[1024,128]{1,0:T(8,128)(2,1)S(1)}, bf16[1024,128]{1,0:T(8,128)(2,1)S(1)}, u32[]{:S(2)}, u32[]{:S(2)}) %collective-permute-start.1) | collective-permute-done | bytes 262176 | tf_op jit(solution)/shard_map/ppermute | solution.py:346
  11.9 0.0 copy-start.2
  11.9 0.0 copy-start.3
  11.9 0.0 copy-start.7
  11.9 0.7 %join.3.own_ref = bf16[1024,128]{1,0:T(8,128)(2,1)S(1)} custom-call(f32[3,5]{1,0:T(4,128)S(1)} %get-tuple-element.10.flags_ref.refs_0_, bf16[1024,128]{1,0:T(8,128)(2,1)S(1)} %get-tuple-element.14.own_ref, bf16[1024,128]{1,0:T(8,128)(2,1)S(1)} %collective-permute-done.1.arrived_ref.refs_7_, f32[4,1024,256]{2,1,0:T(8,128)S(1)} %near.1.rest_0_.refs_4_), custom_call_target="tpu_custom_call" | custom-call | tf_op jit(solution)/shard_map/join/pallas_call | solution.py:349
  12.6 0.3 collective-permute-start.2
  12.9 0.1 copy-done.2
  13.0 0.2 copy-done.3
  13.1 0.0 copy-done.7
  13.1 4.9 %window.2.rest_1_.rest_0_ = bf16[4,1024,256]{2,1,0:T(8,128)(2,1)S(1)} custom-call(f32[3,5]{1,0:T(4,128)S(1)} %get-tuple-element.10.flags_ref.refs_0_, bf16[1024,1024]{1,0:T(8,128)(2,1)S(1)} %copy-done, bf16[1024,256]{1,0:T(8,128)(2,1)S(1)} %copy-done.2, bf16[1024,256]{1,0:T(8,128)(2,1)S(1)} %copy-done.3, f32[8,1,128]{2,1,0:T(1,128)S(1)} %bitcast.5), custom_call_target="tpu_custom_call" | custom-call | tf_op jit(solution)/shard_map/window/pallas_call | solution.py:390
  18.0 0.0 slice-start
  18.1 0.0 slice-start.1
  18.1 0.9 %collective-permute-done.2.arrived_ref.refs_8_ = bf16[1024,128]{1,0:T(8,128)(2,1)S(1)} collective-permute-done((bf16[1024,128]{1,0:T(8,128)(2,1)S(1)}, bf16[1024,128]{1,0:T(8,128)(2,1)S(1)}, u32[]{:S(2)}, u32[]{:S(2)}) %collective-permute-start.2) | collective-permute-done | bytes 262176 | tf_op jit(solution)/shard_map/ppermute | solution.py:346
  19.0 0.7 %join.4.own_ref = bf16[1024,128]{1,0:T(8,128)(2,1)S(1)} custom-call(f32[3,5]{1,0:T(4,128)S(1)} %get-tuple-element.10.flags_ref.refs_0_, bf16[1024,128]{1,0:T(8,128)(2,1)S(1)} %join.3.own_ref, bf16[1024,128]{1,0:T(8,128)(2,1)S(1)} %collective-permute-done.2.arrived_ref.refs_8_, bf16[4,1024,256]{2,1,0:T(8,128)(2,1)S(1)} %window.2.rest_1_.rest_0_), custom_call_target="tpu_custom_call" | custom-call | tf_op jit(solution)/shard_map/join/pallas_call | solution.py:349
  19.7 1.3 %collective-permute-start.3 = (bf16[1024,128]{1,0:T(8,128)(2,1)S(1)}, bf16[1024,128]{1,0:T(8,128)(2,1)S(1)}, u32[]{:S(2)}, u32[]{:S(2)}) collective-permute-start(bf16[1024,128]{1,0:T(8,128)(2,1)S(1)} %join.4.own_ref), channel_id=1, source_target_pairs={{0,8},{2,10},{4,12},{6,14},{8,0},{10,2},{12,4},{14,6},{16,24},{18,... | collective-permute-start | bytes 786440 | tf_op jit(solution)/shard_map/ppermute | solution.py:346
  21.0 0.0 slice-done
  21.0 0.0 slice-done.1
  21.1 0.4 collective-permute-start
  21.5 3.5 %collective-permute-done.3.arrived_ref.refs_9_ = bf16[1024,128]{1,0:T(8,128)(2,1)S(1)} collective-permute-done((bf16[1024,128]{1,0:T(8,128)(2,1)S(1)}, bf16[1024,128]{1,0:T(8,128)(2,1)S(1)}, u32[]{:S(2)}, u32[]{:S(2)}) %collective-permute-start.3) | collective-permute-done | bytes 262176 | tf_op jit(solution)/shard_map/ppermute | solution.py:346
  25.0 0.7 %join.5 = bf16[1024,128]{1,0:T(8,128)(2,1)S(1)} custom-call(f32[3,5]{1,0:T(4,128)S(1)} %get-tuple-element.10.flags_ref.refs_0_, bf16[1024,128]{1,0:T(8,128)(2,1)S(1)} %join.4.own_ref, bf16[1024,128]{1,0:T(8,128)(2,1)S(1)} %collective-permute-done.3.arrived_ref.refs_9_), custom_call_target="tpu_custom_call" | custom-call | tf_op jit(solution)/shard_map/join/pallas_call | solution.py:349
  25.6 0.0 copy-start.1
  25.6 0.0 copy-start.6
  25.7 2.4 %collective-permute-start.4 = (bf16[1024,128]{1,0:T(8,128)(2,1)S(1)}, bf16[1024,128]{1,0:T(8,128)(2,1)S(1)}, u32[]{:S(2)}, u32[]{:S(2)}) collective-permute-start(bf16[1024,128]{1,0:T(8,128)(2,1)S(1)} %join.5), channel_id=1, source_target_pairs={{0,16},{2,18},{4,20},{6,22},{8,24},{10,26},{12,28},{14,30},{16,0},... | collective-permute-start | bytes 786440 | tf_op jit(solution)/shard_map/ppermute | solution.py:346
  28.0 1.9 %collective-permute-done.rest_0_ = bf16[256,512]{1,0:T(8,128)(2,1)S(1)} collective-permute-done((bf16[256,512]{1,0:T(8,128)(2,1)S(1)}, bf16[256,512]{1,0:T(8,128)(2,1)S(1)}, u32[]{:S(2)}, u32[]{:S(2)}) %collective-permute-start) | collective-permute-done | bytes 262176 | tf_op jit(solution)/shard_map/ppermute | solution.py:412
  29.9 1.9 %window.3.refs_5_ = bf16[4,1024,256]{2,1,0:T(8,128)(2,1)S(1)} custom-call(f32[3,5]{1,0:T(4,128)S(1)} %get-tuple-element.10.flags_ref.refs_0_, bf16[1024,1024]{1,0:T(8,128)(2,1)S(1)} %copy-done, bf16[1024,256]{1,0:T(8,128)(2,1)S(1)} %copy-done.2, bf16[1024,256]{1,0:T(8,128)(2,1)S(1)} %copy-done.3, ...), custom_call_target="tpu_custom_call", output_to_operand_aliasing={{}: (6, {})} | custom-call | tf_op jit(solution)/shard_map/window/pallas_call | solution.py:390
  31.9 11.4 %collective-permute-done.4.refs_10_ = bf16[1024,128]{1,0:T(8,128)(2,1)S(1)} collective-permute-done((bf16[1024,128]{1,0:T(8,128)(2,1)S(1)}, bf16[1024,128]{1,0:T(8,128)(2,1)S(1)}, u32[]{:S(2)}, u32[]{:S(2)}) %collective-permute-start.4) | collective-permute-done | bytes 262176 | tf_op jit(solution)/shard_map/ppermute | solution.py:346
  43.2 0.0 copy-done.1
  43.2 0.0 copy-done.6
  43.2 2.5 %partial.2 = bf16[256,2048]{1,0:T(8,128)(2,1)S(1)} custom-call(f32[3,5]{1,0:T(4,128)S(1)} %get-tuple-element.10.flags_ref.refs_0_, f32[8,8]{1,0:T(8,128)S(1)} %copy-done.5, s32[15,1024]{1,0:T(8,128)S(1)} %copy-done.4, bf16[1024,1024]{1,0:T(8,128)(2,1)S(1)} %copy-done, f32[4,1024,256]{2,1,0:T(8,128)S(1)} %near.1.rest_0_.refs_4_, ...), custom_call_target="tpu_custom_call" | custom-call | tf_op jit(solution)/shard_map/partial/pallas_call | solution.py:425
  45.8 2.4 %collective-permute-start.5 = (bf16[256,2048]{1,0:T(8,128)(2,1)S(1)}, bf16[256,2048]{1,0:T(8,128)(2,1)S(1)}, u32[]{:S(2)}, u32[]{:S(2)}) collective-permute-start(bf16[256,2048]{1,0:T(8,128)(2,1)S(1)} %partial.2), channel_id=1, source_target_pairs={{0,1},{1,0},{2,3},{3,2},{4,5},{5,4},{6,7},{7,6},{8,9},{9,8},{10,11... | collective-permute-start | bytes 3145736 | tf_op jit(solution)/shard_map/ppermute | solution.py:440
  48.1 2.5 %partial.3 = bf16[256,2048]{1,0:T(8,128)(2,1)S(1)} custom-call(f32[3,5]{1,0:T(4,128)S(1)} %get-tuple-element.10.flags_ref.refs_0_, f32[8,8]{1,0:T(8,128)S(1)} %copy-done.5, s32[15,1024]{1,0:T(8,128)S(1)} %copy-done.4, bf16[1024,1024]{1,0:T(8,128)(2,1)S(1)} %copy-done, f32[4,1024,256]{2,1,0:T(8,128)S(1)} %near.1.rest_0_.refs_4_, ...), custom_call_target="tpu_custom_call" | custom-call | tf_op jit(solution)/shard_map/partial/pallas_call | solution.py:425
  50.7 0.1 collective-permute-start.6
  50.7 2.3 %attend.1.attended_ref = bf16[512,1024]{1,0:T(8,128)(2,1)S(1)} custom-call(f32[3,5]{1,0:T(4,128)S(1)} %get-tuple-element.10.flags_ref.refs_0_, f32[8,8]{1,0:T(8,128)S(1)} %copy-done.5, s32[15,1024]{1,0:T(8,128)S(1)} %copy-done.4, bf16[1024,1024]{1,0:T(8,128)(2,1)S(1)} %copy-done, f32[4,1024,256]{2,1,0:T(8,128)S(1)} %near.1.rest_0_.refs_4_, ...), custom_call_target="tpu_custom_call" | custom-call | tf_op jit(solution)/shard_map/attend/pallas_call | solution.py:441
  53.0 0.0 collective-permute-done.5.refs_0_
  53.0 0.4 collective-permute-done.6.refs_1_
  53.4 4.2 %project.1 = bf16[512,2048]{1,0:T(8,128)(2,1)} custom-call(bf16[512,1024]{1,0:T(8,128)(2,1)S(1)} %attend.1.attended_ref, bf16[1024,2048]{1,0:T(8,128)(2,1)S(1)} %copy-done.1, bf16[256,2048]{1,0:T(8,128)(2,1)S(1)} %collective-permute-done.5.refs_0_, bf16[256,2048]{1,0:T(8,128)(2,1)S(1)} %collective-permute-done.6.refs_1_), custom_call_target="tpu_custom_call" | custom-call | tf_op jit(solution)/shard_map/project/pallas_call | solution.py:451
  (1 shorter events, 0.0 us)
Async XLA Ops:
  0.0 5.0 %copy-start = (bf16[1024,1024]{1,0:T(8,128)(2,1)S(1)}, bf16[1024,1024]{1,0:T(8,128)(2,1)}, u32[]{:S(2)}) copy-start(bf16[1024,1024]{1,0:T(8,128)(2,1)} %refs_3_.5) | copy-start | bytes 6291460
  0.0 5.0 %copy-start.5 = (f32[8,8]{1,0:T(8,128)S(1)}, f32[8,8]{1,0:T(8,128)}, u32[]{:S(2)}) copy-start(f32[8,8]{1,0:T(8,128)} %refs_1_.5) | copy-start | bytes 772
  0.0 5.0 %copy-start.4 = (s32[15,1024]{1,0:T(8,128)S(1)}, s32[15,1024]{1,0:T(8,128)}, u32[]{:S(2)}) copy-start(s32[15,1024]{1,0:T(8,128)} %refs_2_.5) | copy-start | bytes 184324
  0.0 0.8 %copy-start.8 = (s32[4]{0:T(128)S(1)}, s32[4]{0:T(128)}, u32[]{:S(2)}) copy-start(s32[4]{0:T(128)} %lengths_ref.1) | copy-start | bytes 52
  4.7 7.3 %collective-permute-start.1 = (bf16[1024,128]{1,0:T(8,128)(2,1)S(1)}, bf16[1024,128]{1,0:T(8,128)(2,1)S(1)}, u32[]{:S(2)}, u32[]{:S(2)}) collective-permute-start(bf16[1024,128]{1,0:T(8,128)(2,1)S(1)} %get-tuple-element.14.own_ref), channel_id=1, source_target_pairs={{0,2},{2,0},{4,6},{6,4},{8,10},{10,8},{12,14},{14,12},{16,18},{18,... | collective-permute-start | bytes 786440 | tf_op jit(solution)/shard_map/ppermute | solution.py:346
  11.9 1.0 %copy-start.2 = (bf16[1024,256]{1,0:T(8,128)(2,1)S(1)}, bf16[1024,256]{1,0:T(8,128)(2,1)}, u32[]{:S(2)}) copy-start(bf16[1024,256]{1,0:T(8,128)(2,1)} %k_ref.3) | copy-start | bytes 1572868
  11.9 1.2 %copy-start.3 = (bf16[1024,256]{1,0:T(8,128)(2,1)S(1)}, bf16[1024,256]{1,0:T(8,128)(2,1)}, u32[]{:S(2)}) copy-start(bf16[1024,256]{1,0:T(8,128)(2,1)} %v_ref.3) | copy-start | bytes 1572868
  11.9 1.2 %copy-start.7 = (f32[1024]{0:T(1024)S(1)}, f32[1024]{0:T(1024)}, u32[]{:S(2)}) copy-start(f32[1024]{0:T(1024)} %param.20) | copy-start | bytes 12292
  12.6 6.4 %collective-permute-start.2 = (bf16[1024,128]{1,0:T(8,128)(2,1)S(1)}, bf16[1024,128]{1,0:T(8,128)(2,1)S(1)}, u32[]{:S(2)}, u32[]{:S(2)}) collective-permute-start(bf16[1024,128]{1,0:T(8,128)(2,1)S(1)} %join.3.own_ref), channel_id=1, source_target_pairs={{0,4},{2,6},{4,0},{6,2},{8,12},{10,14},{12,8},{14,10},{16,20},{18,... | collective-permute-start | bytes 786440 | tf_op jit(solution)/shard_map/ppermute | solution.py:346
  18.0 3.0 %slice-start = ((bf16[1024,256]{1,0:T(8,128)(2,1)}), bf16[256,256]{1,0:T(8,128)(2,1)S(1)}, s32[]{:S(2)}) async-start(bf16[1024,256]{1,0:T(8,128)(2,1)} %k_ref.3), calls=%async_computation | async-start | bytes 262144 | tf_op jit(solution)/shard_map/slice | solution.py:343
  18.1 3.0 %slice-start.1 = ((bf16[1024,256]{1,0:T(8,128)(2,1)}), bf16[256,256]{1,0:T(8,128)(2,1)S(1)}, s32[]{:S(2)}) async-start(bf16[1024,256]{1,0:T(8,128)(2,1)} %v_ref.3), calls=%async_computation.1 | async-start | bytes 262144 | tf_op jit(solution)/shard_map/slice | solution.py:343
  19.7 5.3 %collective-permute-start.3 = (bf16[1024,128]{1,0:T(8,128)(2,1)S(1)}, bf16[1024,128]{1,0:T(8,128)(2,1)S(1)}, u32[]{:S(2)}, u32[]{:S(2)}) collective-permute-start(bf16[1024,128]{1,0:T(8,128)(2,1)S(1)} %join.4.own_ref), channel_id=1, source_target_pairs={{0,8},{2,10},{4,12},{6,14},{8,0},{10,2},{12,4},{14,6},{16,24},{18,... | collective-permute-start | bytes 786440 | tf_op jit(solution)/shard_map/ppermute | solution.py:346
  21.1 8.9 %collective-permute-start = (bf16[256,512]{1,0:T(8,128)(2,1)S(1)}, bf16[256,512]{1,0:T(8,128)(2,1)S(1)}, u32[]{:S(2)}, u32[]{:S(2)}) collective-permute-start(bf16[256,512]{1,0:T(8,128)(2,1)S(1)} %pad_maximum_fusion), channel_id=1, source_target_pairs={{0,2},{2,4},{4,6},{6,8},{8,10},{10,12},{12,14},{14,16},{16,18},{18... | collective-permute-start | bytes 786440 | tf_op jit(solution)/shard_map/ppermute | solution.py:412
  25.6 17.6 %copy-start.1 = (bf16[1024,2048]{1,0:T(8,128)(2,1)S(1)}, bf16[1024,2048]{1,0:T(8,128)(2,1)}, u32[]{:S(2)}) copy-start(bf16[1024,2048]{1,0:T(8,128)(2,1)} %w_ref.1) | copy-start | bytes 12582916
  25.6 17.6 %copy-start.6 = (f32[1024]{0:T(1024)S(1)}, f32[1024]{0:T(1024)}, u32[]{:S(2)}) copy-start(f32[1024]{0:T(1024)} %param.19) | copy-start | bytes 12292
  25.7 17.6 %collective-permute-start.4 = (bf16[1024,128]{1,0:T(8,128)(2,1)S(1)}, bf16[1024,128]{1,0:T(8,128)(2,1)S(1)}, u32[]{:S(2)}, u32[]{:S(2)}) collective-permute-start(bf16[1024,128]{1,0:T(8,128)(2,1)S(1)} %join.5), channel_id=1, source_target_pairs={{0,16},{2,18},{4,20},{6,22},{8,24},{10,26},{12,28},{14,30},{16,0},... | collective-permute-start | bytes 786440 | tf_op jit(solution)/shard_map/ppermute | solution.py:346
  45.8 7.3 %collective-permute-start.5 = (bf16[256,2048]{1,0:T(8,128)(2,1)S(1)}, bf16[256,2048]{1,0:T(8,128)(2,1)S(1)}, u32[]{:S(2)}, u32[]{:S(2)}) collective-permute-start(bf16[256,2048]{1,0:T(8,128)(2,1)S(1)} %partial.2), channel_id=1, source_target_pairs={{0,1},{1,0},{2,3},{3,2},{4,5},{5,4},{6,7},{7,6},{8,9},{9,8},{10,11... | collective-permute-start | bytes 3145736 | tf_op jit(solution)/shard_map/ppermute | solution.py:440
  50.7 2.7 %collective-permute-start.6 = (bf16[256,2048]{1,0:T(8,128)(2,1)S(1)}, bf16[256,2048]{1,0:T(8,128)(2,1)S(1)}, u32[]{:S(2)}, u32[]{:S(2)}) collective-permute-start(bf16[256,2048]{1,0:T(8,128)(2,1)S(1)} %partial.3), channel_id=1, source_target_pairs={{0,1},{1,0},{2,3},{3,2},{4,5},{5,4},{6,7},{7,6},{8,9},{9,8},{10,11... | collective-permute-start | bytes 3145736 | tf_op jit(solution)/shard_map/ppermute | solution.py:440

commit v3 on v2

--- a/solution.py
+++ b/solution.py
@@ -9,7 +9,6 @@
 
 DH = 128
 WINDOW = 256
-BLOCK = 512
 NEAR = 256
 TILE = 128
 GROUP = 8
@@ -55,7 +54,24 @@
 
 
 def state_kernel(
-    lengths_ref, k_hbm, v_hbm, k_ref, v_ref, local_ref, total_ref, flags_ref, states, sems, *, levels
+    lengths_hbm,
+    k_hbm,
+    v_hbm,
+    wk_hbm,
+    wv_hbm,
+    k_ref,
+    v_ref,
+    rim_ref,
+    local_ref,
+    total_ref,
+    flags_ref,
+    states,
+    lengths_ref,
+    sems,
+    rim_sems,
+    lengths_sem,
+    *,
+    levels,
 ):
     blocks = states.shape[0]
     heads = k_ref.shape[1] // DH
@@ -69,6 +85,15 @@
         for copy in pair:
             copy.start()
         copies.append(pair)
+    last_rows = pl.ds(wk_hbm.shape[0] - WINDOW, WINDOW)
+    width = wk_hbm.shape[1]
+    late = [
+        pltpu.make_async_copy(wk_hbm.at[last_rows], rim_ref.at[:, pl.ds(0, width)], rim_sems.at[0]),
+        pltpu.make_async_copy(wv_hbm.at[last_rows], rim_ref.at[:, pl.ds(width, width)], rim_sems.at[1]),
+        pltpu.make_async_copy(lengths_hbm, lengths_ref, lengths_sem),
+    ]
+    for copy in late:
+        copy.start()
     for b in range(blocks):
         rows = slice(b * NEAR, (b + 1) * NEAR)
         for copy in copies[b]:
@@ -81,6 +106,8 @@
         local_ref[place] = functools.reduce(jnp.add, members).astype(BF16)
     total_ref[...] = functools.reduce(jnp.add, [states[b] for b in range(blocks)]).astype(BF16)
 
+    for copy in late:
+        copy.wait()
     shard = lax.axis_index("seq")
     starts = [jnp.int32(0)]
     for s in range(lengths_ref.shape[0] - 1):
@@ -93,21 +120,28 @@
         return begin
 
     begin = begin_of(shard)
+    rows = []
     for level in range(levels):
         last = shard | ((2 << level) - 1)
         middle = last - (1 << level)
         joined = jnp.where(begin_of(last) <= middle, 1.0, 0.0)
         right = (shard & (1 << level)) != 0
-        flags_ref[0, level] = jnp.where(right, 1.0, joined)
-        flags_ref[1, level] = jnp.where(right, joined, 1.0)
-        flags_ref[2, level] = jnp.where(right & (begin <= middle), 1.0, 0.0)
-    for row in range(3):
-        flags_ref[row, levels] = jnp.where(begin == shard, -1e30, 0.0)
+        rows.append(jnp.where(right, 1.0, joined))
+        rows.append(jnp.where(right, joined, 1.0))
+        rows.append(jnp.where(right & (begin <= middle), 1.0, 0.0))
+    rows.append(jnp.where(begin == shard, -1e30, 0.0))
+    for i, value in enumerate(rows):
+        flags_ref[i : i + 1, :] = jnp.full((1, flags_ref.shape[1]), value, F32)
+
+
+def flag_row(flags_ref, level, kind):
+    return flags_ref[3 * level + kind : 3 * level + kind + 1, :]
 
 
 def join_kernel(flags_ref, own_ref, arrived_ref, *rest, level):
-    own, arrived = own_ref[...].astype(F32), arrived_ref[...].astype(F32)
-    rest[-1][...] = (own * flags_ref[0, level] + arrived * flags_ref[1, level]).astype(BF16)
+    columns = own_ref.shape[1]
+    own = own_ref[...] * flag_row(flags_ref, level, 0)[:, :columns].astype(BF16)
+    rest[-1][...] = own + arrived_ref[...] * flag_row(flags_ref, level, 1)[:, :columns].astype(BF16)
 
 
 def tile_mixing(weights):
@@ -136,7 +170,7 @@
 
 
 def near_kernel(table_ref, index_ref, q_ref, k_ref, v_ref, local_ref, *rest, spans, start):
-    out_ref = rest[-1]
+    out_ref, weights_ref = rest[-2:]
     block = start + pl.program_id(0)
     blocks, width, _ = out_ref.shape
     near_bits = NEAR.bit_length() - 1
@@ -152,6 +186,7 @@
     for h in range(width // DH):
         at = head_columns(h)
         weights = weight_rows(index, table_ref, h, 0)
+        weights_ref[block, h] = weights
         queries_t = q_ref[tokens, at].T
         scores = dot(k_ref[tokens, at], queries_t)
         low = scores[:TILE, :TILE] * tile_mixing(weights[:, :TILE])
@@ -174,6 +209,11 @@
     return jnp.broadcast_to(gain_ref[h], (DH, DH)).T
 
 
+def crosses_late(shard, seq_count):
+    quarter = seq_count // 4
+    return (shard % quarter == 0) & (shard != 2 * quarter)
+
+
 def window_kernel(flags_ref, q_ref, k_ref, v_ref, gain_ref, *rest, has_rim, members, start):
     out_ref, gains = rest[-2:]
     block = start + pl.program_id(0)
@@ -191,13 +231,14 @@
     lower = jnp.where(causal, 1.0, 0.0).astype(BF16)
     now = pl.multiple_of(block * NEAR, NEAR)
     if has_rim:
-        bias = flags_ref[0, flags_ref.shape[1] - 1]
+        bias = flags_ref[flags_ref.shape[0] - 1 :, :TILE]
     for g in range(heads // members):
         at = head_columns(g)
         if has_rim:
-            rim_ref = rest[0]
-            old_k = rim_ref[:, at]
-            old_v = rim_ref[:, head_columns(g + heads // members)]
+            is_late = crosses_late(lax.axis_index("seq"), lax.axis_size("seq"))
+            beside = head_columns(g + heads // members)
+            old_k = jnp.where(is_late, rest[1][:, at], rest[0][:, at])
+            old_v = jnp.where(is_late, rest[1][:, beside], rest[0][:, beside])
         else:
             old_k = k_ref[pl.ds(now - WINDOW, WINDOW), at]
             old_v = v_ref[pl.ds(now - WINDOW, WINDOW), at]
@@ -227,23 +268,35 @@
                 out_ref[block, head_columns(h), tile * TILE : (tile + 1) * TILE] = scaled.astype(BF16)
 
 
-def attend_block(block, flags_ref, table_ref, index_ref, q_ref, near_ref, win_ref, gain_ref, bucket_refs):
-    levels = len(bucket_refs)
-    width = q_ref.shape[1]
-    first = index_ref.shape[0] - levels
+def far_terms(block, first, h, flags_ref, weights_ref, q_ref, bucket_refs):
+    above = weights_ref.shape[2] - flags_ref.shape[0] // 3 + first
     tokens = pl.ds(pl.multiple_of(block * NEAR, NEAR), NEAR)
-    index = index_ref[first:, tokens]
+    at = head_columns(h)
+    queries_t = q_ref[tokens, at].T
+    lhs, rhs = [], []
+    for i, bucket_ref in enumerate(bucket_refs):
+        row = weights_ref[block, h, above + i : above + i + 1, :] * flag_row(flags_ref, first + i, 2)
+        lhs.append(bucket_ref[at, :])
+        rhs.append(queries_t * row.astype(BF16))
+    return dot(jnp.concatenate(lhs, axis=1), jnp.concatenate(rhs, axis=0))
+
+
+def far_kernel(flags_ref, weights_ref, q_ref, near_ref, *rest):
+    bucket_refs, out_ref = rest[:-1], rest[-1]
+    block = pl.program_id(0)
+    for h in range(q_ref.shape[1] // DH):
+        at = head_columns(h)
+        reached = far_terms(block, 0, h, flags_ref, weights_ref, q_ref, bucket_refs)
+        out_ref[block, at, :] = near_ref[block, at, :] + reached
+
+
+def attend_block(block, flags_ref, weights_ref, q_ref, near_ref, win_ref, gain_ref, bucket_ref):
+    last = flags_ref.shape[0] // 3 - 1
     attended = []
-    for h in range(width // DH):
+    for h in range(q_ref.shape[1] // DH):
         at = head_columns(h)
-        weights = weight_rows(index, table_ref, h, first)
-        queries_t = q_ref[tokens, at].T
-        lhs, rhs = [], []
-        for level in range(levels):
-            row = (weights[level : level + 1] * flags_ref[2, level]).astype(BF16)
-            lhs.append(bucket_refs[level][at, :])
-            rhs.append(queries_t * row)
-        total = near_ref[block, at, :] + dot(jnp.concatenate(lhs, axis=1), jnp.concatenate(rhs, axis=0))
+        reached = far_terms(block, last, h, flags_ref, weights_ref, q_ref, [bucket_ref])
+        total = near_ref[block, at, :] + reached
         mean = jnp.sum(total * total, axis=0, keepdims=True) * (1.0 / DH)
         gain = gain_column(gain_ref, h)
         gain = jnp.concatenate([gain] * (NEAR // DH), axis=1)
@@ -265,26 +318,45 @@
     return lax.rem(lax.axis_index("head") + away, head_count) * pieces
 
 
-def partial_kernel(*refs, levels, away, head_count, pieces, piece):
+def partial_kernel(*refs, away, head_count, pieces, piece):
     block = first_block(away, head_count, pieces) + piece
-    project(attend_block(block, *refs[:7], refs[7 : 7 + levels]), refs[7 + levels], [], refs[-1])
-
-
-def attend_kernel(*refs, levels, head_count, pieces):
-    block = first_block(0, head_count, pieces) + pl.program_id(0)
-    rows = pl.ds(pl.multiple_of(pl.program_id(0) * NEAR, NEAR), NEAR)
-    refs[-1][rows, :] = attend_block(block, *refs[:7], refs[7 : 7 + levels])
+    project(attend_block(block, *refs[:7]), refs[7], [], refs[-1])
+
+
+def attend_kernel(*refs, head_count, pieces, piece):
+    block = first_block(0, head_count, pieces) + piece
+    refs[-1][...] = attend_block(block, *refs[:7])
 
 
 def project_kernel(attended_ref, w_ref, *refs):
-    added, out_ref = refs[:-1], refs[-1]
-    pieces = len(added) * NEAR // out_ref.shape[0]
-    for piece in range(out_ref.shape[0] // NEAR):
-        rows = slice(piece * NEAR, (piece + 1) * NEAR)
-        product = dot(attended_ref[rows, :], w_ref[...])
-        for part in added[piece::out_ref.shape[0] // NEAR]:
-            product = product + part[...].astype(F32)
-        out_ref[rows, :] = product.astype(BF16)
+    project(attended_ref[...], w_ref, refs[:-1], refs[-1])
+
+
+def last_kernel(*refs, head_count, pieces, others):
+    w_ref = refs[7]
+    added = refs[8 : 8 + others]
+    done = refs[8 + others : 8 + others + pieces - 1]
+    out_ref, result, sems = refs[8 + others + pieces - 1 :]
+    copies = []
+    for piece, source in enumerate(done):
+        rows = pl.ds(piece * NEAR, NEAR)
+        copies.append(pltpu.make_async_copy(source, out_ref.at[rows], sems.at[piece]))
+        copies[-1].start()
+    attended = attend_block(first_block(0, head_count, pieces) + pieces - 1, *refs[:7])
+    step = w_ref.shape[1] // (sems.shape[0] - pieces + 1)
+    rows = pl.ds((pieces - 1) * NEAR, NEAR)
+    for i, c in enumerate(range(0, w_ref.shape[1], step)):
+        columns = slice(c, c + step)
+        product = dot(attended, w_ref[:, columns])
+        for part in added:
+            product = product + part[:, columns].astype(F32)
+        result[:, columns] = product.astype(BF16)
+        at = pl.ds(c, step)
+        copy = pltpu.make_async_copy(result.at[:, at], out_ref.at[rows, at], sems.at[pieces - 1 + i])
+        copy.start()
+        copies.append(copy)
+    for copy in copies:
+        copy.wait()
 
 
 def in_hbm(array):
@@ -297,7 +369,7 @@
 
 
 def make_shards(seq_count, head_count):
-    def shards(
+    def layer(
         queries,
         lin_keys,
         lin_values,
@@ -321,34 +393,40 @@
         def params(megabytes):
             return pltpu.CompilerParams(vmem_limit_bytes=megabytes * MEGABYTE)
 
-        keys, values, local_states, state, flags = pl.pallas_call(
+        states_call = pl.pallas_call(
             functools.partial(state_kernel, levels=levels),
-            in_specs=[SMEM, HELD, HELD],
-            out_specs=[VMEM, VMEM, VMEM, VMEM, SMEM],
+            in_specs=[HELD] * 5,
+            out_specs=[VMEM] * 6,
             out_shape=[
                 jax.ShapeDtypeStruct(lin_keys.shape, BF16),
                 jax.ShapeDtypeStruct(lin_values.shape, BF16),
+                jax.ShapeDtypeStruct((WINDOW, 2 * window_keys.shape[1]), BF16),
                 jax.ShapeDtypeStruct((buckets, width_in, DH), BF16),
                 jax.ShapeDtypeStruct((width_in, DH), BF16),
-                jax.ShapeDtypeStruct((3, levels + 1), F32),
+                jax.ShapeDtypeStruct((3 * levels + 1, NEAR), F32),
             ],
             scratch_shapes=[
                 pltpu.VMEM((blocks, width_in, DH), F32),
+                pltpu.SMEM(seq_lengths.shape, jnp.int32),
                 pltpu.SemaphoreType.DMA((2, blocks)),
+                pltpu.SemaphoreType.DMA((2,)),
+                pltpu.SemaphoreType.DMA,
             ],
             compiler_params=params(16),
             name="states",
-        )(seq_lengths, in_hbm(lin_keys), in_hbm(lin_values))
-
-        rim = jnp.concatenate([window_keys[tokens - WINDOW :], window_values[tokens - WINDOW :]], axis=1)
+        )
+        keys, values, rim, local_states, state, flags = states_call(
+            *[in_hbm(a) for a in (seq_lengths, lin_keys, lin_values, window_keys, window_values)]
+        )
 
         def exchanged(level, state):
-            return lax.ppermute(state, "seq", [(i, i ^ (1 << level)) for i in range(seq_count)])
+            route = [(i, i ^ (1 << level)) for i in range(seq_count)]
+            return lax.ppermute(state, "seq", route)
 
         def joined(level, state, arrived, cover):
             return pl.pallas_call(
                 functools.partial(join_kernel, level=level),
-                in_specs=[SMEM, VMEM, VMEM] + [HELD] * len(cover),
+                in_specs=[VMEM, VMEM, VMEM] + [HELD] * len(cover),
                 out_specs=VMEM,
                 out_shape=jax.ShapeDtypeStruct(state.shape, BF16),
                 compiler_params=params(4),
@@ -367,8 +445,11 @@
                 functools.partial(near_kernel, spans=local_spans(tokens), start=start),
                 grid=(count,),
                 in_specs=specs,
-                out_specs=VMEM,
-                out_shape=jax.ShapeDtypeStruct((blocks, width_in, NEAR), F32),
+                out_specs=[VMEM, VMEM],
+                out_shape=[
+                    jax.ShapeDtypeStruct((blocks, width_in, NEAR), F32),
+                    jax.ShapeDtypeStruct((blocks, heads, level_index.shape[0], NEAR), F32),
+                ],
                 input_output_aliases=aliases,
                 compiler_params=params(8),
                 name="near",
@@ -378,11 +459,11 @@
 
         def windowed(start, count, rim, base):
             operands = [flags, queries, window_keys, window_values, window_gains]
-            specs = [SMEM] + [VMEM] * 4
+            specs = [VMEM] * 5
             aliases = {}
             if rim is not None:
-                operands.append(rim)
-                specs.append(VMEM)
+                operands += rim
+                specs += [VMEM] * len(rim)
             if base is not None:
                 aliases = {len(operands): 0}
                 operands.append(base)
@@ -400,36 +481,45 @@
             )(*operands)
 
         received = [exchanged(0, state)]
-        near = neared(0, blocks, None)
+        near, weights = neared(0, blocks, None)
         state = joined(0, state, received[0], [near])
         received.append(exchanged(1, state))
         windows = windowed(1, blocks - 1, None, None)
         cover = [windows]
+        steps = [(i, i + 1) for i in range(seq_count - 1)]
+        late = [(i, j) for i, j in steps if crosses_late(j, seq_count)]
         for level in range(1, levels - 1):
+            if level == levels - 2:
+                early_rim = lax.ppermute(rim, "seq", [step for step in steps if step not in late])
             state = joined(level, state, received[level], cover)
             received.append(exchanged(level + 1, state))
             cover = []
-        rim = lax.ppermute(rim, "seq", [(i, (i + 1) % seq_count) for i in range(seq_count)])
-        windows = windowed(0, 1, rim, windows)
+        late_rim = lax.ppermute(rim, "seq", late)
+        windows = windowed(0, 1, (early_rim, late_rim), windows)
+        near = pl.pallas_call(
+            far_kernel,
+            grid=(blocks,),
+            in_specs=[VMEM] * (3 + levels),
+            out_specs=VMEM,
+            out_shape=jax.ShapeDtypeStruct(near.shape, F32),
+            input_output_aliases={3: 0},
+            compiler_params=params(8),
+            name="far",
+        )(flags, weights, queries, near, *received[:-1])
 
         pieces = tokens // head_count // NEAR
         width = w_out.shape[1]
-        shared = [flags, level_table, level_index, queries, near, windows]
-        shared += [gain_linear.reshape(heads, 1, DH)] + received
-        specs = [SMEM, SMEM] + [VMEM] * (5 + levels)
-
-        arrived = []
+        shared = [flags, weights, queries, near, windows]
+        shared += [gain_linear.reshape(heads, 1, DH), received[-1]]
+        specs = [VMEM] * 7
+
+        arrived = [[] for _ in range(pieces)]
         for away in range(1, head_count):
             route = [(i, (i + away) % head_count) for i in range(head_count)]
             for piece in range(pieces):
                 partial = pl.pallas_call(
                     functools.partial(
-                        partial_kernel,
-                        levels=levels,
-                        away=away,
-                        head_count=head_count,
-                        pieces=pieces,
-                        piece=piece,
+                        partial_kernel, away=away, head_count=head_count, pieces=pieces, piece=piece
                     ),
                     in_specs=specs + [VMEM],
                     out_specs=VMEM,
@@ -437,30 +527,43 @@
                     compiler_params=params(8),
                     name="partial",
                 )(*shared, w_out)
-                arrived.append(lax.ppermute(partial, "head", route))
-        attended = pl.pallas_call(
-            functools.partial(attend_kernel, levels=levels, head_count=head_count, pieces=pieces),
-            grid=(pieces,),
-            in_specs=specs,
-            out_specs=VMEM,
-            out_shape=jax.ShapeDtypeStruct((pieces * NEAR, width_in), BF16),
+                arrived[piece].append(lax.ppermute(partial, "head", route))
+        finished = []
+        for piece in range(pieces - 1):
+            attended = pl.pallas_call(
+                functools.partial(attend_kernel, head_count=head_count, pieces=pieces, piece=piece),
+                in_specs=specs,
+                out_specs=VMEM,
+                out_shape=jax.ShapeDtypeStruct((NEAR, width_in), BF16),
+                compiler_params=params(8),
+                name="attend",
+            )(*shared)
+            finished.append(
+                pl.pallas_call(
+                    project_kernel,
+                    in_specs=[VMEM] * (2 + len(arrived[piece])),
+                    out_specs=VMEM,
+                    out_shape=jax.ShapeDtypeStruct((NEAR, width), BF16),
+                    compiler_params=params(8),
+                    name="project",
+                )(attended, w_out, *arrived[piece])
+            )
+        others = len(arrived[-1])
+        parts = 4
+        return pl.pallas_call(
+            functools.partial(last_kernel, head_count=head_count, pieces=pieces, others=others),
+            in_specs=specs + [VMEM] * (others + pieces),
+            out_specs=HELD,
+            out_shape=jax.ShapeDtypeStruct((pieces * NEAR, width), BF16),
+            scratch_shapes=[
+                pltpu.VMEM((NEAR, width), BF16),
+                pltpu.SemaphoreType.DMA((pieces - 1 + parts,)),
+            ],
             compiler_params=params(8),
-            name="attend",
-        )(*shared)
-        step = 512
-        return pl.pallas_call(
-            project_kernel,
-            grid=(width // step,),
-            in_specs=[pl.BlockSpec((pieces * NEAR, width_in), lambda c: (0, 0))]
-            + [pl.BlockSpec((width_in, step), lambda c: (0, c))]
-            + [pl.BlockSpec((NEAR, step), lambda c: (0, c))] * len(arrived),
-            out_specs=pl.BlockSpec((pieces * NEAR, step), lambda c: (0, c)),
-            out_shape=jax.ShapeDtypeStruct((pieces * NEAR, width), BF16),
-            compiler_params=params(12),
-            name="project",
-        )(attended, w_out, *arrived)
-
-    return shards
+            name="last",
+        )(*shared, w_out, *arrived[-1], *finished)
+
+    return layer
 
 
 def solution(mesh):

time: 57.7 us -> 52.5 us (0.910)
  the two profiles are of different devices: /device:TPU:7 before, /device:TPU:17 now
where the time goes in v3:
time: 52.5 us; the launch traced here: 52.3 us
  Pallas kernels  23.6 us (45%)
  starting transfers between devices  18 us (34%)
  waiting for transfers between devices  10.4 us (20%)
    ppermute x2, starting transfers between devices, layer(): arrived[piece].append(lax.ppermute(partial, 'head', route))  9.15 us
    pallas_call x2, Pallas kernels, windowed(): pl.pallas_call(functools.partial(window_kernel, has_rim=rim is not None,...  5.63 us
    ppermute x4, waiting for transfers between devices, exchanged(): return lax.ppermute(state, 'seq', route)  5.33 us
    ppermute x4, starting transfers between devices, exchanged(): return lax.ppermute(state, 'seq', route)  4.85 us
    ppermute x1, waiting for transfers between devices, layer(): lax.ppermute(rim, 'seq', [step for step in steps if step not in late])  4.6 us
    pallas_call x1, Pallas kernels, neared(): pl.pallas_call(functools.partial(near_kernel, spans=local_spans(tokens),...  4.43 us
    pallas_call x2, Pallas kernels, layer(): pl.pallas_call(functools.partial(partial_kernel, away=away, head_count=he...  3.58 us
    ppermute x1, starting transfers between devices, layer(): lax.ppermute(rim, 'seq', [step for step in steps if step not in late])  3.29 us
  transfers between devices with their start and end apart: 8, of which 5 were waited for; matrix products, arithmetic and copies ran while one was open for 0% of the time, Pallas kernels for 31%

profile of v3, /device:TPU:17, one launch (start us, length us, event | category | flops | bytes accessed | tf_op | source)
XLA Modules:
  0.0 52.3 jit_solution(9277785276620158586)
XLA Ops:
  0.0 0.0 copy-start
  0.0 0.0 copy-start.7
  0.0 0.0 copy-start.4
  0.0 3.0 %states.1 = (bf16[1024,1024]{1,0:T(8,128)(2,1)S(1)}, bf16[1024,1024]{1,0:T(8,128)(2,1)S(1)}, bf16[256,512]{1,0:T(8,128)(2,1)S(1)}, bf16[3,1024,128]{2,1,0:T(8,12...) custom-call(s32[4]{0:T(128)} %lengths_hbm.1, bf16[1024,1024]{1,0:T(8,128)(2,1)} %k_hbm.1, ...), custom_call_target="tpu_custom_call" | custom-call | tf_op jit(solution)/shard_map/states/pallas_call | solution.py:418
  3.0 1.3 %collective-permute-start = (bf16[1024,128]{1,0:T(8,128)(2,1)S(1)}, bf16[1024,128]{1,0:T(8,128)(2,1)S(1)}, u32[]{:S(2)}, u32[]{:S(2)}) collective-permute-start(bf16[1024,128]{1,0:T(8,128)(2,1)S(1)} %get-tuple-element.19.own_ref), channel_id=1, source_target_pairs={{0,2},{2,0},{4,6},{6,4},{8,10},{10,8},{12,14},{14,12},{16,18},{18,... | collective-permute-start | bytes 786440 | tf_op jit(solution)/shard_map/ppermute | solution.py:424
  4.3 0.0 copy-done
  4.3 0.0 copy-done.7
  4.3 0.0 copy-done.4
  4.3 4.4 %near.1 = (f32[4,1024,256]{2,1,0:T(8,128)S(1)}, f32[4,8,15,256]{3,2,1,0:T(8,128)S(1)}) custom-call(f32[8,8]{1,0:T(8,128)S(1)} %copy-done.7, s32[15,1024]{1,0:T(8,128)S(1)} %copy-done.4, bf16[1024,1024]{1,0:T(8,128)(2,1)S(1)} %copy-done, bf16[1024,1024]{1,0:T(8,128)(2,1)S(1)} %get-tuple-element.14.k_ref, bf16[1024,1024]{1,0:T(8,128)(2,1)S(1)} %get-tuple-element.15.v_ref, ...), custom_call_target="tpu_custom_call" | custom-call | tf_op jit(solution)/shard_map/near/pallas_call | solution.py:444
  8.7 1.5 %collective-permute-done.arrived_ref.rest_0_ = bf16[1024,128]{1,0:T(8,128)(2,1)S(1)} collective-permute-done((bf16[1024,128]{1,0:T(8,128)(2,1)S(1)}, bf16[1024,128]{1,0:T(8,128)(2,1)S(1)}, u32[]{:S(2)}, u32[]{:S(2)}) %collective-permute-start) | collective-permute-done | bytes 262176 | tf_op jit(solution)/shard_map/ppermute | solution.py:424
  10.3 0.0 copy-start.2
  10.3 0.0 copy-start.3
  10.3 0.0 copy-start.6
  10.3 0.1 join.3.own_ref
  10.3 1.3 %collective-permute-start.1 = (bf16[1024,128]{1,0:T(8,128)(2,1)S(1)}, bf16[1024,128]{1,0:T(8,128)(2,1)S(1)}, u32[]{:S(2)}, u32[]{:S(2)}) collective-permute-start(bf16[1024,128]{1,0:T(8,128)(2,1)S(1)} %join.3.own_ref), channel_id=1, source_target_pairs={{0,4},{2,6},{4,0},{6,2},{8,12},{10,14},{12,8},{14,10},{16,20},{18,... | collective-permute-start | bytes 786440 | tf_op jit(solution)/shard_map/ppermute | solution.py:424
  11.6 0.0 copy-done.2
  11.6 0.0 copy-done.3
  11.6 0.0 copy-done.6
  11.6 4.3 %window.2.rest_0_.rest_2_ = bf16[4,1024,256]{2,1,0:T(8,128)(2,1)S(1)} custom-call(f32[13,256]{1,0:T(8,128)S(1)} %get-tuple-element.13.flags_ref.refs_0_, bf16[1024,1024]{1,0:T(8,128)(2,1)S(1)} %copy-done, bf16[1024,256]{1,0:T(8,128)(2,1)S(1)} %copy-done.2, bf16[1024,256]{1,0:T(8,128)(2,1)S(1)} %copy-done.3, f32[8,1,128]{2,1,0:T(1,128)S(1)} %bitcast.6), custom_call_target="tpu_custom_call" | custom-call | tf_op jit(solution)/shard_map/window/pallas_call | solution.py:471
  15.9 0.8 %collective-permute-done.1.arrived_ref.rest_1_ = bf16[1024,128]{1,0:T(8,128)(2,1)S(1)} collective-permute-done((bf16[1024,128]{1,0:T(8,128)(2,1)S(1)}, bf16[1024,128]{1,0:T(8,128)(2,1)S(1)}, u32[]{:S(2)}, u32[]{:S(2)}) %collective-permute-start.1) | collective-permute-done | bytes 262176 | tf_op jit(solution)/shard_map/ppermute | solution.py:424
  16.7 0.1 join.4.own_ref
  16.8 1.4 %collective-permute-start.2 = (bf16[1024,128]{1,0:T(8,128)(2,1)S(1)}, bf16[1024,128]{1,0:T(8,128)(2,1)S(1)}, u32[]{:S(2)}, u32[]{:S(2)}) collective-permute-start(bf16[1024,128]{1,0:T(8,128)(2,1)S(1)} %join.4.own_ref), channel_id=1, source_target_pairs={{0,8},{2,10},{4,12},{6,14},{8,0},{10,2},{12,4},{14,6},{16,24},{18,... | collective-permute-start | bytes 786440 | tf_op jit(solution)/shard_map/ppermute | solution.py:424
  18.2 0.7 %collective-permute-start.4 = (bf16[256,512]{1,0:T(8,128)(2,1)S(1)}, bf16[256,512]{1,0:T(8,128)(2,1)S(1)}, u32[]{:S(2)}, u32[]{:S(2)}) collective-permute-start(bf16[256,512]{1,0:T(8,128)(2,1)S(1)} %get-tuple-element.20), channel_id=1, source_target_pairs={{6,8},{22,24},{7,9},{23,25}} | collective-permute-start | bytes 786440 | tf_op jit(solution)/shard_map/ppermute | solution.py:497
  18.8 3.3 %collective-permute-start.3 = (bf16[256,512]{1,0:T(8,128)(2,1)S(1)}, bf16[256,512]{1,0:T(8,128)(2,1)S(1)}, u32[]{:S(2)}, u32[]{:S(2)}) collective-permute-start(bf16[256,512]{1,0:T(8,128)(2,1)S(1)} %get-tuple-element.20), channel_id=1, source_target_pairs={{0,2},{2,4},{4,6},{8,10},{10,12},{12,14},{14,16},{16,18},{18,20},{... | collective-permute-start | bytes 786440 | tf_op jit(solution)/shard_map/ppermute | solution.py:493
  22.1 0.0 collective-permute-done.2.rest_2_.arrived_ref
  22.1 0.1 join.5
  22.2 0.9 %collective-permute-start.5 = (bf16[1024,128]{1,0:T(8,128)(2,1)S(1)}, bf16[1024,128]{1,0:T(8,128)(2,1)S(1)}, u32[]{:S(2)}, u32[]{:S(2)}) collective-permute-start(bf16[1024,128]{1,0:T(8,128)(2,1)S(1)} %join.5), channel_id=1, source_target_pairs={{0,16},{2,18},{4,20},{6,22},{8,24},{10,26},{12,28},{14,30},{16,0},... | collective-permute-start | bytes 786440 | tf_op jit(solution)/shard_map/ppermute | solution.py:424
  23.1 0.0 collective-permute-done.4.rest_1_
  23.2 4.6 %collective-permute-done.3.rest_0_ = bf16[256,512]{1,0:T(8,128)(2,1)S(1)} collective-permute-done((bf16[256,512]{1,0:T(8,128)(2,1)S(1)}, bf16[256,512]{1,0:T(8,128)(2,1)S(1)}, u32[]{:S(2)}, u32[]{:S(2)}) %collective-permute-start.3) | collective-permute-done | bytes 262176 | tf_op jit(solution)/shard_map/ppermute | solution.py:493
  27.8 1.4 %window.3.refs_4_ = bf16[4,1024,256]{2,1,0:T(8,128)(2,1)S(1)} custom-call(f32[13,256]{1,0:T(8,128)S(1)} %get-tuple-element.13.flags_ref.refs_0_, bf16[1024,1024]{1,0:T(8,128)(2,1)S(1)} %copy-done, bf16[1024,256]{1,0:T(8,128)(2,1)S(1)} %copy-done.2, bf16[1024,256]{1,0:T(8,128)(2,1)S(1)} %copy-done.3, ...), custom_call_target="tpu_custom_call", output_to_operand_aliasing={{}: (7, {})} | custom-call | tf_op jit(solution)/shard_map/window/pallas_call | solution.py:471
  29.1 0.0 copy-start.1
  29.1 0.0 copy-start.5
  29.1 2.1 %far.1.refs_3_ = f32[4,1024,256]{2,1,0:T(8,128)S(1)} custom-call(f32[13,256]{1,0:T(8,128)S(1)} %get-tuple-element.13.flags_ref.refs_0_, f32[4,8,15,256]{3,2,1,0:T(8,128)S(1)} %get-tuple-element.17.weights_ref.refs_1_, bf16[1024,1024]{1,0:T(8,128)(2,1)S(1)} %copy-done, ...), custom_call_target="tpu_custom_call", output_to_operand_aliasing={{}: (3, {})} | custom-call | tf_op jit(solution)/shard_map/far/pallas_call | solution.py:499
  31.3 3.0 %collective-permute-done.5.refs_6_ = bf16[1024,128]{1,0:T(8,128)(2,1)S(1)} collective-permute-done((bf16[1024,128]{1,0:T(8,128)(2,1)S(1)}, bf16[1024,128]{1,0:T(8,128)(2,1)S(1)}, u32[]{:S(2)}, u32[]{:S(2)}) %collective-permute-start.5) | collective-permute-done | bytes 262176 | tf_op jit(solution)/shard_map/ppermute | solution.py:424
  34.2 0.0 copy-done.1
  34.2 0.0 copy-done.5
  34.2 1.8 %partial.3 = bf16[256,2048]{1,0:T(8,128)(2,1)S(1)} custom-call(f32[13,256]{1,0:T(8,128)S(1)} %get-tuple-element.13.flags_ref.refs_0_, f32[4,8,15,256]{3,2,1,0:T(8,128)S(1)} %get-tuple-element.17.weights_ref.refs_1_, bf16[1024,1024]{1,0:T(8,128)(2,1)S(1)} %copy-done, f32[4,1024,256]{2,1,0:T(8,128)S(1)} %far.1.refs_3_, ...), custom_call_target="tpu_custom_call" | custom-call | tf_op jit(solution)/shard_map/partial/pallas_call | solution.py:520
  36.0 9.1 %collective-permute-start.7 = (bf16[256,2048]{1,0:T(8,128)(2,1)S(1)}, bf16[256,2048]{1,0:T(8,128)(2,1)S(1)}, u32[]{:S(2)}, u32[]{:S(2)}) collective-permute-start(bf16[256,2048]{1,0:T(8,128)(2,1)S(1)} %partial.3), channel_id=1, source_target_pairs={{0,1},{1,0},{2,3},{3,2},{4,5},{5,4},{6,7},{7,6},{8,9},{9,8},{10,11... | collective-permute-start | bytes 3145736 | tf_op jit(solution)/shard_map/ppermute | solution.py:530
  45.1 1.8 %partial.2 = bf16[256,2048]{1,0:T(8,128)(2,1)S(1)} custom-call(f32[13,256]{1,0:T(8,128)S(1)} %get-tuple-element.13.flags_ref.refs_0_, f32[4,8,15,256]{3,2,1,0:T(8,128)S(1)} %get-tuple-element.17.weights_ref.refs_1_, bf16[1024,1024]{1,0:T(8,128)(2,1)S(1)} %copy-done, f32[4,1024,256]{2,1,0:T(8,128)S(1)} %far.1.refs_3_, ...), custom_call_target="tpu_custom_call" | custom-call | tf_op jit(solution)/shard_map/partial/pallas_call | solution.py:520
  46.9 0.1 collective-permute-start.6
  47.0 0.8 %attend.1.attended_ref = bf16[256,1024]{1,0:T(8,128)(2,1)S(1)} custom-call(f32[13,256]{1,0:T(8,128)S(1)} %get-tuple-element.13.flags_ref.refs_0_, f32[4,8,15,256]{3,2,1,0:T(8,128)S(1)} %get-tuple-element.17.weights_ref.refs_1_, bf16[1024,1024]{1,0:T(8,128)(2,1)S(1)} %copy-done, f32[4,1024,256]{2,1,0:T(8,128)S(1)} %far.1.refs_3_, ...), custom_call_target="tpu_custom_call" | custom-call | tf_op jit(solution)/shard_map/attend/pallas_call | solution.py:533
  47.8 0.0 collective-permute-done.7.refs_0_
  47.8 1.3 %project.1.refs_9_ = bf16[256,2048]{1,0:T(8,128)(2,1)S(1)} custom-call(bf16[256,1024]{1,0:T(8,128)(2,1)S(1)} %attend.1.attended_ref, bf16[1024,2048]{1,0:T(8,128)(2,1)S(1)} %copy-done.1, bf16[256,2048]{1,0:T(8,128)(2,1)S(1)} %collective-permute-done.7.refs_0_), custom_call_target="tpu_custom_call" | custom-call | tf_op jit(solution)/shard_map/project/pallas_call | solution.py:542
  49.1 0.5 collective-permute-done.6.refs_8_
  49.6 2.5 %last.1 = bf16[512,2048]{1,0:T(8,128)(2,1)} custom-call(f32[13,256]{1,0:T(8,128)S(1)} %get-tuple-element.13.flags_ref.refs_0_, f32[4,8,15,256]{3,2,1,0:T(8,128)S(1)} %get-tuple-element.17.weights_ref.refs_1_, bf16[1024,1024]{1,0:T(8,128)(2,1)S(1)} %copy-done, f32[4,1024,256]{2,1,0:T(8,128)S(1)} %far.1.refs_3_, bf16[4,1024,256]{2,1,0:T(8,128)(2,1)S(1)} %window.3.refs_4_, ...), custom_call_target="tpu_custom_call" | custom-call | tf_op jit(solution)/shard_map/last/pallas_call | solution.py:553
Async XLA Ops:
  0.0 4.3 %copy-start = (bf16[1024,1024]{1,0:T(8,128)(2,1)S(1)}, bf16[1024,1024]{1,0:T(8,128)(2,1)}, u32[]{:S(2)}) copy-start(bf16[1024,1024]{1,0:T(8,128)(2,1)} %refs_2_.7) | copy-start | bytes 6291460
  0.0 4.3 %copy-start.7 = (f32[8,8]{1,0:T(8,128)S(1)}, f32[8,8]{1,0:T(8,128)}, u32[]{:S(2)}) copy-start(f32[8,8]{1,0:T(8,128)} %table_ref.1) | copy-start | bytes 772
  0.0 4.3 %copy-start.4 = (s32[15,1024]{1,0:T(8,128)S(1)}, s32[15,1024]{1,0:T(8,128)}, u32[]{:S(2)}) copy-start(s32[15,1024]{1,0:T(8,128)} %index_ref.1) | copy-start | bytes 184324
  3.0 7.3 %collective-permute-start = (bf16[1024,128]{1,0:T(8,128)(2,1)S(1)}, bf16[1024,128]{1,0:T(8,128)(2,1)S(1)}, u32[]{:S(2)}, u32[]{:S(2)}) collective-permute-start(bf16[1024,128]{1,0:T(8,128)(2,1)S(1)} %get-tuple-element.19.own_ref), channel_id=1, source_target_pairs={{0,2},{2,0},{4,6},{6,4},{8,10},{10,8},{12,14},{14,12},{16,18},{18,... | collective-permute-start | bytes 786440 | tf_op jit(solution)/shard_map/ppermute | solution.py:424
  10.3 1.4 %copy-start.2 = (bf16[1024,256]{1,0:T(8,128)(2,1)S(1)}, bf16[1024,256]{1,0:T(8,128)(2,1)}, u32[]{:S(2)}) copy-start(bf16[1024,256]{1,0:T(8,128)(2,1)} %k_ref.3) | copy-start | bytes 1572868
  10.3 1.4 %copy-start.3 = (bf16[1024,256]{1,0:T(8,128)(2,1)S(1)}, bf16[1024,256]{1,0:T(8,128)(2,1)}, u32[]{:S(2)}) copy-start(bf16[1024,256]{1,0:T(8,128)(2,1)} %v_ref.3) | copy-start | bytes 1572868
  10.3 1.4 %copy-start.6 = (f32[1024]{0:T(1024)S(1)}, f32[1024]{0:T(1024)}, u32[]{:S(2)}) copy-start(f32[1024]{0:T(1024)} %param.20) | copy-start | bytes 12292
  10.3 6.4 %collective-permute-start.1 = (bf16[1024,128]{1,0:T(8,128)(2,1)S(1)}, bf16[1024,128]{1,0:T(8,128)(2,1)S(1)}, u32[]{:S(2)}, u32[]{:S(2)}) collective-permute-start(bf16[1024,128]{1,0:T(8,128)(2,1)S(1)} %join.3.own_ref), channel_id=1, source_target_pairs={{0,4},{2,6},{4,0},{6,2},{8,12},{10,14},{12,8},{14,10},{16,20},{18,... | collective-permute-start | bytes 786440 | tf_op jit(solution)/shard_map/ppermute | solution.py:424
  16.8 5.3 %collective-permute-start.2 = (bf16[1024,128]{1,0:T(8,128)(2,1)S(1)}, bf16[1024,128]{1,0:T(8,128)(2,1)S(1)}, u32[]{:S(2)}, u32[]{:S(2)}) collective-permute-start(bf16[1024,128]{1,0:T(8,128)(2,1)S(1)} %join.4.own_ref), channel_id=1, source_target_pairs={{0,8},{2,10},{4,12},{6,14},{8,0},{10,2},{12,4},{14,6},{16,24},{18,... | collective-permute-start | bytes 786440 | tf_op jit(solution)/shard_map/ppermute | solution.py:424
  18.2 5.0 %collective-permute-start.4 = (bf16[256,512]{1,0:T(8,128)(2,1)S(1)}, bf16[256,512]{1,0:T(8,128)(2,1)S(1)}, u32[]{:S(2)}, u32[]{:S(2)}) collective-permute-start(bf16[256,512]{1,0:T(8,128)(2,1)S(1)} %get-tuple-element.20), channel_id=1, source_target_pairs={{6,8},{22,24},{7,9},{23,25}} | collective-permute-start | bytes 786440 | tf_op jit(solution)/shard_map/ppermute | solution.py:497
  18.8 8.9 %collective-permute-start.3 = (bf16[256,512]{1,0:T(8,128)(2,1)S(1)}, bf16[256,512]{1,0:T(8,128)(2,1)S(1)}, u32[]{:S(2)}, u32[]{:S(2)}) collective-permute-start(bf16[256,512]{1,0:T(8,128)(2,1)S(1)} %get-tuple-element.20), channel_id=1, source_target_pairs={{0,2},{2,4},{4,6},{8,10},{10,12},{12,14},{14,16},{16,18},{18,20},{... | collective-permute-start | bytes 786440 | tf_op jit(solution)/shard_map/ppermute | solution.py:493
  22.2 12.0 %collective-permute-start.5 = (bf16[1024,128]{1,0:T(8,128)(2,1)S(1)}, bf16[1024,128]{1,0:T(8,128)(2,1)S(1)}, u32[]{:S(2)}, u32[]{:S(2)}) collective-permute-start(bf16[1024,128]{1,0:T(8,128)(2,1)S(1)} %join.5), channel_id=1, source_target_pairs={{0,16},{2,18},{4,20},{6,22},{8,24},{10,26},{12,28},{14,30},{16,0},... | collective-permute-start | bytes 786440 | tf_op jit(solution)/shard_map/ppermute | solution.py:424
  29.1 5.1 %copy-start.1 = (bf16[1024,2048]{1,0:T(8,128)(2,1)S(1)}, bf16[1024,2048]{1,0:T(8,128)(2,1)}, u32[]{:S(2)}) copy-start(bf16[1024,2048]{1,0:T(8,128)(2,1)} %refs_7_.5) | copy-start | bytes 12582916
  29.1 5.1 %copy-start.5 = (f32[1024]{0:T(1024)S(1)}, f32[1024]{0:T(1024)}, u32[]{:S(2)}) copy-start(f32[1024]{0:T(1024)} %param.19) | copy-start | bytes 12292
  36.0 11.8 %collective-permute-start.7 = (bf16[256,2048]{1,0:T(8,128)(2,1)S(1)}, bf16[256,2048]{1,0:T(8,128)(2,1)S(1)}, u32[]{:S(2)}, u32[]{:S(2)}) collective-permute-start(bf16[256,2048]{1,0:T(8,128)(2,1)S(1)} %partial.3), channel_id=1, source_target_pairs={{0,1},{1,0},{2,3},{3,2},{4,5},{5,4},{6,7},{7,6},{8,9},{9,8},{10,11... | collective-permute-start | bytes 3145736 | tf_op jit(solution)/shard_map/ppermute | solution.py:530
  46.9 2.7 %collective-permute-start.6 = (bf16[256,2048]{1,0:T(8,128)(2,1)S(1)}, bf16[256,2048]{1,0:T(8,128)(2,1)S(1)}, u32[]{:S(2)}, u32[]{:S(2)}) collective-permute-start(bf16[256,2048]{1,0:T(8,128)(2,1)S(1)} %partial.2), channel_id=1, source_target_pairs={{0,1},{1,0},{2,3},{3,2},{4,5},{5,4},{6,7},{7,6},{8,9},{9,8},{10,11... | collective-permute-start | bytes 3145736 | tf_op jit(solution)/shard_map/ppermute | solution.py:530

commit v4 on v3

--- a/solution.py
+++ b/solution.py
@@ -63,7 +63,8 @@
     v_ref,
     rim_ref,
     local_ref,
-    total_ref,
+    total_a_ref,
+    total_b_ref,
     flags_ref,
     states,
     lengths_ref,
@@ -104,7 +105,10 @@
     for place, (span, group) in enumerate(local_buckets(blocks * NEAR)):
         members = [states[b] for b in range((group - 1) * span, group * span)]
         local_ref[place] = functools.reduce(jnp.add, members).astype(BF16)
-    total_ref[...] = functools.reduce(jnp.add, [states[b] for b in range(blocks)]).astype(BF16)
+    middle_row = total_a_ref.shape[0]
+    for total_ref, rows in ((total_a_ref, slice(0, middle_row)), (total_b_ref, slice(middle_row, None))):
+        members = [states[b, rows, :] for b in range(blocks)]
+        total_ref[...] = functools.reduce(jnp.add, members).astype(BF16)
 
     for copy in late:
         copy.wait()
@@ -169,13 +173,18 @@
     return jnp.concatenate(pieces, axis=0)
 
 
-def near_kernel(table_ref, index_ref, q_ref, k_ref, v_ref, local_ref, *rest, spans, start):
-    out_ref, weights_ref = rest[-2:]
+def weights_kernel(table_ref, index_ref, weights_ref):
+    for h in range(weights_ref.shape[0]):
+        weights_ref[h] = weight_rows(index_ref[...], table_ref, h, 0)
+
+
+def near_kernel(weights_ref, q_ref, k_ref, v_ref, local_ref, *rest, spans, start):
+    out_ref, token_ref = rest[-2:]
+    token_ref[...] = jnp.zeros(token_ref.shape, F32)
     block = start + pl.program_id(0)
     blocks, width, _ = out_ref.shape
     near_bits = NEAR.bit_length() - 1
     tokens = pl.ds(pl.multiple_of(block * NEAR, NEAR), NEAR)
-    index = index_ref[:, tokens]
     places, present = [], []
     first = 0
     for span in spans:
@@ -185,8 +194,7 @@
         first += blocks // span // 2
     for h in range(width // DH):
         at = head_columns(h)
-        weights = weight_rows(index, table_ref, h, 0)
-        weights_ref[block, h] = weights
+        weights = weights_ref[h, :, tokens]
         queries_t = q_ref[tokens, at].T
         scores = dot(k_ref[tokens, at], queries_t)
         low = scores[:TILE, :TILE] * tile_mixing(weights[:, :TILE])
@@ -209,13 +217,14 @@
     return jnp.broadcast_to(gain_ref[h], (DH, DH)).T
 
 
-def crosses_late(shard, seq_count):
-    quarter = seq_count // 4
-    return (shard % quarter == 0) & (shard != 2 * quarter)
+def pick_kernel(own_ref, ahead_ref, out_ref, *, plane):
+    closes = lax.axis_index("seq") % plane == plane - 1
+    out_ref[...] = jnp.where(closes, ahead_ref[...], own_ref[...])
 
 
 def window_kernel(flags_ref, q_ref, k_ref, v_ref, gain_ref, *rest, has_rim, members, start):
-    out_ref, gains = rest[-2:]
+    out_ref, token_ref, gains = rest[-3:]
+    token_ref[...] = jnp.zeros(token_ref.shape, F32)
     block = start + pl.program_id(0)
     heads = q_ref.shape[1] // DH
     scale = LOG2_E * DH**-0.5
@@ -235,10 +244,8 @@
     for g in range(heads // members):
         at = head_columns(g)
         if has_rim:
-            is_late = crosses_late(lax.axis_index("seq"), lax.axis_size("seq"))
-            beside = head_columns(g + heads // members)
-            old_k = jnp.where(is_late, rest[1][:, at], rest[0][:, at])
-            old_v = jnp.where(is_late, rest[1][:, beside], rest[0][:, beside])
+            old_k = rest[0][:, at]
+            old_v = rest[0][:, head_columns(g + heads // members)]
         else:
             old_k = k_ref[pl.ds(now - WINDOW, WINDOW), at]
             old_v = v_ref[pl.ds(now - WINDOW, WINDOW), at]
@@ -269,14 +276,15 @@
 
 
 def far_terms(block, first, h, flags_ref, weights_ref, q_ref, bucket_refs):
-    above = weights_ref.shape[2] - flags_ref.shape[0] // 3 + first
+    above = weights_ref.shape[1] - flags_ref.shape[0] // 3 + first
     tokens = pl.ds(pl.multiple_of(block * NEAR, NEAR), NEAR)
-    at = head_columns(h)
-    queries_t = q_ref[tokens, at].T
+    queries_t = q_ref[tokens, head_columns(h)].T
+    half = q_ref.shape[1] // 2 // DH
     lhs, rhs = [], []
-    for i, bucket_ref in enumerate(bucket_refs):
-        row = weights_ref[block, h, above + i : above + i + 1, :] * flag_row(flags_ref, first + i, 2)
-        lhs.append(bucket_ref[at, :])
+    for i in range(len(bucket_refs) // 2):
+        level = slice(above + i, above + i + 1)
+        row = weights_ref[h, level, tokens] * flag_row(flags_ref, first + i, 2)
+        lhs.append(bucket_refs[2 * i + h // half][head_columns(h % half), :])
         rhs.append(queries_t * row.astype(BF16))
     return dot(jnp.concatenate(lhs, axis=1), jnp.concatenate(rhs, axis=0))
 
@@ -290,12 +298,12 @@
         out_ref[block, at, :] = near_ref[block, at, :] + reached
 
 
-def attend_block(block, flags_ref, weights_ref, q_ref, near_ref, win_ref, gain_ref, bucket_ref):
+def attend_block(block, flags_ref, weights_ref, q_ref, near_ref, win_ref, gain_ref, *bucket_refs):
     last = flags_ref.shape[0] // 3 - 1
     attended = []
     for h in range(q_ref.shape[1] // DH):
         at = head_columns(h)
-        reached = far_terms(block, last, h, flags_ref, weights_ref, q_ref, [bucket_ref])
+        reached = far_terms(block, last, h, flags_ref, weights_ref, q_ref, bucket_refs)
         total = near_ref[block, at, :] + reached
         mean = jnp.sum(total * total, axis=0, keepdims=True) * (1.0 / DH)
         gain = gain_column(gain_ref, h)
@@ -320,12 +328,12 @@
 
 def partial_kernel(*refs, away, head_count, pieces, piece):
     block = first_block(away, head_count, pieces) + piece
-    project(attend_block(block, *refs[:7]), refs[7], [], refs[-1])
+    project(attend_block(block, *refs[:8]), refs[8], [], refs[-1])
 
 
 def attend_kernel(*refs, head_count, pieces, piece):
     block = first_block(0, head_count, pieces) + piece
-    refs[-1][...] = attend_block(block, *refs[:7])
+    refs[-1][...] = attend_block(block, *refs[:8])
 
 
 def project_kernel(attended_ref, w_ref, *refs):
@@ -333,16 +341,16 @@
 
 
 def last_kernel(*refs, head_count, pieces, others):
-    w_ref = refs[7]
-    added = refs[8 : 8 + others]
-    done = refs[8 + others : 8 + others + pieces - 1]
-    out_ref, result, sems = refs[8 + others + pieces - 1 :]
+    w_ref = refs[8]
+    added = refs[9 : 9 + others]
+    done = refs[9 + others : 8 + others + pieces]
+    out_ref, result, sems = refs[8 + others + pieces :]
     copies = []
     for piece, source in enumerate(done):
         rows = pl.ds(piece * NEAR, NEAR)
         copies.append(pltpu.make_async_copy(source, out_ref.at[rows], sems.at[piece]))
         copies[-1].start()
-    attended = attend_block(first_block(0, head_count, pieces) + pieces - 1, *refs[:7])
+    attended = attend_block(first_block(0, head_count, pieces) + pieces - 1, *refs[:8])
     step = w_ref.shape[1] // (sems.shape[0] - pieces + 1)
     rows = pl.ds((pieces - 1) * NEAR, NEAR)
     for i, c in enumerate(range(0, w_ref.shape[1], step)):
@@ -366,6 +374,16 @@
 SMEM = pl.BlockSpec(memory_space=pltpu.SMEM)
 VMEM = pl.BlockSpec(memory_space=pltpu.VMEM)
 HELD = pl.BlockSpec(memory_space=pl.ANY)
+
+
+COVERS = {
+    ("a", 0): ("near", 0, 2),
+    ("b", 0): ("near", 2, 1),
+    ("a", 1): ("near", 3, 1),
+    ("b", 1): ("window", 1, 1),
+    ("a", 2): ("window", 2, 1),
+    ("b", 2): ("window", 3, 1),
+}
 
 
 def make_shards(seq_count, head_count):
@@ -396,13 +414,14 @@
         states_call = pl.pallas_call(
             functools.partial(state_kernel, levels=levels),
             in_specs=[HELD] * 5,
-            out_specs=[VMEM] * 6,
+            out_specs=[VMEM] * 7,
             out_shape=[
                 jax.ShapeDtypeStruct(lin_keys.shape, BF16),
                 jax.ShapeDtypeStruct(lin_values.shape, BF16),
                 jax.ShapeDtypeStruct((WINDOW, 2 * window_keys.shape[1]), BF16),
                 jax.ShapeDtypeStruct((buckets, width_in, DH), BF16),
-                jax.ShapeDtypeStruct((width_in, DH), BF16),
+                jax.ShapeDtypeStruct((width_in // 2, DH), BF16),
+                jax.ShapeDtypeStruct((width_in // 2, DH), BF16),
                 jax.ShapeDtypeStruct((3 * levels + 1, NEAR), F32),
             ],
             scratch_shapes=[
@@ -415,7 +434,7 @@
             compiler_params=params(16),
             name="states",
         )
-        keys, values, rim, local_states, state, flags = states_call(
+        keys, values, rim, local_states, state_a, state_b, flags = states_call(
             *[in_hbm(a) for a in (seq_lengths, lin_keys, lin_values, window_keys, window_values)]
         )
 
@@ -426,30 +445,35 @@
         def joined(level, state, arrived, cover):
             return pl.pallas_call(
                 functools.partial(join_kernel, level=level),
-                in_specs=[VMEM, VMEM, VMEM] + [HELD] * len(cover),
+                in_specs=[VMEM] * (3 + len(cover)),
                 out_specs=VMEM,
                 out_shape=jax.ShapeDtypeStruct(state.shape, BF16),
                 compiler_params=params(4),
                 name="join",
             )(flags, state, arrived, *cover)
 
+        token = jax.ShapeDtypeStruct((GROUP, TILE), F32)
+        weights = pl.pallas_call(
+            weights_kernel,
+            in_specs=[SMEM, VMEM],
+            out_specs=VMEM,
+            out_shape=jax.ShapeDtypeStruct((heads, *level_index.shape), F32),
+            compiler_params=params(8),
+            name="weights",
+        )(level_table, level_index)
+
         def neared(start, count, base):
-            operands = [level_table, level_index, queries, keys, values, local_states]
-            specs = [SMEM] + [VMEM] * 5
+            operands = [weights, queries, keys, values, local_states]
             aliases = {}
             if base is not None:
                 aliases = {len(operands): 0}
                 operands.append(base)
-                specs.append(VMEM)
             return pl.pallas_call(
                 functools.partial(near_kernel, spans=local_spans(tokens), start=start),
                 grid=(count,),
-                in_specs=specs,
+                in_specs=[VMEM] * len(operands),
                 out_specs=[VMEM, VMEM],
-                out_shape=[
-                    jax.ShapeDtypeStruct((blocks, width_in, NEAR), F32),
-                    jax.ShapeDtypeStruct((blocks, heads, level_index.shape[0], NEAR), F32),
-                ],
+                out_shape=[jax.ShapeDtypeStruct((blocks, width_in, NEAR), F32), token],
                 input_output_aliases=aliases,
                 compiler_params=params(8),
                 name="near",
@@ -459,59 +483,76 @@
 
         def windowed(start, count, rim, base):
             operands = [flags, queries, window_keys, window_values, window_gains]
-            specs = [VMEM] * 5
             aliases = {}
             if rim is not None:
                 operands += rim
-                specs += [VMEM] * len(rim)
             if base is not None:
                 aliases = {len(operands): 0}
                 operands.append(base)
-                specs.append(VMEM)
             return pl.pallas_call(
-                functools.partial(window_kernel, has_rim=rim is not None, members=members, start=start),
+                functools.partial(
+                    window_kernel, has_rim=rim is not None, members=members, start=start
+                ),
                 grid=(count,),
-                in_specs=specs,
-                out_specs=VMEM,
+                in_specs=[VMEM] * len(operands),
+                out_specs=[VMEM, VMEM],
                 scratch_shapes=[pltpu.VMEM((heads, DH, DH), F32)],
-                out_shape=jax.ShapeDtypeStruct((blocks, width_in, NEAR), BF16),
+                out_shape=[jax.ShapeDtypeStruct((blocks, width_in, NEAR), BF16), token],
                 input_output_aliases=aliases,
                 compiler_params=params(8),
                 name="window",
             )(*operands)
 
-        received = [exchanged(0, state)]
-        near, weights = neared(0, blocks, None)
-        state = joined(0, state, received[0], [near])
-        received.append(exchanged(1, state))
-        windows = windowed(1, blocks - 1, None, None)
-        cover = [windows]
-        steps = [(i, i + 1) for i in range(seq_count - 1)]
-        late = [(i, j) for i, j in steps if crosses_late(j, seq_count)]
-        for level in range(1, levels - 1):
-            if level == levels - 2:
-                early_rim = lax.ppermute(rim, "seq", [step for step in steps if step not in late])
-            state = joined(level, state, received[level], cover)
-            received.append(exchanged(level + 1, state))
-            cover = []
-        late_rim = lax.ppermute(rim, "seq", late)
-        windows = windowed(0, 1, (early_rim, late_rim), windows)
+        near, windows = None, None
+        plane = seq_count // 4
+        state = {"a": state_a, "b": state_b}
+        received = []
+        for half in "ab":
+            received.append(exchanged(0, state[half]))
+        target = [(i + plane) % seq_count if i % plane == plane - 1 else i for i in range(seq_count)]
+        ahead_rim = lax.ppermute(rim, "seq", list(enumerate(target)))
+        for level in range(levels - 1):
+            if level == 2:
+                picked = pl.pallas_call(
+                    functools.partial(pick_kernel, plane=plane),
+                    in_specs=[VMEM, VMEM],
+                    out_specs=VMEM,
+                    out_shape=jax.ShapeDtypeStruct(rim.shape, BF16),
+                    compiler_params=params(4),
+                    name="pick",
+                )(rim, ahead_rim)
+                target = [i // plane * plane + (i + 1) % plane for i in range(seq_count)]
+                rim = lax.ppermute(picked, "seq", list(enumerate(target)))
+            for half in "ab":
+                step = COVERS.get((half, level))
+                cover = []
+                if step is not None:
+                    kind, start, count = step
+                    if kind == "near":
+                        near, held = neared(start, count, near)
+                    else:
+                        windows, held = windowed(start, count, None, windows)
+                    cover = [held]
+                arrived = received[2 * level + "ab".index(half)]
+                state[half] = joined(level, state[half], arrived, cover)
+                received.append(exchanged(level + 1, state[half]))
+        windows, _ = windowed(0, 1, [rim], windows)
         near = pl.pallas_call(
             far_kernel,
             grid=(blocks,),
-            in_specs=[VMEM] * (3 + levels),
+            in_specs=[VMEM] * (2 + 2 * levels),
             out_specs=VMEM,
             out_shape=jax.ShapeDtypeStruct(near.shape, F32),
             input_output_aliases={3: 0},
             compiler_params=params(8),
             name="far",
-        )(flags, weights, queries, near, *received[:-1])
+        )(flags, weights, queries, near, *received[:-2])
 
         pieces = tokens // head_count // NEAR
         width = w_out.shape[1]
         shared = [flags, weights, queries, near, windows]
-        shared += [gain_linear.reshape(heads, 1, DH), received[-1]]
-        specs = [VMEM] * 7
+        shared += [gain_linear.reshape(heads, 1, DH), *received[-2:]]
+        specs = [VMEM] * 8
 
         arrived = [[] for _ in range(pieces)]
         for away in range(1, head_count):

time: 52.5 us -> 47.1 us (0.90)
  the two profiles are of different devices: /device:TPU:17 before, /device:TPU:0 now
where the time goes in v4:
time: 47.1 us; the launch traced here: 46.9 us
  Pallas kernels  23.7 us (50%)
  starting transfers between devices  17.6 us (37%)
  waiting for transfers between devices  4.88 us (10%)
    ppermute x8, starting transfers between devices, exchanged(): return lax.ppermute(state, 'seq', route)  15 us
    pallas_call x4, Pallas kernels, windowed(): pl.pallas_call(functools.partial(window_kernel, has_rim=rim is not None,...  5.5 us
    ppermute x8, waiting for transfers between devices, exchanged(): return lax.ppermute(state, 'seq', route)  4.72 us
    pallas_call x3, Pallas kernels, neared(): pl.pallas_call(functools.partial(near_kernel, spans=local_spans(tokens),...  3.73 us
    pallas_call x2, Pallas kernels, layer(): pl.pallas_call(functools.partial(partial_kernel, away=away, head_count=he...  3.59 us
    pallas_call x1, Pallas kernels, layer(): states_call(*[in_hbm(a) for a in (seq_lengths, lin_keys, lin_values, wind...  3 us
    pallas_call x1, Pallas kernels, layer(): pl.pallas_call(functools.partial(last_kernel, head_count=head_count, piec...  2.54 us
    pallas_call x1, Pallas kernels, layer(): pl.pallas_call(far_kernel, grid=(blocks,), in_specs=[VMEM] * (2 + 2 * lev...  2.09 us
  transfers between devices with their start and end apart: 12, of which 4 were waited for; matrix products, arithmetic and copies ran while one was open for 0% of the time, Pallas kernels for 35%

profile of v4, /device:TPU:0, one launch (start us, length us, event | category | flops | bytes accessed | tf_op | source)
XLA Modules:
  0.0 46.9 jit_solution(9359438833697106319)
XLA Ops:
  0.0 3.0 %states.1 = (bf16[1024,1024]{1,0:T(8,128)(2,1)S(1)}, bf16[1024,1024]{1,0:T(8,128)(2,1)S(1)}, bf16[256,512]{1,0:T(8,128)(2,1)S(1)}, bf16[3,1024,128]{2,1,0:T(8,12...) custom-call(s32[4]{0:T(128)} %lengths_hbm.1, ...), custom_call_target="tpu_custom_call" | custom-call | tf_op jit(solution)/shard_map/states/pallas_call | solution.py:437
  3.0 3.0 %collective-permute-start = (bf16[512,128]{1,0:T(8,128)(2,1)S(1)}, bf16[512,128]{1,0:T(8,128)(2,1)S(1)}, u32[]{:S(2)}, u32[]{:S(2)}) collective-permute-start(bf16[512,128]{1,0:T(8,128)(2,1)S(1)} %get-tuple-element.32.own_ref), channel_id=1, source_target_pairs={{0,2},{2,0},{4,6},{6,4},{8,10},{10,8},{12,14},{14,12},{16,18},{18,... | collective-permute-start | bytes 393224 | tf_op jit(solution)/shard_map/ppermute | solution.py:443
  6.0 0.7 %collective-permute-start.6 = (bf16[256,512]{1,0:T(8,128)(2,1)S(1)}, bf16[256,512]{1,0:T(8,128)(2,1)S(1)}, u32[]{:S(2)}, u32[]{:S(2)}) collective-permute-start(bf16[256,512]{1,0:T(8,128)(2,1)S(1)} %get-tuple-element.38.own_ref), channel_id=1, source_target_pairs={{0,0},{2,2},{4,4},{6,14},{8,8},{10,10},{12,12},{14,22},{16,16},{18... | collective-permute-start | bytes 786440 | tf_op jit(solution)/shard_map/ppermute | solution.py:513
  6.7 0.1 collective-permute-start.1
  6.8 0.9 %weights.1.weights_ref.refs_1_ = f32[8,15,1024]{2,1,0:T(8,128)S(1)} custom-call(f32[8,8]{1,0:T(8,128)S(1)} %copy-done.7, s32[15,1024]{1,0:T(8,128)S(1)} %copy-done.4), custom_call_target="tpu_custom_call" | custom-call | tf_op jit(solution)/shard_map/weights/pallas_call | solution.py:456
  7.7 1.9 %near.3 = (f32[4,1024,256]{2,1,0:T(8,128)S(1)}, f32[8,128]{1,0:T(8,128)S(1)}) custom-call(f32[8,15,1024]{2,1,0:T(8,128)S(1)} %weights.1.weights_ref.refs_1_, bf16[1024,1024]{1,0:T(8,128)(2,1)S(1)} %copy-done, bf16[1024,1024]{1,0:T(8,128)(2,1)S(1)} %get-tuple-element.26.k_ref, bf16[1024,1024]{1,0:T(8,128)(2,1)S(1)} %get-tuple-element.27.v_ref, ...), custom_call_target="tpu_custom_call" | custom-call | tf_op jit(solution)/shard_map/near/pallas_call | solution.py:471
  9.6 0.5 %collective-permute-done.arrived_ref.rest_0_ = bf16[512,128]{1,0:T(8,128)(2,1)S(1)} collective-permute-done((bf16[512,128]{1,0:T(8,128)(2,1)S(1)}, bf16[512,128]{1,0:T(8,128)(2,1)S(1)}, u32[]{:S(2)}, u32[]{:S(2)}) %collective-permute-start) | collective-permute-done | bytes 131104 | tf_op jit(solution)/shard_map/ppermute | solution.py:443
  10.2 4.4 %collective-permute-start.2 = (bf16[512,128]{1,0:T(8,128)(2,1)S(1)}, bf16[512,128]{1,0:T(8,128)(2,1)S(1)}, u32[]{:S(2)}, u32[]{:S(2)}) collective-permute-start(bf16[512,128]{1,0:T(8,128)(2,1)S(1)} %join.6.own_ref), channel_id=1, source_target_pairs={{0,4},{2,6},{4,0},{6,2},{8,12},{10,14},{12,8},{14,10},{16,20},{18,... | collective-permute-start | bytes 393224 | tf_op jit(solution)/shard_map/ppermute | solution.py:443
  14.6 0.9 %near.4 = (f32[4,1024,256]{2,1,0:T(8,128)S(1)}, f32[8,128]{1,0:T(8,128)S(1)}) custom-call(f32[8,15,1024]{2,1,0:T(8,128)S(1)} %weights.1.weights_ref.refs_1_, bf16[1024,1024]{1,0:T(8,128)(2,1)S(1)} %copy-done, bf16[1024,1024]{1,0:T(8,128)(2,1)S(1)} %get-tuple-element.26.k_ref, ...), custom_call_target="tpu_custom_call", output_to_operand_aliasing={{0}: (5, {})} | custom-call | tf_op jit(solution)/shard_map/near/pallas_call | solution.py:471
  15.5 0.0 collective-permute-done.1.arrived_ref.rest_1_
  15.5 0.1 join.7.own_ref
  15.6 0.1 collective-permute-start.3
  15.7 0.0 copy-start.2
  15.7 0.0 copy-start.3
  15.7 0.0 copy-start.5
  15.7 0.9 %near.5 = (f32[4,1024,256]{2,1,0:T(8,128)S(1)}, f32[8,128]{1,0:T(8,128)S(1)}) custom-call(f32[8,15,1024]{2,1,0:T(8,128)S(1)} %weights.1.weights_ref.refs_1_, bf16[1024,1024]{1,0:T(8,128)(2,1)S(1)} %copy-done, bf16[1024,1024]{1,0:T(8,128)(2,1)S(1)} %get-tuple-element.26.k_ref, ...), custom_call_target="tpu_custom_call", output_to_operand_aliasing={{0}: (5, {})} | custom-call | tf_op jit(solution)/shard_map/near/pallas_call | solution.py:471
  16.6 0.1 copy-done.2
  16.7 0.2 copy-done.3
  16.9 1.3 %window.4 = (bf16[4,1024,256]{2,1,0:T(8,128)(2,1)S(1)}, f32[8,128]{1,0:T(8,128)S(1)}) custom-call(f32[13,256]{1,0:T(8,128)S(1)} %get-tuple-element.25.flags_ref.refs_0_, bf16[1024,1024]{1,0:T(8,128)(2,1)S(1)} %copy-done, bf16[1024,256]{1,0:T(8,128)(2,1)S(1)} %copy-done.2, bf16[1024,256]{1,0:T(8,128)(2,1)S(1)} %copy-done.3, f32[8,1,128]{2,1,0:T(1,128)S(1)} %bitcast.2), custom_call_target="tpu_custom_call" | custom-call | tf_op jit(solution)/shard_map/window/pallas_call | solution.py:492
  18.2 0.0 collective-permute-done.2.arrived_ref.rest_2_
  18.2 0.1 join.8.own_ref
  18.3 1.6 %collective-permute-start.4 = (bf16[512,128]{1,0:T(8,128)(2,1)S(1)}, bf16[512,128]{1,0:T(8,128)(2,1)S(1)}, u32[]{:S(2)}, u32[]{:S(2)}) collective-permute-start(bf16[512,128]{1,0:T(8,128)(2,1)S(1)} %join.8.own_ref), channel_id=1, source_target_pairs={{0,8},{2,10},{4,12},{6,14},{8,0},{10,2},{12,4},{14,6},{16,24},{18,... | collective-permute-start | bytes 393224 | tf_op jit(solution)/shard_map/ppermute | solution.py:443
  19.9 0.0 collective-permute-done.6.ahead_ref
  20.0 1.3 %collective-permute-start.7 = (bf16[256,512]{1,0:T(8,128)(2,1)S(1)}, bf16[256,512]{1,0:T(8,128)(2,1)S(1)}, u32[]{:S(2)}, u32[]{:S(2)}) collective-permute-start(bf16[256,512]{1,0:T(8,128)(2,1)S(1)} %pick.1), channel_id=1, source_target_pairs={{0,2},{2,4},{4,6},{6,0},{8,10},{10,12},{12,14},{14,8},{16,18},{18,... | collective-permute-start | bytes 786440 | tf_op jit(solution)/shard_map/ppermute | solution.py:525
  21.3 0.0 collective-permute-done.3.arrived_ref.rest_3_
  21.3 1.0 %collective-permute-start.5 = (bf16[512,128]{1,0:T(8,128)(2,1)S(1)}, bf16[512,128]{1,0:T(8,128)(2,1)S(1)}, u32[]{:S(2)}, u32[]{:S(2)}) collective-permute-start(bf16[512,128]{1,0:T(8,128)(2,1)S(1)} %join.9.own_ref), channel_id=1, source_target_pairs={{0,8},{2,10},{4,12},{6,14},{8,0},{10,2},{12,4},{14,6},{16,24},{18,... | collective-permute-start | bytes 393224 | tf_op jit(solution)/shard_map/ppermute | solution.py:443
  22.3 1.3 %window.5 = (bf16[4,1024,256]{2,1,0:T(8,128)(2,1)S(1)}, f32[8,128]{1,0:T(8,128)S(1)}) custom-call(f32[13,256]{1,0:T(8,128)S(1)} %get-tuple-element.25.flags_ref.refs_0_, bf16[1024,1024]{1,0:T(8,128)(2,1)S(1)} %copy-done, bf16[1024,256]{1,0:T(8,128)(2,1)S(1)} %copy-done.2, bf16[1024,256]{1,0:T(8,128)(2,1)S(1)} %copy-done.3, ...), custom_call_target="tpu_custom_call", output_to_operand_aliasing={{0}: (5, {})} | custom-call | tf_op jit(solution)/shard_map/window/pallas_call | solution.py:492
  23.6 1.3 %window.6 = (bf16[4,1024,256]{2,1,0:T(8,128)(2,1)S(1)}, f32[8,128]{1,0:T(8,128)S(1)}) custom-call(f32[13,256]{1,0:T(8,128)S(1)} %get-tuple-element.25.flags_ref.refs_0_, bf16[1024,1024]{1,0:T(8,128)(2,1)S(1)} %copy-done, bf16[1024,256]{1,0:T(8,128)(2,1)S(1)} %copy-done.2, bf16[1024,256]{1,0:T(8,128)(2,1)S(1)} %copy-done.3, ...), custom_call_target="tpu_custom_call", output_to_operand_aliasing={{0}: (5, {})} | custom-call | tf_op jit(solution)/shard_map/window/pallas_call | solution.py:492
  25.0 0.0 collective-permute-done.4.rest_4_.arrived_ref
  25.1 2.2 %collective-permute-start.8 = (bf16[512,128]{1,0:T(8,128)(2,1)S(1)}, bf16[512,128]{1,0:T(8,128)(2,1)S(1)}, u32[]{:S(2)}, u32[]{:S(2)}) collective-permute-start(bf16[512,128]{1,0:T(8,128)(2,1)S(1)} %join.10), channel_id=1, source_target_pairs={{0,16},{2,18},{4,20},{6,22},{8,24},{10,26},{12,28},{14,30},{16,0},... | collective-permute-start | bytes 393224 | tf_op jit(solution)/shard_map/ppermute | solution.py:443
  27.2 0.0 collective-permute-done.5.rest_5_.arrived_ref
  27.3 2.6 %collective-permute-start.9 = (bf16[512,128]{1,0:T(8,128)(2,1)S(1)}, bf16[512,128]{1,0:T(8,128)(2,1)S(1)}, u32[]{:S(2)}, u32[]{:S(2)}) collective-permute-start(bf16[512,128]{1,0:T(8,128)(2,1)S(1)} %join.11), channel_id=1, source_target_pairs={{0,16},{2,18},{4,20},{6,22},{8,24},{10,26},{12,28},{14,30},{16,0},... | collective-permute-start | bytes 393224 | tf_op jit(solution)/shard_map/ppermute | solution.py:443
  29.9 2.1 %far.1.refs_3_ = f32[4,1024,256]{2,1,0:T(8,128)S(1)} custom-call(f32[13,256]{1,0:T(8,128)S(1)} %get-tuple-element.25.flags_ref.refs_0_, f32[8,15,1024]{2,1,0:T(8,128)S(1)} %weights.1.weights_ref.refs_1_, bf16[1024,1024]{1,0:T(8,128)(2,1)S(1)} %copy-done, f32[4,1024,256]{2,1,0:T(8,128)S(1)} %get-tuple-element.31.near_ref, ...), custom_call_target="tpu_custom_call", output_to_operand_aliasing={{}: (3, {})} | custom-call | tf_op jit(solution)/shard_map/far/pallas_call | solution.py:540
  32.0 0.0 collective-permute-done.7.rest_0_
  32.0 0.0 copy-start.1
  32.0 0.0 copy-start.6
  32.0 1.5 %window.7 = (bf16[4,1024,256]{2,1,0:T(8,128)(2,1)S(1)}, f32[8,128]{1,0:T(8,128)}) custom-call(f32[13,256]{1,0:T(8,128)S(1)} %get-tuple-element.25.flags_ref.refs_0_, bf16[1024,1024]{1,0:T(8,128)(2,1)S(1)} %copy-done, bf16[1024,256]{1,0:T(8,128)(2,1)S(1)} %copy-done.2, bf16[1024,256]{1,0:T(8,128)(2,1)S(1)} %copy-done.3, ...), custom_call_target="tpu_custom_call", output_to_operand_aliasing={{0}: (6, {})} | custom-call | tf_op jit(solution)/shard_map/window/pallas_call | solution.py:492
  33.5 2.8 %collective-permute-done.8.refs_6_ = bf16[512,128]{1,0:T(8,128)(2,1)S(1)} collective-permute-done((bf16[512,128]{1,0:T(8,128)(2,1)S(1)}, bf16[512,128]{1,0:T(8,128)(2,1)S(1)}, u32[]{:S(2)}, u32[]{:S(2)}) %collective-permute-start.8) | collective-permute-done | bytes 131104 | tf_op jit(solution)/shard_map/ppermute | solution.py:443
  36.3 1.4 %collective-permute-done.9.refs_7_ = bf16[512,128]{1,0:T(8,128)(2,1)S(1)} collective-permute-done((bf16[512,128]{1,0:T(8,128)(2,1)S(1)}, bf16[512,128]{1,0:T(8,128)(2,1)S(1)}, u32[]{:S(2)}, u32[]{:S(2)}) %collective-permute-start.9) | collective-permute-done | bytes 131104 | tf_op jit(solution)/shard_map/ppermute | solution.py:443
  37.7 1.8 %partial.3 = bf16[256,2048]{1,0:T(8,128)(2,1)S(1)} custom-call(f32[13,256]{1,0:T(8,128)S(1)} %get-tuple-element.25.flags_ref.refs_0_, f32[8,15,1024]{2,1,0:T(8,128)S(1)} %weights.1.weights_ref.refs_1_, bf16[1024,1024]{1,0:T(8,128)(2,1)S(1)} %copy-done, f32[4,1024,256]{2,1,0:T(8,128)S(1)} %far.1.refs_3_, bf16[4,1024,256]{2,1,0:T(8,128)(2,1)S(1)} %get-tuple-element.42.refs_4_, ...), custom_call_target="tpu_custom_call" | custom-call | tf_op jit(solution)/shard_map/partial/pallas_call | solution.py:561
  39.5 0.1 collective-permute-start.11
  39.6 1.8 %partial.2 = bf16[256,2048]{1,0:T(8,128)(2,1)S(1)} custom-call(f32[13,256]{1,0:T(8,128)S(1)} %get-tuple-element.25.flags_ref.refs_0_, f32[8,15,1024]{2,1,0:T(8,128)S(1)} %weights.1.weights_ref.refs_1_, bf16[1024,1024]{1,0:T(8,128)(2,1)S(1)} %copy-done, f32[4,1024,256]{2,1,0:T(8,128)S(1)} %far.1.refs_3_, bf16[4,1024,256]{2,1,0:T(8,128)(2,1)S(1)} %get-tuple-element.42.refs_4_, ...), custom_call_target="tpu_custom_call" | custom-call | tf_op jit(solution)/shard_map/partial/pallas_call | solution.py:561
  41.4 0.6 %collective-permute-start.10 = (bf16[256,2048]{1,0:T(8,128)(2,1)S(1)}, bf16[256,2048]{1,0:T(8,128)(2,1)S(1)}, u32[]{:S(2)}, u32[]{:S(2)}) collective-permute-start(bf16[256,2048]{1,0:T(8,128)(2,1)S(1)} %partial.2), channel_id=1, source_target_pairs={{0,1},{1,0},{2,3},{3,2},{4,5},{5,4},{6,7},{7,6},{8,9},{9,8},{10,11... | collective-permute-start | bytes 3145736 | tf_op jit(solution)/shard_map/ppermute | solution.py:571
  41.9 0.8 %attend.1.attended_ref = bf16[256,1024]{1,0:T(8,128)(2,1)S(1)} custom-call(f32[13,256]{1,0:T(8,128)S(1)} %get-tuple-element.25.flags_ref.refs_0_, f32[8,15,1024]{2,1,0:T(8,128)S(1)} %weights.1.weights_ref.refs_1_, bf16[1024,1024]{1,0:T(8,128)(2,1)S(1)} %copy-done, f32[4,1024,256]{2,1,0:T(8,128)S(1)} %far.1.refs_3_, ...), custom_call_target="tpu_custom_call" | custom-call | tf_op jit(solution)/shard_map/attend/pallas_call | solution.py:574
  42.8 0.0 collective-permute-done.11.refs_0_
  42.8 1.3 %project.1.refs_10_ = bf16[256,2048]{1,0:T(8,128)(2,1)S(1)} custom-call(bf16[256,1024]{1,0:T(8,128)(2,1)S(1)} %attend.1.attended_ref, bf16[1024,2048]{1,0:T(8,128)(2,1)S(1)} %copy-done.1, bf16[256,2048]{1,0:T(8,128)(2,1)S(1)} %collective-permute-done.11.refs_0_), custom_call_target="tpu_custom_call" | custom-call | tf_op jit(solution)/shard_map/project/pallas_call | solution.py:583
  44.1 0.2 collective-permute-done.10.refs_9_
  44.2 2.5 %last.1 = bf16[512,2048]{1,0:T(8,128)(2,1)} custom-call(f32[13,256]{1,0:T(8,128)S(1)} %get-tuple-element.25.flags_ref.refs_0_, f32[8,15,1024]{2,1,0:T(8,128)S(1)} %weights.1.weights_ref.refs_1_, bf16[1024,1024]{1,0:T(8,128)(2,1)S(1)} %copy-done, f32[4,1024,256]{2,1,0:T(8,128)S(1)} %far.1.refs_3_, bf16[4,1024,256]{2,1,0:T(8,128)(2,1)S(1)} %get-tuple-element.42.refs_4_, ...), custom_call_target="tpu_custom_call" | custom-call | tf_op jit(solution)/shard_map/last/pallas_call | solution.py:594
  (14 shorter events, 0.2 us)
Async XLA Ops:
  0.0 6.8 %copy-start.7 = (f32[8,8]{1,0:T(8,128)S(1)}, f32[8,8]{1,0:T(8,128)}, u32[]{:S(2)}) copy-start(f32[8,8]{1,0:T(8,128)} %table_ref.1) | copy-start | bytes 772
  0.0 6.8 %copy-start.4 = (s32[15,1024]{1,0:T(8,128)S(1)}, s32[15,1024]{1,0:T(8,128)}, u32[]{:S(2)}) copy-start(s32[15,1024]{1,0:T(8,128)} %index_ref.1) | copy-start | bytes 184324
  0.0 7.7 %copy-start = (bf16[1024,1024]{1,0:T(8,128)(2,1)S(1)}, bf16[1024,1024]{1,0:T(8,128)(2,1)}, u32[]{:S(2)}) copy-start(bf16[1024,1024]{1,0:T(8,128)(2,1)} %refs_2_.7) | copy-start | bytes 6291460
  3.0 7.1 %collective-permute-start = (bf16[512,128]{1,0:T(8,128)(2,1)S(1)}, bf16[512,128]{1,0:T(8,128)(2,1)S(1)}, u32[]{:S(2)}, u32[]{:S(2)}) collective-permute-start(bf16[512,128]{1,0:T(8,128)(2,1)S(1)} %get-tuple-element.32.own_ref), channel_id=1, source_target_pairs={{0,2},{2,0},{4,6},{6,4},{8,10},{10,8},{12,14},{14,12},{16,18},{18,... | collective-permute-start | bytes 393224 | tf_op jit(solution)/shard_map/ppermute | solution.py:443
  6.0 13.9 %collective-permute-start.6 = (bf16[256,512]{1,0:T(8,128)(2,1)S(1)}, bf16[256,512]{1,0:T(8,128)(2,1)S(1)}, u32[]{:S(2)}, u32[]{:S(2)}) collective-permute-start(bf16[256,512]{1,0:T(8,128)(2,1)S(1)} %get-tuple-element.38.own_ref), channel_id=1, source_target_pairs={{0,0},{2,2},{4,4},{6,14},{8,8},{10,10},{12,12},{14,22},{16,16},{18... | collective-permute-start | bytes 786440 | tf_op jit(solution)/shard_map/ppermute | solution.py:513
  6.7 8.8 %collective-permute-start.1 = (bf16[512,128]{1,0:T(8,128)(2,1)S(1)}, bf16[512,128]{1,0:T(8,128)(2,1)S(1)}, u32[]{:S(2)}, u32[]{:S(2)}) collective-permute-start(bf16[512,128]{1,0:T(8,128)(2,1)S(1)} %get-tuple-element.33.own_ref), channel_id=1, source_target_pairs={{0,2},{2,0},{4,6},{6,4},{8,10},{10,8},{12,14},{14,12},{16,18},{18,... | collective-permute-start | bytes 393224 | tf_op jit(solution)/shard_map/ppermute | solution.py:443
  10.2 8.0 %collective-permute-start.2 = (bf16[512,128]{1,0:T(8,128)(2,1)S(1)}, bf16[512,128]{1,0:T(8,128)(2,1)S(1)}, u32[]{:S(2)}, u32[]{:S(2)}) collective-permute-start(bf16[512,128]{1,0:T(8,128)(2,1)S(1)} %join.6.own_ref), channel_id=1, source_target_pairs={{0,4},{2,6},{4,0},{6,2},{8,12},{10,14},{12,8},{14,10},{16,20},{18,... | collective-permute-start | bytes 393224 | tf_op jit(solution)/shard_map/ppermute | solution.py:443
  15.6 5.7 %collective-permute-start.3 = (bf16[512,128]{1,0:T(8,128)(2,1)S(1)}, bf16[512,128]{1,0:T(8,128)(2,1)S(1)}, u32[]{:S(2)}, u32[]{:S(2)}) collective-permute-start(bf16[512,128]{1,0:T(8,128)(2,1)S(1)} %join.7.own_ref), channel_id=1, source_target_pairs={{0,4},{2,6},{4,0},{6,2},{8,12},{10,14},{12,8},{14,10},{16,20},{18,... | collective-permute-start | bytes 393224 | tf_op jit(solution)/shard_map/ppermute | solution.py:443
  15.7 1.0 %copy-start.2 = (bf16[1024,256]{1,0:T(8,128)(2,1)S(1)}, bf16[1024,256]{1,0:T(8,128)(2,1)}, u32[]{:S(2)}) copy-start(bf16[1024,256]{1,0:T(8,128)(2,1)} %k_ref.7) | copy-start | bytes 1572868
  15.7 1.2 %copy-start.3 = (bf16[1024,256]{1,0:T(8,128)(2,1)S(1)}, bf16[1024,256]{1,0:T(8,128)(2,1)}, u32[]{:S(2)}) copy-start(bf16[1024,256]{1,0:T(8,128)(2,1)} %v_ref.7) | copy-start | bytes 1572868
  15.7 1.2 %copy-start.5 = (f32[1024]{0:T(1024)S(1)}, f32[1024]{0:T(1024)}, u32[]{:S(2)}) copy-start(f32[1024]{0:T(1024)} %param.20) | copy-start | bytes 12292
  18.3 6.7 %collective-permute-start.4 = (bf16[512,128]{1,0:T(8,128)(2,1)S(1)}, bf16[512,128]{1,0:T(8,128)(2,1)S(1)}, u32[]{:S(2)}, u32[]{:S(2)}) collective-permute-start(bf16[512,128]{1,0:T(8,128)(2,1)S(1)} %join.8.own_ref), channel_id=1, source_target_pairs={{0,8},{2,10},{4,12},{6,14},{8,0},{10,2},{12,4},{14,6},{16,24},{18,... | collective-permute-start | bytes 393224 | tf_op jit(solution)/shard_map/ppermute | solution.py:443
  20.0 12.1 %collective-permute-start.7 = (bf16[256,512]{1,0:T(8,128)(2,1)S(1)}, bf16[256,512]{1,0:T(8,128)(2,1)S(1)}, u32[]{:S(2)}, u32[]{:S(2)}) collective-permute-start(bf16[256,512]{1,0:T(8,128)(2,1)S(1)} %pick.1), channel_id=1, source_target_pairs={{0,2},{2,4},{4,6},{6,0},{8,10},{10,12},{12,14},{14,8},{16,18},{18,... | collective-permute-start | bytes 786440 | tf_op jit(solution)/shard_map/ppermute | solution.py:525
  21.3 5.9 %collective-permute-start.5 = (bf16[512,128]{1,0:T(8,128)(2,1)S(1)}, bf16[512,128]{1,0:T(8,128)(2,1)S(1)}, u32[]{:S(2)}, u32[]{:S(2)}) collective-permute-start(bf16[512,128]{1,0:T(8,128)(2,1)S(1)} %join.9.own_ref), channel_id=1, source_target_pairs={{0,8},{2,10},{4,12},{6,14},{8,0},{10,2},{12,4},{14,6},{16,24},{18,... | collective-permute-start | bytes 393224 | tf_op jit(solution)/shard_map/ppermute | solution.py:443
  25.1 11.3 %collective-permute-start.8 = (bf16[512,128]{1,0:T(8,128)(2,1)S(1)}, bf16[512,128]{1,0:T(8,128)(2,1)S(1)}, u32[]{:S(2)}, u32[]{:S(2)}) collective-permute-start(bf16[512,128]{1,0:T(8,128)(2,1)S(1)} %join.10), channel_id=1, source_target_pairs={{0,16},{2,18},{4,20},{6,22},{8,24},{10,26},{12,28},{14,30},{16,0},... | collective-permute-start | bytes 393224 | tf_op jit(solution)/shard_map/ppermute | solution.py:443
  27.3 10.4 %collective-permute-start.9 = (bf16[512,128]{1,0:T(8,128)(2,1)S(1)}, bf16[512,128]{1,0:T(8,128)(2,1)S(1)}, u32[]{:S(2)}, u32[]{:S(2)}) collective-permute-start(bf16[512,128]{1,0:T(8,128)(2,1)S(1)} %join.11), channel_id=1, source_target_pairs={{0,16},{2,18},{4,20},{6,22},{8,24},{10,26},{12,28},{14,30},{16,0},... | collective-permute-start | bytes 393224 | tf_op jit(solution)/shard_map/ppermute | solution.py:443
  32.0 5.7 %copy-start.1 = (bf16[1024,2048]{1,0:T(8,128)(2,1)S(1)}, bf16[1024,2048]{1,0:T(8,128)(2,1)}, u32[]{:S(2)}) copy-start(bf16[1024,2048]{1,0:T(8,128)(2,1)} %refs_8_.5) | copy-start | bytes 12582916
  32.0 5.7 %copy-start.6 = (f32[1024]{0:T(1024)S(1)}, f32[1024]{0:T(1024)}, u32[]{:S(2)}) copy-start(f32[1024]{0:T(1024)} %param.19) | copy-start | bytes 12292
  39.5 3.3 %collective-permute-start.11 = (bf16[256,2048]{1,0:T(8,128)(2,1)S(1)}, bf16[256,2048]{1,0:T(8,128)(2,1)S(1)}, u32[]{:S(2)}, u32[]{:S(2)}) collective-permute-start(bf16[256,2048]{1,0:T(8,128)(2,1)S(1)} %partial.3), channel_id=1, source_target_pairs={{0,1},{1,0},{2,3},{3,2},{4,5},{5,4},{6,7},{7,6},{8,9},{9,8},{10,11... | collective-permute-start | bytes 3145736 | tf_op jit(solution)/shard_map/ppermute | solution.py:571
  41.4 2.8 %collective-permute-start.10 = (bf16[256,2048]{1,0:T(8,128)(2,1)S(1)}, bf16[256,2048]{1,0:T(8,128)(2,1)S(1)}, u32[]{:S(2)}, u32[]{:S(2)}) collective-permute-start(bf16[256,2048]{1,0:T(8,128)(2,1)S(1)} %partial.2), channel_id=1, source_target_pairs={{0,1},{1,0},{2,3},{3,2},{4,5},{5,4},{6,7},{7,6},{8,9},{9,8},{10,11... | collective-permute-start | bytes 3145736 | tf_op jit(solution)/shard_map/ppermute | solution.py:571

commit v5 on v4

--- a/solution.py
+++ b/solution.py
@@ -298,71 +298,54 @@
         out_ref[block, at, :] = near_ref[block, at, :] + reached
 
 
-def attend_block(block, flags_ref, weights_ref, q_ref, near_ref, win_ref, gain_ref, *bucket_refs):
+def attend_head(block, h, flags_ref, weights_ref, q_ref, near_ref, win_ref, gain_ref, *bucket_refs):
     last = flags_ref.shape[0] // 3 - 1
-    attended = []
-    for h in range(q_ref.shape[1] // DH):
-        at = head_columns(h)
-        reached = far_terms(block, last, h, flags_ref, weights_ref, q_ref, bucket_refs)
-        total = near_ref[block, at, :] + reached
-        mean = jnp.sum(total * total, axis=0, keepdims=True) * (1.0 / DH)
-        gain = gain_column(gain_ref, h)
-        gain = jnp.concatenate([gain] * (NEAR // DH), axis=1)
-        total = total * lax.rsqrt(mean + EPSILON) * gain
-        attended.append((total + win_ref[block, at, :].astype(F32)).astype(BF16).T)
-    return jnp.concatenate(attended, axis=1)
-
-
-def project(attended, w_ref, added, out_ref):
-    step = 2 * DH
-    for c in range(0, w_ref.shape[1], step):
-        product = dot(attended, w_ref[:, c : c + step])
-        for part in added:
-            product = product + part[:, c : c + step].astype(F32)
-        out_ref[:, c : c + step] = product.astype(BF16)
-
-
-def first_block(away, head_count, pieces):
-    return lax.rem(lax.axis_index("head") + away, head_count) * pieces
-
-
-def partial_kernel(*refs, away, head_count, pieces, piece):
-    block = first_block(away, head_count, pieces) + piece
-    project(attend_block(block, *refs[:8]), refs[8], [], refs[-1])
-
-
-def attend_kernel(*refs, head_count, pieces, piece):
-    block = first_block(0, head_count, pieces) + piece
-    refs[-1][...] = attend_block(block, *refs[:8])
-
-
-def project_kernel(attended_ref, w_ref, *refs):
-    project(attended_ref[...], w_ref, refs[:-1], refs[-1])
-
-
-def last_kernel(*refs, head_count, pieces, others):
-    w_ref = refs[8]
-    added = refs[9 : 9 + others]
-    done = refs[9 + others : 8 + others + pieces]
-    out_ref, result, sems = refs[8 + others + pieces :]
+    at = head_columns(h)
+    reached = far_terms(block, last, h, flags_ref, weights_ref, q_ref, bucket_refs)
+    total = near_ref[block, at, :] + reached
+    mean = jnp.sum(total * total, axis=0, keepdims=True) * (1.0 / DH)
+    gain = gain_column(gain_ref, h)
+    gain = jnp.concatenate([gain] * (NEAR // DH), axis=1)
+    total = total * lax.rsqrt(mean + EPSILON) * gain
+    return (total + win_ref[block, at, :].astype(F32)).astype(BF16).T
+
+
+def stage_kernel(*refs, head_count, pieces, now, after, carries):
+    shared, w_ref = refs[:8], refs[8]
+    heads = shared[2].shape[1] // DH
+
+    def block_of(stage):
+        away, piece = stage
+        return lax.rem(lax.axis_index("head") + away, head_count) * pieces + piece
+
+    if carries:
+        attended = refs[9][...]
+    else:
+        attended = [attend_head(block_of(now), h, *shared) for h in range(heads)]
+        attended = jnp.concatenate(attended, axis=1)
+    out_ref = refs[-1] if after is None else refs[-2]
+    step = w_ref.shape[1] // heads
+    for h in range(heads):
+        columns = slice(h * step, (h + 1) * step)
+        out_ref[:, columns] = dot(attended, w_ref[:, columns]).astype(out_ref.dtype)
+        if after is not None:
+            refs[-1][:, head_columns(h)] = attend_head(block_of(after), h, *shared)
+
+
+def finish_kernel(*refs, pieces):
+    out_ref, result, sems = refs[-3:]
     copies = []
-    for piece, source in enumerate(done):
-        rows = pl.ds(piece * NEAR, NEAR)
-        copies.append(pltpu.make_async_copy(source, out_ref.at[rows], sems.at[piece]))
-        copies[-1].start()
-    attended = attend_block(first_block(0, head_count, pieces) + pieces - 1, *refs[:8])
-    step = w_ref.shape[1] // (sems.shape[0] - pieces + 1)
-    rows = pl.ds((pieces - 1) * NEAR, NEAR)
-    for i, c in enumerate(range(0, w_ref.shape[1], step)):
-        columns = slice(c, c + step)
-        product = dot(attended, w_ref[:, columns])
-        for part in added:
-            product = product + part[:, columns].astype(F32)
-        result[:, columns] = product.astype(BF16)
-        at = pl.ds(c, step)
-        copy = pltpu.make_async_copy(result.at[:, at], out_ref.at[rows, at], sems.at[pieces - 1 + i])
-        copy.start()
-        copies.append(copy)
+    for piece in range(pieces):
+        parts = refs[piece:-3:pieces]
+        for row in range(0, NEAR, TILE):
+            rows = slice(row, row + TILE)
+            total = parts[0][rows, :]
+            for part in parts[1:]:
+                total = total + part[rows, :].astype(F32)
+            at = pl.ds(piece * NEAR + row, TILE)
+            result[piece * NEAR + row : piece * NEAR + row + TILE, :] = total.astype(BF16)
+            copies.append(pltpu.make_async_copy(result.at[at], out_ref.at[at], sems.at[len(copies)]))
+            copies[-1].start()
     for copy in copies:
         copy.wait()
 
@@ -554,55 +537,48 @@
         shared += [gain_linear.reshape(heads, 1, DH), *received[-2:]]
         specs = [VMEM] * 8
 
-        arrived = [[] for _ in range(pieces)]
-        for away in range(1, head_count):
-            route = [(i, (i + away) % head_count) for i in range(head_count)]
-            for piece in range(pieces):
-                partial = pl.pallas_call(
-                    functools.partial(
-                        partial_kernel, away=away, head_count=head_count, pieces=pieces, piece=piece
-                    ),
-                    in_specs=specs + [VMEM],
-                    out_specs=VMEM,
-                    out_shape=jax.ShapeDtypeStruct((NEAR, width), BF16),
-                    compiler_params=params(8),
-                    name="partial",
-                )(*shared, w_out)
-                arrived[piece].append(lax.ppermute(partial, "head", route))
-        finished = []
-        for piece in range(pieces - 1):
-            attended = pl.pallas_call(
-                functools.partial(attend_kernel, head_count=head_count, pieces=pieces, piece=piece),
-                in_specs=specs,
-                out_specs=VMEM,
-                out_shape=jax.ShapeDtypeStruct((NEAR, width_in), BF16),
+        stages = [(away, piece) for away in range(1, head_count) for piece in range(pieces)]
+        stages += [(0, piece) for piece in range(pieces)]
+        attended, arrived, own = None, [], []
+        for i, (away, piece) in enumerate(stages):
+            after = stages[i + 1] if i + 1 < len(stages) else None
+            carried = [] if attended is None else [attended]
+            shapes = [jax.ShapeDtypeStruct((NEAR, width), BF16 if away else F32)]
+            if after is not None:
+                shapes.append(jax.ShapeDtypeStruct((NEAR, width_in), BF16))
+            product, *attended = pl.pallas_call(
+                functools.partial(
+                    stage_kernel,
+                    head_count=head_count,
+                    pieces=pieces,
+                    now=(away, piece),
+                    after=after,
+                    carries=bool(carried),
+                ),
+                in_specs=specs + [VMEM] * (1 + len(carried)),
+                out_specs=[VMEM] * len(shapes),
+                out_shape=shapes,
                 compiler_params=params(8),
-                name="attend",
-            )(*shared)
-            finished.append(
-                pl.pallas_call(
-                    project_kernel,
-                    in_specs=[VMEM] * (2 + len(arrived[piece])),
-                    out_specs=VMEM,
-                    out_shape=jax.ShapeDtypeStruct((NEAR, width), BF16),
-                    compiler_params=params(8),
-                    name="project",
-                )(attended, w_out, *arrived[piece])
-            )
-        others = len(arrived[-1])
-        parts = 4
+                name="stage",
+            )(*shared, w_out, *carried)
+            attended = attended[0] if attended else None
+            if away:
+                route = [(i, (i + away) % head_count) for i in range(head_count)]
+                arrived.append(lax.ppermute(product, "head", route))
+            else:
+                own.append(product)
         return pl.pallas_call(
-            functools.partial(last_kernel, head_count=head_count, pieces=pieces, others=others),
-            in_specs=specs + [VMEM] * (others + pieces),
+            functools.partial(finish_kernel, pieces=pieces),
+            in_specs=[VMEM] * (len(own) + len(arrived)),
             out_specs=HELD,
             out_shape=jax.ShapeDtypeStruct((pieces * NEAR, width), BF16),
             scratch_shapes=[
-                pltpu.VMEM((NEAR, width), BF16),
-                pltpu.SemaphoreType.DMA((pieces - 1 + parts,)),
+                pltpu.VMEM((pieces * NEAR, width), BF16),
+                pltpu.SemaphoreType.DMA((pieces * (NEAR // TILE),)),
             ],
             compiler_params=params(8),
-            name="last",
-        )(*shared, w_out, *arrived[-1], *finished)
+            name="finish",
+        )(*own, *arrived)
 
     return layer
 

time: 47.1 us -> 46.7 us (level)
  transfers between devices with their start and end apart: 12 -> 12, of which waited for: 4 -> 3; matrix products, arithmetic and copies ran while one was open for 0% -> 0% of each run, Pallas kernels for 35% -> 36%
where the time goes in v5:
time: 46.7 us; the launch traced here: 46.5 us
  Pallas kernels  23.5 us (50%)
  starting transfers between devices  17.7 us (38%)
  waiting for transfers between devices  4.63 us (10%)
    ppermute x8, starting transfers between devices, exchanged(): return lax.ppermute(state, 'seq', route)  15.1 us
    pallas_call x4, Pallas kernels, layer(): pl.pallas_call(functools.partial(stage_kernel, head_count=head_count, pie...  6.62 us
    pallas_call x4, Pallas kernels, windowed(): pl.pallas_call(functools.partial(window_kernel, has_rim=rim is not None,...  5.41 us
    ppermute x8, waiting for transfers between devices, exchanged(): return lax.ppermute(state, 'seq', route)  4.62 us
    pallas_call x3, Pallas kernels, neared(): pl.pallas_call(functools.partial(near_kernel, spans=local_spans(tokens),...  3.73 us
    pallas_call x1, Pallas kernels, layer(): states_call(*[in_hbm(a) for a in (seq_lengths, lin_keys, lin_values, wind...  2.98 us
    pallas_call x1, Pallas kernels, layer(): pl.pallas_call(far_kernel, grid=(blocks,), in_specs=[VMEM] * (2 + 2 * lev...  2.11 us
    pallas_call x1, Pallas kernels, layer(): pl.pallas_call(functools.partial(finish_kernel, pieces=pieces), in_specs=...  1.44 us
  transfers between devices with their start and end apart: 12, of which 3 were waited for; matrix products, arithmetic and copies ran while one was open for 0% of the time, Pallas kernels for 36%

profile of v5, /device:TPU:0, one launch (start us, length us, event | category | flops | bytes accessed | tf_op | source)
XLA Modules:
  0.0 46.5 jit_solution(15222792600807600439)
XLA Ops:
  0.0 3.0 %states.1 = (bf16[1024,1024]{1,0:T(8,128)(2,1)S(1)}, bf16[1024,1024]{1,0:T(8,128)(2,1)S(1)}, bf16[256,512]{1,0:T(8,128)(2,1)S(1)}, bf16[3,1024,128]{2,1,0:T(8,12...) custom-call(s32[4]{0:T(128)} %lengths_hbm.1, ...), custom_call_target="tpu_custom_call" | custom-call | tf_op jit(solution)/shard_map/states/pallas_call | solution.py:420
  3.0 3.0 %collective-permute-start = (bf16[512,128]{1,0:T(8,128)(2,1)S(1)}, bf16[512,128]{1,0:T(8,128)(2,1)S(1)}, u32[]{:S(2)}, u32[]{:S(2)}) collective-permute-start(bf16[512,128]{1,0:T(8,128)(2,1)S(1)} %get-tuple-element.38.own_ref), channel_id=1, source_target_pairs={{0,2},{2,0},{4,6},{6,4},{8,10},{10,8},{12,14},{14,12},{16,18},{18,... | collective-permute-start | bytes 393224 | tf_op jit(solution)/shard_map/ppermute | solution.py:426
  6.0 0.7 %collective-permute-start.6 = (bf16[256,512]{1,0:T(8,128)(2,1)S(1)}, bf16[256,512]{1,0:T(8,128)(2,1)S(1)}, u32[]{:S(2)}, u32[]{:S(2)}) collective-permute-start(bf16[256,512]{1,0:T(8,128)(2,1)S(1)} %get-tuple-element.44.own_ref), channel_id=1, source_target_pairs={{0,0},{2,2},{4,4},{6,14},{8,8},{10,10},{12,12},{14,22},{16,16},{18... | collective-permute-start | bytes 786440 | tf_op jit(solution)/shard_map/ppermute | solution.py:496
  6.7 0.1 collective-permute-start.1
  6.8 0.0 copy-done.7
  6.8 0.9 %weights.1.weights_ref.refs_1_ = f32[8,15,1024]{2,1,0:T(8,128)S(1)} custom-call(f32[8,8]{1,0:T(8,128)S(1)} %copy-done.7, s32[15,1024]{1,0:T(8,128)S(1)} %copy-done.5), custom_call_target="tpu_custom_call" | custom-call | tf_op jit(solution)/shard_map/weights/pallas_call | solution.py:439
  7.7 1.9 %near.3 = (f32[4,1024,256]{2,1,0:T(8,128)S(1)}, f32[8,128]{1,0:T(8,128)S(1)}) custom-call(f32[8,15,1024]{2,1,0:T(8,128)S(1)} %weights.1.weights_ref.refs_1_, bf16[1024,1024]{1,0:T(8,128)(2,1)S(1)} %copy-done, bf16[1024,1024]{1,0:T(8,128)(2,1)S(1)} %get-tuple-element.32.k_ref, bf16[1024,1024]{1,0:T(8,128)(2,1)S(1)} %get-tuple-element.33.v_ref, ...), custom_call_target="tpu_custom_call" | custom-call | tf_op jit(solution)/shard_map/near/pallas_call | solution.py:454
  9.6 0.5 %collective-permute-done.arrived_ref.rest_0_ = bf16[512,128]{1,0:T(8,128)(2,1)S(1)} collective-permute-done((bf16[512,128]{1,0:T(8,128)(2,1)S(1)}, bf16[512,128]{1,0:T(8,128)(2,1)S(1)}, u32[]{:S(2)}, u32[]{:S(2)}) %collective-permute-start) | collective-permute-done | bytes 131104 | tf_op jit(solution)/shard_map/ppermute | solution.py:426
  10.2 4.4 %collective-permute-start.2 = (bf16[512,128]{1,0:T(8,128)(2,1)S(1)}, bf16[512,128]{1,0:T(8,128)(2,1)S(1)}, u32[]{:S(2)}, u32[]{:S(2)}) collective-permute-start(bf16[512,128]{1,0:T(8,128)(2,1)S(1)} %join.6.own_ref), channel_id=1, source_target_pairs={{0,4},{2,6},{4,0},{6,2},{8,12},{10,14},{12,8},{14,10},{16,20},{18,... | collective-permute-start | bytes 393224 | tf_op jit(solution)/shard_map/ppermute | solution.py:426
  14.6 0.9 %near.4 = (f32[4,1024,256]{2,1,0:T(8,128)S(1)}, f32[8,128]{1,0:T(8,128)S(1)}) custom-call(f32[8,15,1024]{2,1,0:T(8,128)S(1)} %weights.1.weights_ref.refs_1_, bf16[1024,1024]{1,0:T(8,128)(2,1)S(1)} %copy-done, bf16[1024,1024]{1,0:T(8,128)(2,1)S(1)} %get-tuple-element.32.k_ref, ...), custom_call_target="tpu_custom_call", output_to_operand_aliasing={{0}: (5, {})} | custom-call | tf_op jit(solution)/shard_map/near/pallas_call | solution.py:454
  15.5 0.0 collective-permute-done.1.arrived_ref.rest_1_
  15.5 0.1 join.7.own_ref
  15.6 0.1 collective-permute-start.3
  15.6 0.0 copy-start.3
  15.7 0.0 copy-start.6
  15.7 0.9 %near.5 = (f32[4,1024,256]{2,1,0:T(8,128)S(1)}, f32[8,128]{1,0:T(8,128)S(1)}) custom-call(f32[8,15,1024]{2,1,0:T(8,128)S(1)} %weights.1.weights_ref.refs_1_, bf16[1024,1024]{1,0:T(8,128)(2,1)S(1)} %copy-done, bf16[1024,1024]{1,0:T(8,128)(2,1)S(1)} %get-tuple-element.32.k_ref, ...), custom_call_target="tpu_custom_call", output_to_operand_aliasing={{0}: (5, {})} | custom-call | tf_op jit(solution)/shard_map/near/pallas_call | solution.py:454
  16.6 0.1 copy-done.2
  16.7 0.2 copy-done.3
  16.8 1.3 %window.4 = (bf16[4,1024,256]{2,1,0:T(8,128)(2,1)S(1)}, f32[8,128]{1,0:T(8,128)S(1)}) custom-call(f32[13,256]{1,0:T(8,128)S(1)} %get-tuple-element.31.flags_ref.refs_0_, bf16[1024,1024]{1,0:T(8,128)(2,1)S(1)} %copy-done, bf16[1024,256]{1,0:T(8,128)(2,1)S(1)} %copy-done.2, bf16[1024,256]{1,0:T(8,128)(2,1)S(1)} %copy-done.3, f32[8,1,128]{2,1,0:T(1,128)S(1)} %bitcast.6), custom_call_target="tpu_custom_call" | custom-call | tf_op jit(solution)/shard_map/window/pallas_call | solution.py:475
  18.2 0.0 collective-permute-done.2.arrived_ref.rest_2_
  18.2 1.6 %collective-permute-start.4 = (bf16[512,128]{1,0:T(8,128)(2,1)S(1)}, bf16[512,128]{1,0:T(8,128)(2,1)S(1)}, u32[]{:S(2)}, u32[]{:S(2)}) collective-permute-start(bf16[512,128]{1,0:T(8,128)(2,1)S(1)} %join.8.own_ref), channel_id=1, source_target_pairs={{0,8},{2,10},{4,12},{6,14},{8,0},{10,2},{12,4},{14,6},{16,24},{18,... | collective-permute-start | bytes 393224 | tf_op jit(solution)/shard_map/ppermute | solution.py:426
  19.9 0.0 collective-permute-done.6.ahead_ref
  19.9 1.3 %collective-permute-start.7 = (bf16[256,512]{1,0:T(8,128)(2,1)S(1)}, bf16[256,512]{1,0:T(8,128)(2,1)S(1)}, u32[]{:S(2)}, u32[]{:S(2)}) collective-permute-start(bf16[256,512]{1,0:T(8,128)(2,1)S(1)} %pick.1), channel_id=1, source_target_pairs={{0,2},{2,4},{4,6},{6,0},{8,10},{10,12},{12,14},{14,8},{16,18},{18,... | collective-permute-start | bytes 786440 | tf_op jit(solution)/shard_map/ppermute | solution.py:508
  21.2 0.0 collective-permute-done.3.arrived_ref.rest_3_
  21.3 1.0 %collective-permute-start.5 = (bf16[512,128]{1,0:T(8,128)(2,1)S(1)}, bf16[512,128]{1,0:T(8,128)(2,1)S(1)}, u32[]{:S(2)}, u32[]{:S(2)}) collective-permute-start(bf16[512,128]{1,0:T(8,128)(2,1)S(1)} %join.9.own_ref), channel_id=1, source_target_pairs={{0,8},{2,10},{4,12},{6,14},{8,0},{10,2},{12,4},{14,6},{16,24},{18,... | collective-permute-start | bytes 393224 | tf_op jit(solution)/shard_map/ppermute | solution.py:426
  22.3 1.3 %window.5 = (bf16[4,1024,256]{2,1,0:T(8,128)(2,1)S(1)}, f32[8,128]{1,0:T(8,128)S(1)}) custom-call(f32[13,256]{1,0:T(8,128)S(1)} %get-tuple-element.31.flags_ref.refs_0_, bf16[1024,1024]{1,0:T(8,128)(2,1)S(1)} %copy-done, bf16[1024,256]{1,0:T(8,128)(2,1)S(1)} %copy-done.2, bf16[1024,256]{1,0:T(8,128)(2,1)S(1)} %copy-done.3, ...), custom_call_target="tpu_custom_call", output_to_operand_aliasing={{0}: (5, {})} | custom-call | tf_op jit(solution)/shard_map/window/pallas_call | solution.py:475
  23.6 1.3 %window.6 = (bf16[4,1024,256]{2,1,0:T(8,128)(2,1)S(1)}, f32[8,128]{1,0:T(8,128)S(1)}) custom-call(f32[13,256]{1,0:T(8,128)S(1)} %get-tuple-element.31.flags_ref.refs_0_, bf16[1024,1024]{1,0:T(8,128)(2,1)S(1)} %copy-done, bf16[1024,256]{1,0:T(8,128)(2,1)S(1)} %copy-done.2, bf16[1024,256]{1,0:T(8,128)(2,1)S(1)} %copy-done.3, ...), custom_call_target="tpu_custom_call", output_to_operand_aliasing={{0}: (5, {})} | custom-call | tf_op jit(solution)/shard_map/window/pallas_call | solution.py:475
  24.9 0.0 collective-permute-done.4.rest_4_.arrived_ref
  25.0 2.2 %collective-permute-start.8 = (bf16[512,128]{1,0:T(8,128)(2,1)S(1)}, bf16[512,128]{1,0:T(8,128)(2,1)S(1)}, u32[]{:S(2)}, u32[]{:S(2)}) collective-permute-start(bf16[512,128]{1,0:T(8,128)(2,1)S(1)} %join.10), channel_id=1, source_target_pairs={{0,16},{2,18},{4,20},{6,22},{8,24},{10,26},{12,28},{14,30},{16,0},... | collective-permute-start | bytes 393224 | tf_op jit(solution)/shard_map/ppermute | solution.py:426
  27.1 0.0 collective-permute-done.5.rest_5_.arrived_ref
  27.2 2.7 %collective-permute-start.9 = (bf16[512,128]{1,0:T(8,128)(2,1)S(1)}, bf16[512,128]{1,0:T(8,128)(2,1)S(1)}, u32[]{:S(2)}, u32[]{:S(2)}) collective-permute-start(bf16[512,128]{1,0:T(8,128)(2,1)S(1)} %join.11), channel_id=1, source_target_pairs={{0,16},{2,18},{4,20},{6,22},{8,24},{10,26},{12,28},{14,30},{16,0},... | collective-permute-start | bytes 393224 | tf_op jit(solution)/shard_map/ppermute | solution.py:426
  29.9 2.1 %far.1.refs_3_ = f32[4,1024,256]{2,1,0:T(8,128)S(1)} custom-call(f32[13,256]{1,0:T(8,128)S(1)} %get-tuple-element.31.flags_ref.refs_0_, f32[8,15,1024]{2,1,0:T(8,128)S(1)} %weights.1.weights_ref.refs_1_, bf16[1024,1024]{1,0:T(8,128)(2,1)S(1)} %copy-done, f32[4,1024,256]{2,1,0:T(8,128)S(1)} %get-tuple-element.37.near_ref, ...), custom_call_target="tpu_custom_call", output_to_operand_aliasing={{}: (3, {})} | custom-call | tf_op jit(solution)/shard_map/far/pallas_call | solution.py:523
  32.0 0.0 collective-permute-done.7.rest_0_
  32.0 0.0 copy-start.1
  32.0 0.0 copy-start.4
  32.0 1.5 %window.7 = (bf16[4,1024,256]{2,1,0:T(8,128)(2,1)S(1)}, f32[8,128]{1,0:T(8,128)}) custom-call(f32[13,256]{1,0:T(8,128)S(1)} %get-tuple-element.31.flags_ref.refs_0_, bf16[1024,1024]{1,0:T(8,128)(2,1)S(1)} %copy-done, bf16[1024,256]{1,0:T(8,128)(2,1)S(1)} %copy-done.2, bf16[1024,256]{1,0:T(8,128)(2,1)S(1)} %copy-done.3, ...), custom_call_target="tpu_custom_call", output_to_operand_aliasing={{0}: (6, {})} | custom-call | tf_op jit(solution)/shard_map/window/pallas_call | solution.py:475
  33.5 2.7 %collective-permute-done.8.refs_6_ = bf16[512,128]{1,0:T(8,128)(2,1)S(1)} collective-permute-done((bf16[512,128]{1,0:T(8,128)(2,1)S(1)}, bf16[512,128]{1,0:T(8,128)(2,1)S(1)}, u32[]{:S(2)}, u32[]{:S(2)}) %collective-permute-start.8) | collective-permute-done | bytes 131104 | tf_op jit(solution)/shard_map/ppermute | solution.py:426
  36.2 1.4 %collective-permute-done.9.refs_7_ = bf16[512,128]{1,0:T(8,128)(2,1)S(1)} collective-permute-done((bf16[512,128]{1,0:T(8,128)(2,1)S(1)}, bf16[512,128]{1,0:T(8,128)(2,1)S(1)}, u32[]{:S(2)}, u32[]{:S(2)}) %collective-permute-start.9) | collective-permute-done | bytes 131104 | tf_op jit(solution)/shard_map/ppermute | solution.py:426
  37.6 0.0 copy-done.4
  37.6 2.1 %stage.4 = (bf16[256,2048]{1,0:T(8,128)(2,1)S(1)}, bf16[256,1024]{1,0:T(8,128)(2,1)S(1)}) custom-call(f32[13,256]{1,0:T(8,128)S(1)} %get-tuple-element.31.flags_ref.refs_0_, f32[8,15,1024]{2,1,0:T(8,128)S(1)} %weights.1.weights_ref.refs_1_, bf16[1024,1024]{1,0:T(8,128)(2,1)S(1)} %copy-done, f32[4,1024,256]{2,1,0:T(8,128)S(1)} %far.1.refs_3_, ...), custom_call_target="tpu_custom_call" | custom-call | tf_op jit(solution)/shard_map/stage/pallas_call | solution.py:549
  39.7 0.1 collective-permute-start.10
  39.8 1.6 %stage.5 = (bf16[256,2048]{1,0:T(8,128)(2,1)S(1)}, bf16[256,1024]{1,0:T(8,128)(2,1)S(1)}) custom-call(f32[13,256]{1,0:T(8,128)S(1)} %get-tuple-element.31.flags_ref.refs_0_, f32[8,15,1024]{2,1,0:T(8,128)S(1)} %weights.1.weights_ref.refs_1_, bf16[1024,1024]{1,0:T(8,128)(2,1)S(1)} %copy-done, f32[4,1024,256]{2,1,0:T(8,128)S(1)} %far.1.refs_3_, ...), custom_call_target="tpu_custom_call" | custom-call | tf_op jit(solution)/shard_map/stage/pallas_call | solution.py:549
  41.4 0.6 %collective-permute-start.11 = (bf16[256,2048]{1,0:T(8,128)(2,1)S(1)}, bf16[256,2048]{1,0:T(8,128)(2,1)S(1)}, u32[]{:S(2)}, u32[]{:S(2)}) collective-permute-start(bf16[256,2048]{1,0:T(8,128)(2,1)S(1)} %get-tuple-element.56), channel_id=1, source_target_pairs={{0,1},{1,0},{2,3},{3,2},{4,5},{5,4},{6,7},{7,6},{8,9},{9,8},{10,11... | collective-permute-start | bytes 3145736 | tf_op jit(solution)/shard_map/ppermute | solution.py:567
  42.0 1.6 %stage.6 = (f32[256,2048]{1,0:T(8,128)S(1)}, bf16[256,1024]{1,0:T(8,128)(2,1)S(1)}) custom-call(f32[13,256]{1,0:T(8,128)S(1)} %get-tuple-element.31.flags_ref.refs_0_, f32[8,15,1024]{2,1,0:T(8,128)S(1)} %weights.1.weights_ref.refs_1_, bf16[1024,1024]{1,0:T(8,128)(2,1)S(1)} %copy-done, f32[4,1024,256]{2,1,0:T(8,128)S(1)} %far.1.refs_3_, ...), custom_call_target="tpu_custom_call" | custom-call | tf_op jit(solution)/shard_map/stage/pallas_call | solution.py:549
  43.6 1.3 %stage.7.refs_1_ = f32[256,2048]{1,0:T(8,128)S(1)} custom-call(f32[13,256]{1,0:T(8,128)S(1)} %get-tuple-element.31.flags_ref.refs_0_, f32[8,15,1024]{2,1,0:T(8,128)S(1)} %weights.1.weights_ref.refs_1_, bf16[1024,1024]{1,0:T(8,128)(2,1)S(1)} %copy-done, f32[4,1024,256]{2,1,0:T(8,128)S(1)} %far.1.refs_3_, bf16[4,1024,256]{2,1,0:T(8,128)(2,1)S(1)} %get-tuple-element.48.refs_4_, ...), custom_call_target="tpu_custom_call" | custom-call | tf_op jit(solution)/shard_map/stage/pallas_call | solution.py:549
  44.9 0.0 collective-permute-done.10.refs_2_
  44.9 0.0 collective-permute-done.11.refs_3_
  44.9 1.4 %finish.1 = bf16[512,2048]{1,0:T(8,128)(2,1)} custom-call(f32[256,2048]{1,0:T(8,128)S(1)} %get-tuple-element.53.refs_0_, f32[256,2048]{1,0:T(8,128)S(1)} %stage.7.refs_1_, bf16[256,2048]{1,0:T(8,128)(2,1)S(1)} %collective-permute-done.10.refs_2_, bf16[256,2048]{1,0:T(8,128)(2,1)S(1)} %collective-permute-done.11.refs_3_), custom_call_target="tpu_custom_call" | custom-call | tf_op jit(solution)/shard_map/finish/pallas_call | solution.py:570
  (14 shorter events, 0.2 us)
Async XLA Ops:
  0.0 6.8 %copy-start.7 = (f32[8,8]{1,0:T(8,128)S(1)}, f32[8,8]{1,0:T(8,128)}, u32[]{:S(2)}) copy-start(f32[8,8]{1,0:T(8,128)} %table_ref.1) | copy-start | bytes 772
  0.0 6.8 %copy-start.5 = (s32[15,1024]{1,0:T(8,128)S(1)}, s32[15,1024]{1,0:T(8,128)}, u32[]{:S(2)}) copy-start(s32[15,1024]{1,0:T(8,128)} %index_ref.1) | copy-start | bytes 184324
  0.0 7.7 %copy-start = (bf16[1024,1024]{1,0:T(8,128)(2,1)S(1)}, bf16[1024,1024]{1,0:T(8,128)(2,1)}, u32[]{:S(2)}) copy-start(bf16[1024,1024]{1,0:T(8,128)(2,1)} %refs_2_.7) | copy-start | bytes 6291460
  3.0 7.1 %collective-permute-start = (bf16[512,128]{1,0:T(8,128)(2,1)S(1)}, bf16[512,128]{1,0:T(8,128)(2,1)S(1)}, u32[]{:S(2)}, u32[]{:S(2)}) collective-permute-start(bf16[512,128]{1,0:T(8,128)(2,1)S(1)} %get-tuple-element.38.own_ref), channel_id=1, source_target_pairs={{0,2},{2,0},{4,6},{6,4},{8,10},{10,8},{12,14},{14,12},{16,18},{18,... | collective-permute-start | bytes 393224 | tf_op jit(solution)/shard_map/ppermute | solution.py:426
  6.0 13.8 %collective-permute-start.6 = (bf16[256,512]{1,0:T(8,128)(2,1)S(1)}, bf16[256,512]{1,0:T(8,128)(2,1)S(1)}, u32[]{:S(2)}, u32[]{:S(2)}) collective-permute-start(bf16[256,512]{1,0:T(8,128)(2,1)S(1)} %get-tuple-element.44.own_ref), channel_id=1, source_target_pairs={{0,0},{2,2},{4,4},{6,14},{8,8},{10,10},{12,12},{14,22},{16,16},{18... | collective-permute-start | bytes 786440 | tf_op jit(solution)/shard_map/ppermute | solution.py:496
  6.7 8.8 %collective-permute-start.1 = (bf16[512,128]{1,0:T(8,128)(2,1)S(1)}, bf16[512,128]{1,0:T(8,128)(2,1)S(1)}, u32[]{:S(2)}, u32[]{:S(2)}) collective-permute-start(bf16[512,128]{1,0:T(8,128)(2,1)S(1)} %get-tuple-element.39.own_ref), channel_id=1, source_target_pairs={{0,2},{2,0},{4,6},{6,4},{8,10},{10,8},{12,14},{14,12},{16,18},{18,... | collective-permute-start | bytes 393224 | tf_op jit(solution)/shard_map/ppermute | solution.py:426
  10.2 8.0 %collective-permute-start.2 = (bf16[512,128]{1,0:T(8,128)(2,1)S(1)}, bf16[512,128]{1,0:T(8,128)(2,1)S(1)}, u32[]{:S(2)}, u32[]{:S(2)}) collective-permute-start(bf16[512,128]{1,0:T(8,128)(2,1)S(1)} %join.6.own_ref), channel_id=1, source_target_pairs={{0,4},{2,6},{4,0},{6,2},{8,12},{10,14},{12,8},{14,10},{16,20},{18,... | collective-permute-start | bytes 393224 | tf_op jit(solution)/shard_map/ppermute | solution.py:426
  15.6 5.7 %collective-permute-start.3 = (bf16[512,128]{1,0:T(8,128)(2,1)S(1)}, bf16[512,128]{1,0:T(8,128)(2,1)S(1)}, u32[]{:S(2)}, u32[]{:S(2)}) collective-permute-start(bf16[512,128]{1,0:T(8,128)(2,1)S(1)} %join.7.own_ref), channel_id=1, source_target_pairs={{0,4},{2,6},{4,0},{6,2},{8,12},{10,14},{12,8},{14,10},{16,20},{18,... | collective-permute-start | bytes 393224 | tf_op jit(solution)/shard_map/ppermute | solution.py:426
  15.6 1.0 %copy-start.2 = (bf16[1024,256]{1,0:T(8,128)(2,1)S(1)}, bf16[1024,256]{1,0:T(8,128)(2,1)}, u32[]{:S(2)}) copy-start(bf16[1024,256]{1,0:T(8,128)(2,1)} %k_ref.7) | copy-start | bytes 1572868
  15.6 1.2 %copy-start.3 = (bf16[1024,256]{1,0:T(8,128)(2,1)S(1)}, bf16[1024,256]{1,0:T(8,128)(2,1)}, u32[]{:S(2)}) copy-start(bf16[1024,256]{1,0:T(8,128)(2,1)} %v_ref.7) | copy-start | bytes 1572868
  15.7 1.2 %copy-start.6 = (f32[1024]{0:T(1024)S(1)}, f32[1024]{0:T(1024)}, u32[]{:S(2)}) copy-start(f32[1024]{0:T(1024)} %param.20) | copy-start | bytes 12292
  18.2 6.7 %collective-permute-start.4 = (bf16[512,128]{1,0:T(8,128)(2,1)S(1)}, bf16[512,128]{1,0:T(8,128)(2,1)S(1)}, u32[]{:S(2)}, u32[]{:S(2)}) collective-permute-start(bf16[512,128]{1,0:T(8,128)(2,1)S(1)} %join.8.own_ref), channel_id=1, source_target_pairs={{0,8},{2,10},{4,12},{6,14},{8,0},{10,2},{12,4},{14,6},{16,24},{18,... | collective-permute-start | bytes 393224 | tf_op jit(solution)/shard_map/ppermute | solution.py:426
  19.9 12.1 %collective-permute-start.7 = (bf16[256,512]{1,0:T(8,128)(2,1)S(1)}, bf16[256,512]{1,0:T(8,128)(2,1)S(1)}, u32[]{:S(2)}, u32[]{:S(2)}) collective-permute-start(bf16[256,512]{1,0:T(8,128)(2,1)S(1)} %pick.1), channel_id=1, source_target_pairs={{0,2},{2,4},{4,6},{6,0},{8,10},{10,12},{12,14},{14,8},{16,18},{18,... | collective-permute-start | bytes 786440 | tf_op jit(solution)/shard_map/ppermute | solution.py:508
  21.3 5.9 %collective-permute-start.5 = (bf16[512,128]{1,0:T(8,128)(2,1)S(1)}, bf16[512,128]{1,0:T(8,128)(2,1)S(1)}, u32[]{:S(2)}, u32[]{:S(2)}) collective-permute-start(bf16[512,128]{1,0:T(8,128)(2,1)S(1)} %join.9.own_ref), channel_id=1, source_target_pairs={{0,8},{2,10},{4,12},{6,14},{8,0},{10,2},{12,4},{14,6},{16,24},{18,... | collective-permute-start | bytes 393224 | tf_op jit(solution)/shard_map/ppermute | solution.py:426
  25.0 11.2 %collective-permute-start.8 = (bf16[512,128]{1,0:T(8,128)(2,1)S(1)}, bf16[512,128]{1,0:T(8,128)(2,1)S(1)}, u32[]{:S(2)}, u32[]{:S(2)}) collective-permute-start(bf16[512,128]{1,0:T(8,128)(2,1)S(1)} %join.10), channel_id=1, source_target_pairs={{0,16},{2,18},{4,20},{6,22},{8,24},{10,26},{12,28},{14,30},{16,0},... | collective-permute-start | bytes 393224 | tf_op jit(solution)/shard_map/ppermute | solution.py:426
  27.2 10.4 %collective-permute-start.9 = (bf16[512,128]{1,0:T(8,128)(2,1)S(1)}, bf16[512,128]{1,0:T(8,128)(2,1)S(1)}, u32[]{:S(2)}, u32[]{:S(2)}) collective-permute-start(bf16[512,128]{1,0:T(8,128)(2,1)S(1)} %join.11), channel_id=1, source_target_pairs={{0,16},{2,18},{4,20},{6,22},{8,24},{10,26},{12,28},{14,30},{16,0},... | collective-permute-start | bytes 393224 | tf_op jit(solution)/shard_map/ppermute | solution.py:426
  32.0 5.6 %copy-start.1 = (bf16[1024,2048]{1,0:T(8,128)(2,1)S(1)}, bf16[1024,2048]{1,0:T(8,128)(2,1)}, u32[]{:S(2)}) copy-start(bf16[1024,2048]{1,0:T(8,128)(2,1)} %refs_8_.7) | copy-start | bytes 12582916
  32.0 5.6 %copy-start.4 = (f32[1024]{0:T(1024)S(1)}, f32[1024]{0:T(1024)}, u32[]{:S(2)}) copy-start(f32[1024]{0:T(1024)} %param.19) | copy-start | bytes 12292
  39.7 5.2 %collective-permute-start.10 = (bf16[256,2048]{1,0:T(8,128)(2,1)S(1)}, bf16[256,2048]{1,0:T(8,128)(2,1)S(1)}, u32[]{:S(2)}, u32[]{:S(2)}) collective-permute-start(bf16[256,2048]{1,0:T(8,128)(2,1)S(1)} %get-tuple-element.55), channel_id=1, source_target_pairs={{0,1},{1,0},{2,3},{3,2},{4,5},{5,4},{6,7},{7,6},{8,9},{9,8},{10,11... | collective-permute-start | bytes 3145736 | tf_op jit(solution)/shard_map/ppermute | solution.py:567
  41.4 3.5 %collective-permute-start.11 = (bf16[256,2048]{1,0:T(8,128)(2,1)S(1)}, bf16[256,2048]{1,0:T(8,128)(2,1)S(1)}, u32[]{:S(2)}, u32[]{:S(2)}) collective-permute-start(bf16[256,2048]{1,0:T(8,128)(2,1)S(1)} %get-tuple-element.56), channel_id=1, source_target_pairs={{0,1},{1,0},{2,3},{3,2},{4,5},{5,4},{6,7},{7,6},{8,9},{9,8},{10,11... | collective-permute-start | bytes 3145736 | tf_op jit(solution)/shard_map/ppermute | solution.py:567

commit v6 on v5

--- a/solution.py
+++ b/solution.py
@@ -289,37 +289,48 @@
     return dot(jnp.concatenate(lhs, axis=1), jnp.concatenate(rhs, axis=0))
 
 
-def far_kernel(flags_ref, weights_ref, q_ref, near_ref, *rest):
-    bucket_refs, out_ref = rest[:-1], rest[-1]
+def far_kernel(flags_ref, weights_ref, q_ref, gain_ref, near_ref, *rest):
+    bucket_refs, (out_ref, asked_ref, gains_ref) = rest[:-3], rest[-3:]
     block = pl.program_id(0)
-    for h in range(q_ref.shape[1] // DH):
+    heads = q_ref.shape[1] // DH
+    last = flags_ref.shape[0] // 3 - 1
+    level = weights_ref.shape[1] - 1
+    tokens = pl.ds(pl.multiple_of(block * NEAR, NEAR), NEAR)
+
+    @pl.when(block == 0)
+    def _():
+        for h in range(heads):
+            gains_ref[h] = gain_column(gain_ref, h)
+
+    for h in range(heads):
         at = head_columns(h)
         reached = far_terms(block, 0, h, flags_ref, weights_ref, q_ref, bucket_refs)
         out_ref[block, at, :] = near_ref[block, at, :] + reached
-
-
-def attend_head(block, h, flags_ref, weights_ref, q_ref, near_ref, win_ref, gain_ref, *bucket_refs):
-    last = flags_ref.shape[0] // 3 - 1
+        row = weights_ref[h, level : level + 1, tokens] * flag_row(flags_ref, last, 2)
+        asked_ref[block, at, :] = q_ref[tokens, at].T * row.astype(BF16)
+
+
+def attend_head(block, h, asked_ref, near_ref, win_ref, gains_ref, *bucket_refs):
     at = head_columns(h)
-    reached = far_terms(block, last, h, flags_ref, weights_ref, q_ref, bucket_refs)
+    half = near_ref.shape[1] // 2 // DH
+    reached = dot(bucket_refs[h // half][head_columns(h % half), :], asked_ref[block, at, :])
     total = near_ref[block, at, :] + reached
     mean = jnp.sum(total * total, axis=0, keepdims=True) * (1.0 / DH)
-    gain = gain_column(gain_ref, h)
-    gain = jnp.concatenate([gain] * (NEAR // DH), axis=1)
+    gain = jnp.concatenate([gains_ref[h]] * (NEAR // DH), axis=1)
     total = total * lax.rsqrt(mean + EPSILON) * gain
     return (total + win_ref[block, at, :].astype(F32)).astype(BF16).T
 
 
 def stage_kernel(*refs, head_count, pieces, now, after, carries):
-    shared, w_ref = refs[:8], refs[8]
-    heads = shared[2].shape[1] // DH
+    shared, w_ref = refs[:6], refs[6]
+    heads = shared[1].shape[1] // DH
 
     def block_of(stage):
         away, piece = stage
         return lax.rem(lax.axis_index("head") + away, head_count) * pieces + piece
 
     if carries:
-        attended = refs[9][...]
+        attended = refs[7][...]
     else:
         attended = [attend_head(block_of(now), h, *shared) for h in range(heads)]
         attended = jnp.concatenate(attended, axis=1)
@@ -520,22 +531,25 @@
                 state[half] = joined(level, state[half], arrived, cover)
                 received.append(exchanged(level + 1, state[half]))
         windows, _ = windowed(0, 1, [rim], windows)
-        near = pl.pallas_call(
+        near, asked, gains = pl.pallas_call(
             far_kernel,
             grid=(blocks,),
-            in_specs=[VMEM] * (2 + 2 * levels),
-            out_specs=VMEM,
-            out_shape=jax.ShapeDtypeStruct(near.shape, F32),
-            input_output_aliases={3: 0},
+            in_specs=[VMEM] * (3 + 2 * levels),
+            out_specs=[VMEM] * 3,
+            out_shape=[
+                jax.ShapeDtypeStruct(near.shape, F32),
+                jax.ShapeDtypeStruct(near.shape, BF16),
+                jax.ShapeDtypeStruct((heads, DH, DH), F32),
+            ],
+            input_output_aliases={4: 0},
             compiler_params=params(8),
             name="far",
-        )(flags, weights, queries, near, *received[:-2])
+        )(flags, weights, queries, gain_linear.reshape(heads, 1, DH), near, *received[:-2])
 
         pieces = tokens // head_count // NEAR
         width = w_out.shape[1]
-        shared = [flags, weights, queries, near, windows]
-        shared += [gain_linear.reshape(heads, 1, DH), *received[-2:]]
-        specs = [VMEM] * 8
+        shared = [asked, near, windows, gains, *received[-2:]]
+        specs = [VMEM] * len(shared)
 
         stages = [(away, piece) for away in range(1, head_count) for piece in range(pieces)]
         stages += [(0, piece) for piece in range(pieces)]

time: 46.7 us -> 46.3 us (level)
  transfers between devices with their start and end apart: 12 -> 12, of which waited for: 3 -> 3; matrix products, arithmetic and copies ran while one was open for 0% -> 0% of each run, Pallas kernels for 36% -> 37%
where the time goes in v6:
time: 46.3 us; the launch traced here: 46.1 us
  Pallas kernels  23.3 us (50%)
  starting transfers between devices  17.7 us (38%)
  waiting for transfers between devices  4.44 us (10%)
    ppermute x8, starting transfers between devices, exchanged(): return lax.ppermute(state, 'seq', route)  15.1 us
    pallas_call x4, Pallas kernels, layer(): pl.pallas_call(functools.partial(stage_kernel, head_count=head_count, pie...  6.21 us
    pallas_call x4, Pallas kernels, windowed(): pl.pallas_call(functools.partial(window_kernel, has_rim=rim is not None,...  5.43 us
    ppermute x8, waiting for transfers between devices, exchanged(): return lax.ppermute(state, 'seq', route)  4.43 us
    pallas_call x3, Pallas kernels, neared(): pl.pallas_call(functools.partial(near_kernel, spans=local_spans(tokens),...  3.71 us
    pallas_call x1, Pallas kernels, layer(): states_call(*[in_hbm(a) for a in (seq_lengths, lin_keys, lin_values, wind...  2.98 us
    pallas_call x1, Pallas kernels, layer(): pl.pallas_call(far_kernel, grid=(blocks,), in_specs=[VMEM] * (3 + 2 * lev...  2.37 us
    pallas_call x1, Pallas kernels, layer(): pl.pallas_call(functools.partial(finish_kernel, pieces=pieces), in_specs=...  1.44 us
  transfers between devices with their start and end apart: 12, of which 3 were waited for; matrix products, arithmetic and copies ran while one was open for 0% of the time, Pallas kernels for 37%

profile of v6, /device:TPU:0, one launch (start us, length us, event | category | flops | bytes accessed | tf_op | source)
XLA Modules:
  0.0 46.1 jit_solution(11161813344908872072)
XLA Ops:
  0.0 3.0 %states.1 = (bf16[1024,1024]{1,0:T(8,128)(2,1)S(1)}, bf16[1024,1024]{1,0:T(8,128)(2,1)S(1)}, bf16[256,512]{1,0:T(8,128)(2,1)S(1)}, bf16[3,1024,128]{2,1,0:T(8,12...) custom-call(s32[4]{0:T(128)} %lengths_hbm.1, ...), custom_call_target="tpu_custom_call" | custom-call | tf_op jit(solution)/shard_map/states/pallas_call | solution.py:431
  3.0 3.0 %collective-permute-start = (bf16[512,128]{1,0:T(8,128)(2,1)S(1)}, bf16[512,128]{1,0:T(8,128)(2,1)S(1)}, u32[]{:S(2)}, u32[]{:S(2)}) collective-permute-start(bf16[512,128]{1,0:T(8,128)(2,1)S(1)} %get-tuple-element.41.own_ref), channel_id=1, source_target_pairs={{0,2},{2,0},{4,6},{6,4},{8,10},{10,8},{12,14},{14,12},{16,18},{18,... | collective-permute-start | bytes 393224 | tf_op jit(solution)/shard_map/ppermute | solution.py:437
  6.0 0.7 %collective-permute-start.6 = (bf16[256,512]{1,0:T(8,128)(2,1)S(1)}, bf16[256,512]{1,0:T(8,128)(2,1)S(1)}, u32[]{:S(2)}, u32[]{:S(2)}) collective-permute-start(bf16[256,512]{1,0:T(8,128)(2,1)S(1)} %get-tuple-element.49.own_ref), channel_id=1, source_target_pairs={{0,0},{2,2},{4,4},{6,14},{8,8},{10,10},{12,12},{14,22},{16,16},{18... | collective-permute-start | bytes 786440 | tf_op jit(solution)/shard_map/ppermute | solution.py:507
  6.7 0.1 collective-permute-start.1
  6.8 0.0 copy-done.7
  6.8 0.9 %weights.1.weights_ref = f32[8,15,1024]{2,1,0:T(8,128)S(1)} custom-call(f32[8,8]{1,0:T(8,128)S(1)} %copy-done.7, s32[15,1024]{1,0:T(8,128)S(1)} %copy-done.4), custom_call_target="tpu_custom_call" | custom-call | tf_op jit(solution)/shard_map/weights/pallas_call | solution.py:450
  7.7 1.9 %near.3 = (f32[4,1024,256]{2,1,0:T(8,128)S(1)}, f32[8,128]{1,0:T(8,128)S(1)}) custom-call(f32[8,15,1024]{2,1,0:T(8,128)S(1)} %weights.1.weights_ref, bf16[1024,1024]{1,0:T(8,128)(2,1)S(1)} %copy-done, bf16[1024,1024]{1,0:T(8,128)(2,1)S(1)} %get-tuple-element.35.k_ref, bf16[1024,1024]{1,0:T(8,128)(2,1)S(1)} %get-tuple-element.36.v_ref, ...), custom_call_target="tpu_custom_call" | custom-call | tf_op jit(solution)/shard_map/near/pallas_call | solution.py:465
  9.6 0.5 %collective-permute-done.arrived_ref.rest_0_ = bf16[512,128]{1,0:T(8,128)(2,1)S(1)} collective-permute-done((bf16[512,128]{1,0:T(8,128)(2,1)S(1)}, bf16[512,128]{1,0:T(8,128)(2,1)S(1)}, u32[]{:S(2)}, u32[]{:S(2)}) %collective-permute-start) | collective-permute-done | bytes 131104 | tf_op jit(solution)/shard_map/ppermute | solution.py:437
  10.2 4.4 %collective-permute-start.2 = (bf16[512,128]{1,0:T(8,128)(2,1)S(1)}, bf16[512,128]{1,0:T(8,128)(2,1)S(1)}, u32[]{:S(2)}, u32[]{:S(2)}) collective-permute-start(bf16[512,128]{1,0:T(8,128)(2,1)S(1)} %join.6.own_ref), channel_id=1, source_target_pairs={{0,4},{2,6},{4,0},{6,2},{8,12},{10,14},{12,8},{14,10},{16,20},{18,... | collective-permute-start | bytes 393224 | tf_op jit(solution)/shard_map/ppermute | solution.py:437
  14.6 0.9 %near.4 = (f32[4,1024,256]{2,1,0:T(8,128)S(1)}, f32[8,128]{1,0:T(8,128)S(1)}) custom-call(f32[8,15,1024]{2,1,0:T(8,128)S(1)} %weights.1.weights_ref, bf16[1024,1024]{1,0:T(8,128)(2,1)S(1)} %copy-done, bf16[1024,1024]{1,0:T(8,128)(2,1)S(1)} %get-tuple-element.35.k_ref, ...), custom_call_target="tpu_custom_call", output_to_operand_aliasing={{0}: (5, {})} | custom-call | tf_op jit(solution)/shard_map/near/pallas_call | solution.py:465
  15.5 0.0 collective-permute-done.1.arrived_ref.rest_1_
  15.5 0.1 collective-permute-start.3
  15.6 0.0 copy-start.3
  15.6 0.0 copy-start.5
  15.7 0.9 %near.5 = (f32[4,1024,256]{2,1,0:T(8,128)S(1)}, f32[8,128]{1,0:T(8,128)S(1)}) custom-call(f32[8,15,1024]{2,1,0:T(8,128)S(1)} %weights.1.weights_ref, bf16[1024,1024]{1,0:T(8,128)(2,1)S(1)} %copy-done, bf16[1024,1024]{1,0:T(8,128)(2,1)S(1)} %get-tuple-element.35.k_ref, ...), custom_call_target="tpu_custom_call", output_to_operand_aliasing={{0}: (5, {})} | custom-call | tf_op jit(solution)/shard_map/near/pallas_call | solution.py:465
  16.6 0.1 copy-done.2
  16.7 0.2 copy-done.3
  16.8 1.3 %window.4 = (bf16[4,1024,256]{2,1,0:T(8,128)(2,1)S(1)}, f32[8,128]{1,0:T(8,128)S(1)}) custom-call(f32[13,256]{1,0:T(8,128)S(1)} %get-tuple-element.34.flags_ref, bf16[1024,1024]{1,0:T(8,128)(2,1)S(1)} %copy-done, bf16[1024,256]{1,0:T(8,128)(2,1)S(1)} %copy-done.2, bf16[1024,256]{1,0:T(8,128)(2,1)S(1)} %copy-done.3, f32[8,1,128]{2,1,0:T(1,128)S(1)} %bitcast.2), custom_call_target="tpu_custom_call" | custom-call | tf_op jit(solution)/shard_map/window/pallas_call | solution.py:486
  18.2 0.0 collective-permute-done.2.arrived_ref.rest_2_
  18.2 1.6 %collective-permute-start.4 = (bf16[512,128]{1,0:T(8,128)(2,1)S(1)}, bf16[512,128]{1,0:T(8,128)(2,1)S(1)}, u32[]{:S(2)}, u32[]{:S(2)}) collective-permute-start(bf16[512,128]{1,0:T(8,128)(2,1)S(1)} %join.8.own_ref), channel_id=1, source_target_pairs={{0,8},{2,10},{4,12},{6,14},{8,0},{10,2},{12,4},{14,6},{16,24},{18,... | collective-permute-start | bytes 393224 | tf_op jit(solution)/shard_map/ppermute | solution.py:437
  19.9 0.0 collective-permute-done.6.ahead_ref
  19.9 1.3 %collective-permute-start.7 = (bf16[256,512]{1,0:T(8,128)(2,1)S(1)}, bf16[256,512]{1,0:T(8,128)(2,1)S(1)}, u32[]{:S(2)}, u32[]{:S(2)}) collective-permute-start(bf16[256,512]{1,0:T(8,128)(2,1)S(1)} %pick.1), channel_id=1, source_target_pairs={{0,2},{2,4},{4,6},{6,0},{8,10},{10,12},{12,14},{14,8},{16,18},{18,... | collective-permute-start | bytes 786440 | tf_op jit(solution)/shard_map/ppermute | solution.py:519
  21.2 0.0 collective-permute-done.3.arrived_ref.rest_3_
  21.3 1.0 %collective-permute-start.5 = (bf16[512,128]{1,0:T(8,128)(2,1)S(1)}, bf16[512,128]{1,0:T(8,128)(2,1)S(1)}, u32[]{:S(2)}, u32[]{:S(2)}) collective-permute-start(bf16[512,128]{1,0:T(8,128)(2,1)S(1)} %join.9.own_ref), channel_id=1, source_target_pairs={{0,8},{2,10},{4,12},{6,14},{8,0},{10,2},{12,4},{14,6},{16,24},{18,... | collective-permute-start | bytes 393224 | tf_op jit(solution)/shard_map/ppermute | solution.py:437
  22.3 1.3 %window.5 = (bf16[4,1024,256]{2,1,0:T(8,128)(2,1)S(1)}, f32[8,128]{1,0:T(8,128)S(1)}) custom-call(f32[13,256]{1,0:T(8,128)S(1)} %get-tuple-element.34.flags_ref, bf16[1024,1024]{1,0:T(8,128)(2,1)S(1)} %copy-done, bf16[1024,256]{1,0:T(8,128)(2,1)S(1)} %copy-done.2, bf16[1024,256]{1,0:T(8,128)(2,1)S(1)} %copy-done.3, ...), custom_call_target="tpu_custom_call", output_to_operand_aliasing={{0}: (5, {})} | custom-call | tf_op jit(solution)/shard_map/window/pallas_call | solution.py:486
  23.6 0.0 copy-start.6
  23.6 1.3 %window.6 = (bf16[4,1024,256]{2,1,0:T(8,128)(2,1)S(1)}, f32[8,128]{1,0:T(8,128)S(1)}) custom-call(f32[13,256]{1,0:T(8,128)S(1)} %get-tuple-element.34.flags_ref, bf16[1024,1024]{1,0:T(8,128)(2,1)S(1)} %copy-done, bf16[1024,256]{1,0:T(8,128)(2,1)S(1)} %copy-done.2, bf16[1024,256]{1,0:T(8,128)(2,1)S(1)} %copy-done.3, ...), custom_call_target="tpu_custom_call", output_to_operand_aliasing={{0}: (5, {})} | custom-call | tf_op jit(solution)/shard_map/window/pallas_call | solution.py:486
  24.9 0.0 collective-permute-done.4.rest_4_.arrived_ref
  24.9 0.1 join.10
  25.0 2.2 %collective-permute-start.8 = (bf16[512,128]{1,0:T(8,128)(2,1)S(1)}, bf16[512,128]{1,0:T(8,128)(2,1)S(1)}, u32[]{:S(2)}, u32[]{:S(2)}) collective-permute-start(bf16[512,128]{1,0:T(8,128)(2,1)S(1)} %join.10), channel_id=1, source_target_pairs={{0,16},{2,18},{4,20},{6,22},{8,24},{10,26},{12,28},{14,30},{16,0},... | collective-permute-start | bytes 393224 | tf_op jit(solution)/shard_map/ppermute | solution.py:437
  27.2 0.0 collective-permute-done.5.rest_5_.arrived_ref
  27.2 2.7 %collective-permute-start.9 = (bf16[512,128]{1,0:T(8,128)(2,1)S(1)}, bf16[512,128]{1,0:T(8,128)(2,1)S(1)}, u32[]{:S(2)}, u32[]{:S(2)}) collective-permute-start(bf16[512,128]{1,0:T(8,128)(2,1)S(1)} %join.11), channel_id=1, source_target_pairs={{0,16},{2,18},{4,20},{6,22},{8,24},{10,26},{12,28},{14,30},{16,0},... | collective-permute-start | bytes 393224 | tf_op jit(solution)/shard_map/ppermute | solution.py:437
  29.9 0.0 copy-done.6
  29.9 2.4 %far.1 = (f32[4,1024,256]{2,1,0:T(8,128)S(1)}, bf16[4,1024,256]{2,1,0:T(8,128)(2,1)S(1)}, f32[8,128,128]{2,1,0:T(8,128)S(1)}) custom-call(f32[13,256]{1,0:T(8,128)S(1)} %get-tuple-element.34.flags_ref, f32[8,15,1024]{2,1,0:T(8,128)S(1)} %weights.1.weights_ref, bf16[1024,1024]{1,0:T(8,128)(2,1)S(1)} %copy-done, ...), custom_call_target="tpu_custom_call", output_to_operand_aliasing={{0}: (4, {})} | custom-call | tf_op jit(solution)/shard_map/far/pallas_call | solution.py:534
  32.3 0.0 collective-permute-done.7.rest_0_
  32.3 0.0 copy-start.1
  32.3 1.5 %window.7 = (bf16[4,1024,256]{2,1,0:T(8,128)(2,1)S(1)}, f32[8,128]{1,0:T(8,128)}) custom-call(f32[13,256]{1,0:T(8,128)S(1)} %get-tuple-element.34.flags_ref, bf16[1024,1024]{1,0:T(8,128)(2,1)S(1)} %copy-done, bf16[1024,256]{1,0:T(8,128)(2,1)S(1)} %copy-done.2, bf16[1024,256]{1,0:T(8,128)(2,1)S(1)} %copy-done.3, ...), custom_call_target="tpu_custom_call", output_to_operand_aliasing={{0}: (6, {})} | custom-call | tf_op jit(solution)/shard_map/window/pallas_call | solution.py:486
  33.8 2.5 %collective-permute-done.8.refs_4_ = bf16[512,128]{1,0:T(8,128)(2,1)S(1)} collective-permute-done((bf16[512,128]{1,0:T(8,128)(2,1)S(1)}, bf16[512,128]{1,0:T(8,128)(2,1)S(1)}, u32[]{:S(2)}, u32[]{:S(2)}) %collective-permute-start.8) | collective-permute-done | bytes 131104 | tf_op jit(solution)/shard_map/ppermute | solution.py:437
  36.2 1.4 %collective-permute-done.9.refs_5_ = bf16[512,128]{1,0:T(8,128)(2,1)S(1)} collective-permute-done((bf16[512,128]{1,0:T(8,128)(2,1)S(1)}, bf16[512,128]{1,0:T(8,128)(2,1)S(1)}, u32[]{:S(2)}, u32[]{:S(2)}) %collective-permute-start.9) | collective-permute-done | bytes 131104 | tf_op jit(solution)/shard_map/ppermute | solution.py:437
  37.6 1.9 %stage.4 = (bf16[256,2048]{1,0:T(8,128)(2,1)S(1)}, bf16[256,1024]{1,0:T(8,128)(2,1)S(1)}) custom-call(bf16[4,1024,256]{2,1,0:T(8,128)(2,1)S(1)} %get-tuple-element.47.refs_0_, f32[4,1024,256]{2,1,0:T(8,128)S(1)} %get-tuple-element.48.refs_1_, bf16[4,1024,256]{2,1,0:T(8,128)(2,1)S(1)} %get-tuple-element.53.refs_2_, ...), custom_call_target="tpu_custom_call" | custom-call | tf_op jit(solution)/shard_map/stage/pallas_call | solution.py:563
  39.5 0.1 collective-permute-start.10
  39.6 1.5 %stage.5 = (bf16[256,2048]{1,0:T(8,128)(2,1)S(1)}, bf16[256,1024]{1,0:T(8,128)(2,1)S(1)}) custom-call(bf16[4,1024,256]{2,1,0:T(8,128)(2,1)S(1)} %get-tuple-element.47.refs_0_, f32[4,1024,256]{2,1,0:T(8,128)S(1)} %get-tuple-element.48.refs_1_, bf16[4,1024,256]{2,1,0:T(8,128)(2,1)S(1)} %get-tuple-element.53.refs_2_, ...), custom_call_target="tpu_custom_call" | custom-call | tf_op jit(solution)/shard_map/stage/pallas_call | solution.py:563
  41.1 0.6 %collective-permute-start.11 = (bf16[256,2048]{1,0:T(8,128)(2,1)S(1)}, bf16[256,2048]{1,0:T(8,128)(2,1)S(1)}, u32[]{:S(2)}, u32[]{:S(2)}) collective-permute-start(bf16[256,2048]{1,0:T(8,128)(2,1)S(1)} %get-tuple-element.62), channel_id=1, source_target_pairs={{0,1},{1,0},{2,3},{3,2},{4,5},{5,4},{6,7},{7,6},{8,9},{9,8},{10,11... | collective-permute-start | bytes 3145736 | tf_op jit(solution)/shard_map/ppermute | solution.py:581
  41.7 1.5 %stage.6 = (f32[256,2048]{1,0:T(8,128)S(1)}, bf16[256,1024]{1,0:T(8,128)(2,1)S(1)}) custom-call(bf16[4,1024,256]{2,1,0:T(8,128)(2,1)S(1)} %get-tuple-element.47.refs_0_, f32[4,1024,256]{2,1,0:T(8,128)S(1)} %get-tuple-element.48.refs_1_, bf16[4,1024,256]{2,1,0:T(8,128)(2,1)S(1)} %get-tuple-element.53.refs_2_, f32[8,128,128]{2,1,0:T(8,128)S(1)} %get-tuple-element.54.refs_3_, ...), custom_call_target="tpu_custom_call" | custom-call | tf_op jit(solution)/shard_map/stage/pallas_call | solution.py:563
  43.3 1.2 %stage.7.refs_1_ = f32[256,2048]{1,0:T(8,128)S(1)} custom-call(bf16[4,1024,256]{2,1,0:T(8,128)(2,1)S(1)} %get-tuple-element.47.refs_0_, f32[4,1024,256]{2,1,0:T(8,128)S(1)} %get-tuple-element.48.refs_1_, bf16[4,1024,256]{2,1,0:T(8,128)(2,1)S(1)} %get-tuple-element.53.refs_2_, f32[8,128,128]{2,1,0:T(8,128)S(1)} %get-tuple-element.54.refs_3_, ...), custom_call_target="tpu_custom_call" | custom-call | tf_op jit(solution)/shard_map/stage/pallas_call | solution.py:563
  44.5 0.0 collective-permute-done.10.refs_2_
  44.5 0.0 collective-permute-done.11.refs_3_
  44.5 1.4 %finish.1 = bf16[512,2048]{1,0:T(8,128)(2,1)} custom-call(f32[256,2048]{1,0:T(8,128)S(1)} %get-tuple-element.59.refs_0_, f32[256,2048]{1,0:T(8,128)S(1)} %stage.7.refs_1_, bf16[256,2048]{1,0:T(8,128)(2,1)S(1)} %collective-permute-done.10.refs_2_, bf16[256,2048]{1,0:T(8,128)(2,1)S(1)} %collective-permute-done.11.refs_3_), custom_call_target="tpu_custom_call" | custom-call | tf_op jit(solution)/shard_map/finish/pallas_call | solution.py:584
  (14 shorter events, 0.3 us)
Async XLA Ops:
  0.0 6.8 %copy-start.7 = (f32[8,8]{1,0:T(8,128)S(1)}, f32[8,8]{1,0:T(8,128)}, u32[]{:S(2)}) copy-start(f32[8,8]{1,0:T(8,128)} %table_ref.1) | copy-start | bytes 772
  0.0 6.8 %copy-start.4 = (s32[15,1024]{1,0:T(8,128)S(1)}, s32[15,1024]{1,0:T(8,128)}, u32[]{:S(2)}) copy-start(s32[15,1024]{1,0:T(8,128)} %index_ref.1) | copy-start | bytes 184324
  0.0 7.7 %copy-start = (bf16[1024,1024]{1,0:T(8,128)(2,1)S(1)}, bf16[1024,1024]{1,0:T(8,128)(2,1)}, u32[]{:S(2)}) copy-start(bf16[1024,1024]{1,0:T(8,128)(2,1)} %q_ref.15) | copy-start | bytes 6291460
  3.0 7.1 %collective-permute-start = (bf16[512,128]{1,0:T(8,128)(2,1)S(1)}, bf16[512,128]{1,0:T(8,128)(2,1)S(1)}, u32[]{:S(2)}, u32[]{:S(2)}) collective-permute-start(bf16[512,128]{1,0:T(8,128)(2,1)S(1)} %get-tuple-element.41.own_ref), channel_id=1, source_target_pairs={{0,2},{2,0},{4,6},{6,4},{8,10},{10,8},{12,14},{14,12},{16,18},{18,... | collective-permute-start | bytes 393224 | tf_op jit(solution)/shard_map/ppermute | solution.py:437
  6.0 13.8 %collective-permute-start.6 = (bf16[256,512]{1,0:T(8,128)(2,1)S(1)}, bf16[256,512]{1,0:T(8,128)(2,1)S(1)}, u32[]{:S(2)}, u32[]{:S(2)}) collective-permute-start(bf16[256,512]{1,0:T(8,128)(2,1)S(1)} %get-tuple-element.49.own_ref), channel_id=1, source_target_pairs={{0,0},{2,2},{4,4},{6,14},{8,8},{10,10},{12,12},{14,22},{16,16},{18... | collective-permute-start | bytes 786440 | tf_op jit(solution)/shard_map/ppermute | solution.py:507
  6.7 8.8 %collective-permute-start.1 = (bf16[512,128]{1,0:T(8,128)(2,1)S(1)}, bf16[512,128]{1,0:T(8,128)(2,1)S(1)}, u32[]{:S(2)}, u32[]{:S(2)}) collective-permute-start(bf16[512,128]{1,0:T(8,128)(2,1)S(1)} %get-tuple-element.42.own_ref), channel_id=1, source_target_pairs={{0,2},{2,0},{4,6},{6,4},{8,10},{10,8},{12,14},{14,12},{16,18},{18,... | collective-permute-start | bytes 393224 | tf_op jit(solution)/shard_map/ppermute | solution.py:437
  10.2 8.0 %collective-permute-start.2 = (bf16[512,128]{1,0:T(8,128)(2,1)S(1)}, bf16[512,128]{1,0:T(8,128)(2,1)S(1)}, u32[]{:S(2)}, u32[]{:S(2)}) collective-permute-start(bf16[512,128]{1,0:T(8,128)(2,1)S(1)} %join.6.own_ref), channel_id=1, source_target_pairs={{0,4},{2,6},{4,0},{6,2},{8,12},{10,14},{12,8},{14,10},{16,20},{18,... | collective-permute-start | bytes 393224 | tf_op jit(solution)/shard_map/ppermute | solution.py:437
  15.5 5.7 %collective-permute-start.3 = (bf16[512,128]{1,0:T(8,128)(2,1)S(1)}, bf16[512,128]{1,0:T(8,128)(2,1)S(1)}, u32[]{:S(2)}, u32[]{:S(2)}) collective-permute-start(bf16[512,128]{1,0:T(8,128)(2,1)S(1)} %join.7.own_ref), channel_id=1, source_target_pairs={{0,4},{2,6},{4,0},{6,2},{8,12},{10,14},{12,8},{14,10},{16,20},{18,... | collective-permute-start | bytes 393224 | tf_op jit(solution)/shard_map/ppermute | solution.py:437
  15.6 1.0 %copy-start.2 = (bf16[1024,256]{1,0:T(8,128)(2,1)S(1)}, bf16[1024,256]{1,0:T(8,128)(2,1)}, u32[]{:S(2)}) copy-start(bf16[1024,256]{1,0:T(8,128)(2,1)} %k_ref.7) | copy-start | bytes 1572868
  15.6 1.2 %copy-start.3 = (bf16[1024,256]{1,0:T(8,128)(2,1)S(1)}, bf16[1024,256]{1,0:T(8,128)(2,1)}, u32[]{:S(2)}) copy-start(bf16[1024,256]{1,0:T(8,128)(2,1)} %v_ref.7) | copy-start | bytes 1572868
  15.6 1.2 %copy-start.5 = (f32[1024]{0:T(1024)S(1)}, f32[1024]{0:T(1024)}, u32[]{:S(2)}) copy-start(f32[1024]{0:T(1024)} %param.20) | copy-start | bytes 12292
  18.2 6.7 %collective-permute-start.4 = (bf16[512,128]{1,0:T(8,128)(2,1)S(1)}, bf16[512,128]{1,0:T(8,128)(2,1)S(1)}, u32[]{:S(2)}, u32[]{:S(2)}) collective-permute-start(bf16[512,128]{1,0:T(8,128)(2,1)S(1)} %join.8.own_ref), channel_id=1, source_target_pairs={{0,8},{2,10},{4,12},{6,14},{8,0},{10,2},{12,4},{14,6},{16,24},{18,... | collective-permute-start | bytes 393224 | tf_op jit(solution)/shard_map/ppermute | solution.py:437
  19.9 12.4 %collective-permute-start.7 = (bf16[256,512]{1,0:T(8,128)(2,1)S(1)}, bf16[256,512]{1,0:T(8,128)(2,1)S(1)}, u32[]{:S(2)}, u32[]{:S(2)}) collective-permute-start(bf16[256,512]{1,0:T(8,128)(2,1)S(1)} %pick.1), channel_id=1, source_target_pairs={{0,2},{2,4},{4,6},{6,0},{8,10},{10,12},{12,14},{14,8},{16,18},{18,... | collective-permute-start | bytes 786440 | tf_op jit(solution)/shard_map/ppermute | solution.py:519
  21.3 5.9 %collective-permute-start.5 = (bf16[512,128]{1,0:T(8,128)(2,1)S(1)}, bf16[512,128]{1,0:T(8,128)(2,1)S(1)}, u32[]{:S(2)}, u32[]{:S(2)}) collective-permute-start(bf16[512,128]{1,0:T(8,128)(2,1)S(1)} %join.9.own_ref), channel_id=1, source_target_pairs={{0,8},{2,10},{4,12},{6,14},{8,0},{10,2},{12,4},{14,6},{16,24},{18,... | collective-permute-start | bytes 393224 | tf_op jit(solution)/shard_map/ppermute | solution.py:437
  23.6 6.3 %copy-start.6 = (f32[1024]{0:T(1024)S(1)}, f32[1024]{0:T(1024)}, u32[]{:S(2)}) copy-start(f32[1024]{0:T(1024)} %param.19) | copy-start | bytes 12292
  25.0 11.2 %collective-permute-start.8 = (bf16[512,128]{1,0:T(8,128)(2,1)S(1)}, bf16[512,128]{1,0:T(8,128)(2,1)S(1)}, u32[]{:S(2)}, u32[]{:S(2)}) collective-permute-start(bf16[512,128]{1,0:T(8,128)(2,1)S(1)} %join.10), channel_id=1, source_target_pairs={{0,16},{2,18},{4,20},{6,22},{8,24},{10,26},{12,28},{14,30},{16,0},... | collective-permute-start | bytes 393224 | tf_op jit(solution)/shard_map/ppermute | solution.py:437
  27.2 10.4 %collective-permute-start.9 = (bf16[512,128]{1,0:T(8,128)(2,1)S(1)}, bf16[512,128]{1,0:T(8,128)(2,1)S(1)}, u32[]{:S(2)}, u32[]{:S(2)}) collective-permute-start(bf16[512,128]{1,0:T(8,128)(2,1)S(1)} %join.11), channel_id=1, source_target_pairs={{0,16},{2,18},{4,20},{6,22},{8,24},{10,26},{12,28},{14,30},{16,0},... | collective-permute-start | bytes 393224 | tf_op jit(solution)/shard_map/ppermute | solution.py:437
  32.3 5.3 %copy-start.1 = (bf16[1024,2048]{1,0:T(8,128)(2,1)S(1)}, bf16[1024,2048]{1,0:T(8,128)(2,1)}, u32[]{:S(2)}) copy-start(bf16[1024,2048]{1,0:T(8,128)(2,1)} %refs_6_.7) | copy-start | bytes 12582916
  39.5 5.0 %collective-permute-start.10 = (bf16[256,2048]{1,0:T(8,128)(2,1)S(1)}, bf16[256,2048]{1,0:T(8,128)(2,1)S(1)}, u32[]{:S(2)}, u32[]{:S(2)}) collective-permute-start(bf16[256,2048]{1,0:T(8,128)(2,1)S(1)} %get-tuple-element.61), channel_id=1, source_target_pairs={{0,1},{1,0},{2,3},{3,2},{4,5},{5,4},{6,7},{7,6},{8,9},{9,8},{10,11... | collective-permute-start | bytes 3145736 | tf_op jit(solution)/shard_map/ppermute | solution.py:581
  41.1 3.4 %collective-permute-start.11 = (bf16[256,2048]{1,0:T(8,128)(2,1)S(1)}, bf16[256,2048]{1,0:T(8,128)(2,1)S(1)}, u32[]{:S(2)}, u32[]{:S(2)}) collective-permute-start(bf16[256,2048]{1,0:T(8,128)(2,1)S(1)} %get-tuple-element.62), channel_id=1, source_target_pairs={{0,1},{1,0},{2,3},{3,2},{4,5},{5,4},{6,7},{7,6},{8,9},{9,8},{10,11... | collective-permute-start | bytes 3145736 | tf_op jit(solution)/shard_map/ppermute | solution.py:581
